TPU v7x, 128 devices: a whole 4x4x4 slice. The times are simulated.
128 devices in a mesh: gx: 8 (over x, core), gy: 16 (over z, y).
Axes of the slice: x: 4, y: 4, z: 4, core: 2. Of those that a mesh axis runs over, the one named last changes fastest.
Arguments:
- fields: float32 [4, 128, 256, 128], P(None, 'gx', 'gy'), may hold values from -6 to 6
- lift: float32 [32, 4], replicated, may hold values from -3 to 3
- lift_bias: float32 [32], replicated, may hold values from -3 to 3
- spectral_in: float32 [256, 2, 8, 32, 64], P(('gx', 'gy')), may hold values from -0.015625 to 0.015625
- bypass_in: float32 [64, 32], replicated, may hold values from -1 to 1
- bias_in: float32 [64], replicated, may hold values from -3 to 3
- spectral_out: float32 [256, 2, 8, 64, 32], P(('gx', 'gy')), may hold values from -0.0234375 to 0.0234375
- bypass_out: float32 [32, 64], replicated, may hold values from -0.75 to 0.75
- bias_out: float32 [32], replicated, may hold values from -3 to 3
- project: float32 [4, 32], replicated, may hold values from -1 to 1
- project_bias: float32 [4], replicated, may hold values from -3 to 3
Outputs:
- result: float32 [4, 128, 256, 128], P(None, 'gx', 'gy')
All inputs are finite; a program needn't handle non-finite values.
Results may differ from a plain program's by a relative error of at most 0.000058.
Values sent between devices are 32-bit elements; how exact they have to be, the bound alone decides.
No kernel may reach another device: no remote copies, remote signals or barrier semaphores. Data moves between devices by JAX's collectives and lax.ppermute only.
A program may use at most 64 MiB of HBM per device.

v0:
```python
import functools
import math

import jax
import jax.numpy as jnp
import numpy as np
from jax import lax
from jax.experimental import pallas as pl
from jax.experimental.pallas import tpu as pltpu
from jax.sharding import PartitionSpec as P

KX, KY, KZ = 16, 16, 8
NX, NY, NZ = 128, 256, 128
CIN, C1, C2 = 4, 32, 64
AXES = ("gx", "gy")
OWNERS = 128
TOTAL = NX * NY * NZ
BACK = math.sqrt(2.0 / (KX * KY * KZ))
F32 = jnp.float32
BF16 = jnp.bfloat16
VMEM = pl.BlockSpec(memory_space=pltpu.VMEM)
SMEM = pl.BlockSpec(memory_space=pltpu.SMEM)
PARAMS = pltpu.CompilerParams(vmem_limit_bytes=40 << 20)


def mode_frequencies():
    centered = np.where(np.arange(16) < 8, np.arange(16), np.arange(16) - 16)
    n = np.arange(OWNERS)
    fx = np.stack([centered[n // 8]] * 2)
    fy = np.stack([centered[2 * (n % 8) + s] for s in range(2)])
    return fx, fy


def place_angles(xs, ys, x_length, y_length):
    fx, fy = mode_frequencies()
    turns = (
        fx[:, :, None, None] * xs[None, None, :, None] / x_length
        + fy[:, :, None, None] * ys[None, None, None, :] / y_length
    )
    return 2.0 * np.pi * turns


def inverse_tables(angles, scale):
    out = []
    for shift in (0.0, 0.5 * np.pi):
        c, s = np.cos(angles + shift), np.sin(angles + shift)
        table = np.array([[c, -s], [s, c]])
        table = table.transpose(0, 4, 5, 2, 1, 3) * scale
        rows = 2 * angles.shape[2] * angles.shape[3]
        out.append(table.reshape(rows, 512).astype(np.float32))
    return out


def forward_tables(angles, scale):
    out = []
    for shift in (0.0, 0.5 * np.pi):
        c, s = np.cos(angles + shift), np.sin(angles + shift)
        table = np.array([[c, s], [-s, c]])
        table = table.transpose(2, 0, 3, 5, 4, 1) * scale
        out.append(table.reshape(512, -1).astype(np.float32))
    return out


def z_angles():
    return 2.0 * np.pi * (np.arange(NZ)[:, None] * np.arange(KZ)[None, :] % NZ) / NZ


def first_z_table():
    c, s = np.cos(z_angles()), np.sin(z_angles())
    parts = np.array([[c, -s], [-s, -c]])
    table = np.zeros((CIN, NZ, 2, 2, KZ, CIN))
    for ch in range(CIN):
        table[ch, :, :, :, :, ch] = parts.transpose(2, 0, 1, 3)
    return table.reshape(CIN, NZ, 128).astype(np.float32)


def first_places_table():
    angles = place_angles(np.arange(16), np.arange(16), NX, NY)
    table = np.stack([np.cos(angles), np.sin(angles)], axis=1) / math.sqrt(TOTAL)
    return table.reshape(512, 256).astype(np.float32)


def split_np(table):
    high = table.astype(BF16)
    low = (table - high.astype(np.float32)).astype(BF16)
    return high, low


def inverse_z_table():
    table = np.stack([np.cos(z_angles()), -np.sin(z_angles())], axis=2)
    high, low = split_np(table.reshape(NZ, 16).astype(np.float32))
    return np.concatenate([high, high, low], axis=1)


def forward_z_table():
    table = np.stack([np.cos(z_angles()).T, -np.sin(z_angles()).T], axis=0)
    return np.concatenate(split_np(table.reshape(16, NZ).astype(np.float32)), axis=0)


def split(x):
    high = x.astype(BF16)
    return high, (x - high.astype(F32)).astype(BF16)


def mm(a, b, dims=((1,), (0,))):
    return lax.dot_general(a, b, (dims, ((), ())), preferred_element_type=F32)


def mm3(a, b, dims=((1,), (0,))):
    ah, al = split(a)
    bh, bl = split(b)
    return mm(ah, bh, dims) + mm(ah, bl, dims) + mm(al, bh, dims)


def gelu(x):
    return 0.5 * x * (1.0 + lax.erf(x * math.sqrt(0.5)))


def half_swap(x):
    return pltpu.roll(x, 64, 1)


def first_spectrum(fields, ztab, ptab, phase, out):
    lane = lax.broadcasted_iota(jnp.int32, (128, 128), 1)
    low = lane < 64
    sign = jnp.where(low, 1.0, -1.0).astype(F32)
    transformed = mm3(fields[0].reshape(256, NZ), ztab[0])
    for ch in range(1, CIN):
        transformed += mm3(fields[ch].reshape(256, NZ), ztab[ch])
    both = mm3(ptab[...], transformed)
    rows = []
    for s in range(2):
        part_cos = both[256 * s : 256 * s + 128]
        part_sin = both[256 * s + 128 : 256 * s + 256]
        pair = part_cos + sign * half_swap(part_sin)
        turn = phase[:, 2 * s : 2 * s + 1], phase[:, 2 * s + 1 : 2 * s + 2]
        rows.append(turn[0] * pair + turn[1] * half_swap(pair))
    out[...] = jnp.where(low, rows[0], half_swap(rows[1]))


def mixed_row(columns, weights, wide):
    pieces = [[[None] * KZ for _ in range(2)] for _ in range(2)]
    for s in range(2):
        for k in range(KZ):
            real, imag = columns(s, 0, k), columns(s, 1, k)
            wr, wi = weights[s, 0, k], weights[s, 1, k]
            pieces[s][0][k] = jnp.sum(real * wr - imag * wi, axis=0, keepdims=True)
            pieces[s][1][k] = jnp.sum(real * wi + imag * wr, axis=0, keepdims=True)
    per = 128 // wide
    return [
        jnp.concatenate(pieces[s][part][k : k + per], axis=1)
        for s in range(2)
        for part in range(2)
        for k in range(0, KZ, per)
    ]


def first_mix(arrived, lift_wide, bias_column, weights, out):
    row = jnp.sum(arrived[...], axis=0, keepdims=True)
    source = lax.broadcasted_iota(jnp.int32, (128, 32), 0) // CIN
    pick = (source == lax.broadcasted_iota(jnp.int32, (128, 32), 1)).astype(F32)
    lifted = (
        lax.dot_general(
            lift_wide[...] * row, pick, (((1,), (0,)), ((), ())),
            precision=lax.Precision.HIGHEST, preferred_element_type=F32,
        )
        + bias_column[...]
    )

    def column(s, part, k):
        at = s * 16 + part * 8 + k
        return lifted[:, at : at + 1]

    for t, piece in enumerate(mixed_row(column, weights, C2)):
        out[:, 128 * t : 128 * t + 128] = jnp.broadcast_to(piece, (OWNERS, 128))


def second_mix(arrived, weights, out):
    rows = [
        jnp.sum(arrived[:, 128 * t : 128 * t + 128], axis=0, keepdims=True) for t in range(16)
    ]
    stacked = jnp.concatenate(rows + [jnp.zeros((112, 128), F32)], axis=0).T

    def column(s, part, k):
        at = (s * 2 + part) * 4 + k // 2
        return stacked[(k % 2) * 64 : (k % 2) * 64 + 64, at : at + 1]

    for t, piece in enumerate(mixed_row(column, weights, C1)):
        out[:, 128 * t : 128 * t + 128] = jnp.broadcast_to(piece, (OWNERS, 128))


def coarse_level(
    arrived, inv0, inv1, fwd0, fwd1, lane_phase, row_phase, fields, z_back, z_fwd,
    pool_mix, pool_bias, wide_mix, wide_bias, out, skip, y_s, rhs_s, g_s, t_s,
):
    low = lax.broadcasted_iota(jnp.int32, (16, 128), 1) < 64
    table = inv0[...] * lane_phase[0:1] + inv1[...] * lane_phase[1:2]
    modes = jnp.concatenate([arrived[:, 512 * t : 512 * t + 512] for t in range(4)], axis=0)
    made = mm3(table, modes)
    for t in range(4):
        y_s[t] = made[:, 128 * t : 128 * t + 128]
    for q in range(0, 8, 2):
        for k in range(0, 8, 2):
            first = y_s[k // 2, pl.ds(q, 16, stride=8), :]
            second = y_s[k // 2, pl.ds(q + 1, 16, stride=8), :]
            rhs_s[q // 2, 16 * k : 16 * k + 16] = jnp.where(low, first, half_swap(second))
            rhs_s[q // 2, 16 * k + 16 : 16 * k + 32] = jnp.where(low, half_swap(first), second)
    pool_h, pool_l = split(pool_mix[...])
    wide_h, wide_l = split(wide_mix[...])

    def step(p, carry):
        rows = [rhs_s[t, pl.ds(p, 16, stride=8), :] for t in range(4)]
        high, less = split(jnp.concatenate(rows, axis=1))
        pooled = []
        for ch in range(CIN):
            total = jnp.zeros((8, 128), F32)
            for dx in range(2):
                for dy in range(2):
                    total += fields[ch, 2 * p + dx, pl.ds(dy, 8, stride=2), :]
            pooled.append(total * 0.25)
        pool_t = jnp.concatenate(pooled, axis=0).T
        ph, pll = split(pool_t)
        before = mm(z_back[...], jnp.concatenate([high, less, high], axis=0))
        before += mm(ph, pool_h) + mm(ph, pool_l) + mm(pll, pool_h)
        value = gelu(before + pool_bias[...])
        vh, vl = split(value)
        both = mm(z_fwd[...], vh)
        both = both[:16] + both[16:] + mm(z_fwd[:16], vl)
        for t in range(4):
            at = slice(128 * t, 128 * t + 128)
            wide = mm(vh[:, at], wide_h) + mm(vh[:, at], wide_l) + mm(vl[:, at], wide_h)
            skip[p, :, at] = wide + wide_bias[...]
            g_s[t, pl.ds(pl.multiple_of(p * 16, 16), 16), :] = both[:, at]
        return carry

    lax.fori_loop(0, 8, step, 0)
    for q in range(0, 8, 2):
        for k in range(0, 8, 2):
            first = g_s[q // 2, pl.ds(k, 16, stride=8), :]
            second = g_s[q // 2, pl.ds(k + 1, 16, stride=8), :]
            at = slice(64 * k, 64 * k + 128)
            t_s[16 * q : 16 * q + 16, at] = jnp.where(low, first, half_swap(second))
            t_s[16 * q + 16 : 16 * q + 32, at] = jnp.where(low, half_swap(first), second)
    th, tl = split(t_s[...])
    for t in range(4):
        at = slice(128 * t, 128 * t + 128)
        turn = row_phase[at]
        ah, al = split(fwd0[at] * turn[:, 0:1] + fwd1[at] * turn[:, 1:2])
        out[:, 512 * t : 512 * t + 512] = mm(ah, th) + mm(ah, tl) + mm(al, th)


def fine_level(
    through, constant, arrived, inv0, inv1, lane_phase, fields, z_back, skip, project_wide,
    out, y_s, rhs_s,
):
    modes = jnp.concatenate([arrived[:, 256 * t : 256 * t + 256] for t in range(4)], axis=0)
    mh, ml = split(modes)
    for t in range(4):
        at = slice(128 * t, 128 * t + 128)
        th, tl = split(inv0[at] * lane_phase[0:1] + inv1[at] * lane_phase[1:2])
        made = mm(th, mh) + mm(th, ml) + mm(tl, mh)
        y_s[0, at] = made[:, :128]
        y_s[1, at] = made[:, 128:]
    quarter = lax.broadcasted_iota(jnp.int32, (32, 128), 1) // 32
    for y in range(0, 16, 4):
        for k in range(0, 8, 4):
            rows = [y_s[k // 4, pl.ds(y + u, 32, stride=16), :] for u in range(4)]
            for v in range(4):
                made = rows[v]
                for u in range(4):
                    if u != v:
                        moved = pltpu.roll(rows[u], ((u - v) % 4) * 32, 1)
                        made = jnp.where(quarter == u, moved, made)
                rhs_s[y // 4, 32 * (k + v) : 32 * (k + v) + 32] = made
    jh, jl = split(project_wide[...])

    def step(x, carry):
        rows = [rhs_s[t, pl.ds(x, 16, stride=16), :] for t in range(4)]
        high, less = split(jnp.concatenate(rows, axis=1))
        before = mm(z_back[...], jnp.concatenate([high, less, high], axis=0))
        value = gelu(before + skip[x // 2])
        vh, vl = split(value)
        made = (mm(vh, jh) + mm(vh, jl) + mm(vl, jh)).T
        for o in range(CIN):
            total = made[16 * o : 16 * o + 16] + constant[o]
            for ch in range(CIN):
                total += through[o, ch] * fields[ch, x]
            out[o, x] = total
        return carry

    lax.fori_loop(0, 16, step, 0)


def exchange(tiles):
    return lax.all_to_all(tiles, AXES, split_axis=0, concat_axis=0, tiled=True)


def product(formula, left, right):
    return jnp.einsum(formula, left, right, precision=lax.Precision.HIGHEST)


def on_device(
    fields, lift, lift_bias, spectral_in, bypass_in, bias_in, spectral_out, bypass_out, bias_out,
    project, project_bias,
):
    gx, gy = lax.axis_index("gx"), lax.axis_index("gy")
    fx, fy = mode_frequencies()
    turns = (jnp.asarray(2 * fx, jnp.int32) * gx + jnp.asarray(fy, jnp.int32) * gy) % 16
    angle = turns.astype(F32) * (2.0 * math.pi / 16)
    cos, sin = jnp.cos(angle), jnp.sin(angle)
    first_phase = jnp.stack([cos[0], sin[0], cos[1], sin[1]], axis=1)
    lanes = [jnp.repeat(v[:, None], 2, axis=1).reshape(1, 512) for v in (cos, sin)]
    lane_phase = jnp.concatenate(lanes, axis=0)
    row_phase = lane_phase.T

    eye8 = jnp.eye(8, dtype=F32)
    pool_mix = product("ed,dc->ce", bypass_in, lift)
    pool_mix = (pool_mix[:, None, None, :] * eye8[None, :, :, None]).reshape(32, 512)
    pool_bias = jnp.tile(bias_in + product("ed,d->e", bypass_in, lift_bias), 8)[None]
    same = np.arange(2)[:, None] == (np.arange(4) // 2)[None, :]
    wide_mix = (
        bypass_out.T[None, :, None, :] * jnp.asarray(same, F32)[:, None, :, None]
    ).reshape(128, 128)
    wide_bias = jnp.tile(bias_out, 4)[None]
    eye16 = jnp.eye(16, dtype=F32)
    project_wide = (project.T[None, :, :, None] * eye16[:, None, None, :]).reshape(512, 64)
    through = product("od,dc->oc", project, lift)
    constant = project_bias + product("od,d->o", project, lift_bias)
    at_zero = ((gx == 0) & (gy == 0)).astype(F32) * math.sqrt(TOTAL)
    bias_column = lift_bias[:, None] * (jnp.arange(32) == 0).astype(F32)[None, :] * at_zero
    lift_wide = jnp.tile(lift, (1, 32))

    call = functools.partial(pl.pallas_call, compiler_params=PARAMS)
    spectrum = call(
        first_spectrum,
        out_shape=jax.ShapeDtypeStruct((OWNERS, 128), F32),
        in_specs=[VMEM] * 4, out_specs=VMEM, name="first_spectrum",
    )(fields, first_z_table(), first_places_table(), first_phase)
    mixed = call(
        first_mix,
        out_shape=jax.ShapeDtypeStruct((OWNERS, 2048), F32),
        in_specs=[VMEM] * 4, out_specs=VMEM, name="first_mix",
    )(exchange(spectrum), lift_wide, bias_column, spectral_in)
    half = place_angles(np.arange(8), np.arange(8), NX // 2, NY // 2)
    whole = place_angles(np.arange(16), np.arange(16), NX, NY)
    z_back = inverse_z_table()
    spectrum, skip = call(
        coarse_level,
        out_shape=(
            jax.ShapeDtypeStruct((OWNERS, 2048), F32),
            jax.ShapeDtypeStruct((8, NZ, 512), F32),
        ),
        in_specs=[VMEM] * 14, out_specs=(VMEM, VMEM), name="coarse_level",
        scratch_shapes=[pltpu.VMEM((4, 128, 128), F32)] * 3 + [pltpu.VMEM((128, 512), F32)],
    )(
        exchange(mixed), *inverse_tables(half, BACK),
        *forward_tables(half, 1.0 / math.sqrt(TOTAL / 4.0)), lane_phase, row_phase, fields,
        z_back, forward_z_table(), pool_mix, pool_bias, wide_mix, wide_bias,
    )
    mixed = call(
        second_mix,
        out_shape=jax.ShapeDtypeStruct((OWNERS, 1024), F32),
        in_specs=[VMEM] * 2, out_specs=VMEM, name="second_mix",
    )(exchange(spectrum), spectral_out)
    return call(
        fine_level,
        out_shape=jax.ShapeDtypeStruct((CIN, 16, 16, NZ), F32),
        in_specs=[SMEM] * 2 + [VMEM] * 8, out_specs=VMEM, name="fine_level",
        scratch_shapes=[pltpu.VMEM((2, 512, 128), F32), pltpu.VMEM((4, 256, 128), F32)],
    )(
        through, constant, exchange(mixed), *inverse_tables(whole, BACK), lane_phase, fields,
        z_back, skip, project_wide,
    )


def solution(mesh):
    owned = P(AXES, None, None, None, None)
    grid = P(None, "gx", "gy", None)
    in_specs = (grid, P(), P(), owned, P(), P(), owned, P(), P(), P(), P())
    return jax.shard_map(
        on_device, mesh=mesh, in_specs=in_specs, out_specs=grid, check_vma=False
    )
```

profile of v0, /device:TPU:1, one launch (start us, length us, event | category | flops | bytes accessed | tf_op | source)
XLA Modules:
  0.0 124.6 jit_solution(1976514377047671217)
XLA Ops:
  0.0 0.8 fusion.10
  1.0 1.0 copy-done.1
  2.0 1.0 copy-done.8
  3.0 0.9 copy-done.13
  4.0 1.9 %first_spectrum.1 = f32[128,128]{1,0:T(8,128)} custom-call(f32[4,16,16,128]{3,2,1,0:T(8,128)S(1)} %copy-done.1, f32[4,128,128]{2,1,0:T(8,128)S(1)} %copy-done.13, f32[512,256]{1,0:T(8,128)S(1)} %copy-done.8, f32[128,4]{1,0:T(8,128)S(1)} %copy.43.phase), custom_call_target="tpu_custom_call" | custom-call | tf_op jit(solution)/shard_map/first_spectrum/pallas_call | solution.py:334
  5.9 11.5 %all-to-all-start = ((f32[128,1,128]{2,1,0:T(1,128)}), f32[128,1,128]{2,1,0:T(1,128)S(1)}, u32[]{:S(2)}, u32[]{:S(2)}) async-start(f32[128,1,128]{2,1,0:T(1,128)} %bitcast.7), calls=%async_computation | async-start | bytes 131072 | tf_op jit(solution)/shard_map/all_to_all | solution.py:295
  17.4 0.7 multiply_multiply_fusion.bias_column
  18.9 8.2 %all-to-all-done = f32[128,1,128]{2,1,0:T(1,128)S(1)} async-done(((f32[128,1,128]{2,1,0:T(1,128)}), f32[128,1,128]{2,1,0:T(1,128)S(1)}, u32[]{:S(2)}, u32[]{:S(2)}) %all-to-all-start) | async-done | bytes 65568 | tf_op jit(solution)/shard_map/all_to_all | solution.py:295
  27.7 2.0 %copy.46 = f32[128,1,2048]{2,1,0:T(1,128)} copy(f32[128,1,2048]{2,0,1:T(8,128)S(1)} %bitcast.60) | data formatting | bytes 2097152 | tf_op jit(solution)/shard_map/all_to_all | solution.py:295
  29.7 5.4 %all-to-all-start.1 = ((f32[128,1,2048]{2,1,0:T(1,128)}), f32[128,1,2048]{2,1,0:T(1,128)}, u32[]{:S(2)}, u32[]{:S(2)}) async-start(f32[128,1,2048]{2,1,0:T(1,128)} %copy.46), calls=%async_computation.1 | async-start | bytes 2097152 | tf_op jit(solution)/shard_map/all_to_all | solution.py:295
  36.4 17.3 %all-to-all-done.1 = f32[128,1,2048]{2,1,0:T(1,128)} async-done(((f32[128,1,2048]{2,1,0:T(1,128)}), f32[128,1,2048]{2,1,0:T(1,128)}, u32[]{:S(2)}, u32[]{:S(2)}) %all-to-all-start.1) | async-done | bytes 1048608 | tf_op jit(solution)/shard_map/all_to_all | solution.py:295
  53.7 1.6 %copy.60 = f32[128,1,2048]{2,0,1:T(8,128)S(1)} copy(f32[128,1,2048]{2,1,0:T(1,128)} %all-to-all-done.1) | data formatting | bytes 2097152
  55.4 6.6 %coarse_level.1 = (f32[128,2048]{1,0:T(8,128)S(1)}, f32[8,128,512]{2,1,0:T(8,128)S(1)}) custom-call(f32[128,2048]{1,0:T(8,128)S(1)} %bitcast.59, f32[128,512]{1,0:T(8,128)S(1)} %copy-done.9, f32[128,512]{1,0:T(8,128)S(1)} %copy-done.10, f32[512,128]{1,0:T(8,128)S(1)} %copy-done.11, f32[512,128]{1,0:T(8,128)S(1)} %copy-done.12, ...), custom_call_target="tpu_custom_call" | custom-call | tf_op jit(solution)/shard_map/coarse_level/pallas_call | solution.py:347
  62.0 1.3 %copy-done.3 = f32[8,128,512]{2,1,0:T(8,128)} copy-done((f32[8,128,512]{2,1,0:T(8,128)}, f32[8,128,512]{2,1,0:T(8,128)S(1)}, u32[]{:S(2)}) %copy-start.3) | copy-done | bytes 2097176
  63.3 2.1 %copy.49 = f32[128,1,2048]{2,1,0:T(1,128)} copy(f32[128,1,2048]{2,0,1:T(8,128)S(1)} %bitcast.64) | data formatting | bytes 2097152 | tf_op jit(solution)/shard_map/all_to_all | solution.py:295
  65.4 4.7 %all-to-all-start.2 = ((f32[128,1,2048]{2,1,0:T(1,128)}), f32[128,1,2048]{2,1,0:T(1,128)S(1)}, u32[]{:S(2)}, u32[]{:S(2)}) async-start(f32[128,1,2048]{2,1,0:T(1,128)} %copy.49), calls=%async_computation.2 | async-start | bytes 2097152 | tf_op jit(solution)/shard_map/all_to_all | solution.py:295
  70.5 18.6 %all-to-all-done.2 = f32[128,1,2048]{2,1,0:T(1,128)S(1)} async-done(((f32[128,1,2048]{2,1,0:T(1,128)}), f32[128,1,2048]{2,1,0:T(1,128)S(1)}, u32[]{:S(2)}, u32[]{:S(2)}) %all-to-all-start.2) | async-done | bytes 1048608 | tf_op jit(solution)/shard_map/all_to_all | solution.py:295
  90.1 1.3 %copy.51 = f32[128,1,1024]{2,1,0:T(1,128)} copy(f32[128,1,1024]{2,0,1:T(8,128)S(1)} %bitcast.63) | data formatting | bytes 1048576 | tf_op jit(solution)/shard_map/all_to_all | solution.py:295
  91.5 5.9 %all-to-all-start.3 = ((f32[128,1,1024]{2,1,0:T(1,128)}), f32[128,1,1024]{2,1,0:T(1,128)}, u32[]{:S(2)}, u32[]{:S(2)}) async-start(f32[128,1,1024]{2,1,0:T(1,128)} %copy.51), calls=%async_computation.3 | async-start | bytes 1048576 | tf_op jit(solution)/shard_map/all_to_all | solution.py:295
  98.1 13.1 %all-to-all-done.3 = f32[128,1,1024]{2,1,0:T(1,128)} async-done(((f32[128,1,1024]{2,1,0:T(1,128)}), f32[128,1,1024]{2,1,0:T(1,128)}, u32[]{:S(2)}, u32[]{:S(2)}) %all-to-all-start.3) | async-done | bytes 524320 | tf_op jit(solution)/shard_map/all_to_all | solution.py:295
  111.2 1.1 copy.61
  112.4 1.2 copy-done.5
  113.6 1.2 copy-done.6
  114.8 9.8 %fine_level.1 = f32[4,16,16,128]{3,2,1,0:T(8,128)} custom-call(f32[4,4]{1,0:T(4,128)S(1)} %fusion.12.through, f32[4]{0:T(128)S(1)} %fusion.1.constant, f32[128,1024]{1,0:T(8,128)S(1)} %bitcast.62, f32[512,512]{1,0:T(8,128)S(1)} %copy-done.5, f32[512,512]{1,0:T(8,128)S(1)} %copy-done.6, f32[2,512]{1,0:T(2,128)S(1)} %get-tuple-element.12.lane_phase, ...), custom_call_target="tpu_custom_call" | custom-call | tf_op jit(solution)/shard_map/fine_level/pallas_call | solution.py:365
  (77 shorter events, 4.8 us)
Async XLA Ops:
  0.0 35.8 %copy-start = (f32[64,32]{0,1:T(8,128)S(1)}, f32[64,32]{0,1:T(8,128)}, u32[]{:S(2)}) copy-start(f32[64,32]{0,1:T(8,128)} %param.28) | copy-start | bytes 24580
  4.0 23.1 %copy-start.7 = (f32[2,2,8,32,64]{4,3,2,1,0:T(8,128)S(1)}, f32[2,2,8,32,64]{4,3,2,1,0:T(8,128)}, u32[]{:S(2)}) copy-start(f32[2,2,8,32,64]{4,3,2,1,0:T(8,128)} %weights.2) | copy-start | bytes 786436
  5.9 21.2 %all-to-all-start = ((f32[128,1,128]{2,1,0:T(1,128)}), f32[128,1,128]{2,1,0:T(1,128)S(1)}, u32[]{:S(2)}, u32[]{:S(2)}) async-start(f32[128,1,128]{2,1,0:T(1,128)} %bitcast.7), calls=%async_computation | async-start | bytes 131072 | tf_op jit(solution)/shard_map/all_to_all | solution.py:295
  27.7 7.7 %copy-start.18 = (f32[32,64]{1,0:T(8,128)S(1)}, f32[32,64]{1,0:T(8,128)}, u32[]{:S(2)}) copy-start(f32[32,64]{1,0:T(8,128)} %param.31) | copy-start | bytes 24580
  27.7 7.7 %copy-start.20 = (f32[2,4]{0,1:T(4,128)S(1)}, f32[2,4]{0,1:T(4,128)}, u32[]{:S(2)}) copy-start(f32[2,4]{0,1:T(4,128)} %constant.60.clone) | copy-start | bytes 100
  27.7 8.1 %copy-start.17 = (f32[32,4]{0,1:T(4,128)S(1)}, f32[32,4]{0,1:T(4,128)}, u32[]{:S(2)}) copy-start(f32[32,4]{0,1:T(4,128)} %param.25) | copy-start | bytes 1540
  29.7 6.4 %copy-start.21 = (f32[32]{0:T(128)S(1)}, f32[32]{0:T(128)}, u32[]{:S(2)}) copy-start(f32[32]{0:T(128)} %param.26) | copy-start | bytes 388
  29.7 6.4 %copy-start.22 = (f32[64]{0:T(128)S(1)}, f32[64]{0:T(128)}, u32[]{:S(2)}) copy-start(f32[64]{0:T(128)} %param.29) | copy-start | bytes 772
  29.7 6.6 %copy-start.23 = (f32[32]{0:T(128)S(1)}, f32[32]{0:T(128)}, u32[]{:S(2)}) copy-start(f32[32]{0:T(128)} %param.32) | copy-start | bytes 388
  29.7 24.0 %all-to-all-start.1 = ((f32[128,1,2048]{2,1,0:T(1,128)}), f32[128,1,2048]{2,1,0:T(1,128)}, u32[]{:S(2)}, u32[]{:S(2)}) async-start(f32[128,1,2048]{2,1,0:T(1,128)} %copy.46), calls=%async_computation.1 | async-start | bytes 2097152 | tf_op jit(solution)/shard_map/all_to_all | solution.py:295
  35.1 20.2 %copy-start.2 = (f32[4,16,16,128]{3,2,1,0:T(8,128)S(1)}, f32[4,16,16,128]{3,2,1,0:T(8,128)}, u32[]{:S(2)}) copy-start(f32[4,16,16,128]{3,2,1,0:T(8,128)} %fields.5) | copy-start | bytes 1572868
  35.1 20.2 %copy-start.9 = (f32[128,512]{1,0:T(8,128)S(1)}, f32[128,512]{1,0:T(8,128)}, u32[]{:S(2)}) copy-start(f32[128,512]{1,0:T(8,128)} %constant.63.clone.inv0) | copy-start | bytes 786436
  35.2 20.2 %copy-start.10 = (f32[128,512]{1,0:T(8,128)S(1)}, f32[128,512]{1,0:T(8,128)}, u32[]{:S(2)}) copy-start(f32[128,512]{1,0:T(8,128)} %constant.64.clone.inv1) | copy-start | bytes 786436
  35.2 20.2 %copy-start.11 = (f32[512,128]{1,0:T(8,128)S(1)}, f32[512,128]{1,0:T(8,128)}, u32[]{:S(2)}) copy-start(f32[512,128]{1,0:T(8,128)} %constant.65.clone.fwd0) | copy-start | bytes 786436
  35.2 20.2 %copy-start.12 = (f32[512,128]{1,0:T(8,128)S(1)}, f32[512,128]{1,0:T(8,128)}, u32[]{:S(2)}) copy-start(f32[512,128]{1,0:T(8,128)} %constant.66.clone.fwd1) | copy-start | bytes 786436
  35.2 20.2 %copy-start.14 = (bf16[128,48]{1,0:T(8,128)(2,1)S(1)}, bf16[128,48]{1,0:T(8,128)(2,1)}, u32[]{:S(2)}) copy-start(bf16[128,48]{1,0:T(8,128)(2,1)} %constant.67.clone.z_back) | copy-start | bytes 36868
  35.2 20.2 %copy-start.15 = (bf16[32,128]{1,0:T(8,128)(2,1)S(1)}, bf16[32,128]{1,0:T(8,128)(2,1)}, u32[]{:S(2)}) copy-start(bf16[32,128]{1,0:T(8,128)(2,1)} %constant.68.clone.z_fwd) | copy-start | bytes 24580
  62.0 1.3 %copy-start.3 = (f32[8,128,512]{2,1,0:T(8,128)}, f32[8,128,512]{2,1,0:T(8,128)S(1)}, u32[]{:S(2)}) copy-start(f32[8,128,512]{2,1,0:T(8,128)S(1)} %get-tuple-element.8.skip) | copy-start | bytes 6291460
  63.3 6.8 %copy-start.16 = (f32[2,2,8,64,32]{3,4,2,1,0:T(8,128)S(1)}, f32[2,2,8,64,32]{3,4,2,1,0:T(8,128)}, u32[]{:S(2)}) copy-start(f32[2,2,8,64,32]{3,4,2,1,0:T(8,128)} %param.30) | copy-start | bytes 786436
  65.4 23.7 %all-to-all-start.2 = ((f32[128,1,2048]{2,1,0:T(1,128)}), f32[128,1,2048]{2,1,0:T(1,128)S(1)}, u32[]{:S(2)}, u32[]{:S(2)}) async-start(f32[128,1,2048]{2,1,0:T(1,128)} %copy.49), calls=%async_computation.2 | async-start | bytes 2097152 | tf_op jit(solution)/shard_map/all_to_all | solution.py:295
  89.4 7.9 %copy-start.19 = (f32[4,32]{1,0:T(4,128)S(1)}, f32[4,32]{1,0:T(4,128)}, u32[]{:S(2)}) copy-start(f32[4,32]{1,0:T(4,128)} %param.33) | copy-start | bytes 1540
  90.1 7.7 %copy-start.24 = (f32[4]{0:T(128)S(1)}, f32[4]{0:T(128)}, u32[]{:S(2)}) copy-start(f32[4]{0:T(128)} %param.34) | copy-start | bytes 52
  91.5 20.9 %copy-start.4 = (f32[8,128,512]{2,1,0:T(8,128)S(1)}, f32[8,128,512]{2,1,0:T(8,128)}, u32[]{:S(2)}) copy-start(f32[8,128,512]{2,1,0:T(8,128)} %copy-done.3) | copy-start | bytes 6291460
  91.5 19.8 %all-to-all-start.3 = ((f32[128,1,1024]{2,1,0:T(1,128)}), f32[128,1,1024]{2,1,0:T(1,128)}, u32[]{:S(2)}, u32[]{:S(2)}) async-start(f32[128,1,1024]{2,1,0:T(1,128)} %copy.51), calls=%async_computation.3 | async-start | bytes 1048576 | tf_op jit(solution)/shard_map/all_to_all | solution.py:295
  (5 other events, 5.5 us)
where the time goes:
time: 125 us
  waiting for transfers between devices  57.2 us (46%)
  starting transfers between devices  27.5 us (22%)
  Pallas kernels  19.5 us (16%)
  local copies, waits for them, and re-layouts  17.6 us (14%)
  other arithmetic  1.82 us (1%)
    all_to_all x4, waiting for transfers between devices, exchange(): return lax.all_to_all(tiles, AXES, split_axis=0, concat_axis=0, tiled=True)  57.2 us
    all_to_all x4, starting transfers between devices, exchange(): return lax.all_to_all(tiles, AXES, split_axis=0, concat_axis=0, tiled=True)  27.5 us
    unnamed x54, local copies, waits for them, and re-layouts  10.3 us
    pallas_call x1, Pallas kernels, on_device(): call(fine_level, out_shape=jax.ShapeDtypeStruct((CIN, 16, 16, NZ), F32),...  9.78 us
    pallas_call x1, Pallas kernels, on_device(): call(coarse_level, out_shape=(jax.ShapeDtypeStruct((OWNERS, 2048), F32),...  6.6 us
    all_to_all x3, local copies, waits for them, and re-layouts, exchange(): return lax.all_to_all(tiles, AXES, split_axis=0, concat_axis=0, tiled=True)  5.43 us
  transfers between devices with their start and end apart: 4, of which 4 were waited for; matrix products, arithmetic and copies ran while one was open for 3% of the time, Pallas kernels for 0%

commit v1 on v0

--- a/solution.py
+++ b/solution.py
@@ -40,44 +40,24 @@
     return 2.0 * np.pi * turns
 
 
-def inverse_tables(angles, scale):
-    out = []
-    for shift in (0.0, 0.5 * np.pi):
-        c, s = np.cos(angles + shift), np.sin(angles + shift)
-        table = np.array([[c, -s], [s, c]])
-        table = table.transpose(0, 4, 5, 2, 1, 3) * scale
-        rows = 2 * angles.shape[2] * angles.shape[3]
-        out.append(table.reshape(rows, 512).astype(np.float32))
-    return out
-
-
-def forward_tables(angles, scale):
-    out = []
-    for shift in (0.0, 0.5 * np.pi):
-        c, s = np.cos(angles + shift), np.sin(angles + shift)
-        table = np.array([[c, s], [-s, c]])
-        table = table.transpose(2, 0, 3, 5, 4, 1) * scale
-        out.append(table.reshape(512, -1).astype(np.float32))
-    return out
+def wave_tables():
+    fx, fy = mode_frequencies()
+    ahead = np.array([0.0, 0.5 * np.pi])[None, None, :, None]
+    places = np.arange(16)[:, None, None, None]
+    along_x = 2.0 * np.pi * places * fx[None, :, None, :] / NX + ahead
+    along_y = 2.0 * np.pi * places * fy[None, :, None, :] / NY + 0.0 * ahead
+    tables = [np.cos(along_x), np.sin(along_x), np.cos(along_y), np.sin(along_y)]
+    return np.stack(tables).reshape(4, 16, 512).astype(np.float32)
+
+
+def phase_steps():
+    fx, fy = mode_frequencies()
+    steps = np.stack([np.stack([2 * fx, 2 * fx], axis=1), np.stack([fy, fy], axis=1)])
+    return steps.reshape(2, 512).astype(np.int32)
 
 
 def z_angles():
     return 2.0 * np.pi * (np.arange(NZ)[:, None] * np.arange(KZ)[None, :] % NZ) / NZ
-
-
-def first_z_table():
-    c, s = np.cos(z_angles()), np.sin(z_angles())
-    parts = np.array([[c, -s], [-s, -c]])
-    table = np.zeros((CIN, NZ, 2, 2, KZ, CIN))
-    for ch in range(CIN):
-        table[ch, :, :, :, :, ch] = parts.transpose(2, 0, 1, 3)
-    return table.reshape(CIN, NZ, 128).astype(np.float32)
-
-
-def first_places_table():
-    angles = place_angles(np.arange(16), np.arange(16), NX, NY)
-    table = np.stack([np.cos(angles), np.sin(angles)], axis=1) / math.sqrt(TOTAL)
-    return table.reshape(512, 256).astype(np.float32)
 
 
 def split_np(table):
@@ -120,22 +100,42 @@
     return pltpu.roll(x, 64, 1)
 
 
-def first_spectrum(fields, ztab, ptab, phase, out):
-    lane = lax.broadcasted_iota(jnp.int32, (128, 128), 1)
-    low = lane < 64
-    sign = jnp.where(low, 1.0, -1.0).astype(F32)
-    transformed = mm3(fields[0].reshape(256, NZ), ztab[0])
-    for ch in range(1, CIN):
-        transformed += mm3(fields[ch].reshape(256, NZ), ztab[ch])
-    both = mm3(ptab[...], transformed)
-    rows = []
-    for s in range(2):
-        part_cos = both[256 * s : 256 * s + 128]
-        part_sin = both[256 * s + 128 : 256 * s + 256]
-        pair = part_cos + sign * half_swap(part_sin)
-        turn = phase[:, 2 * s : 2 * s + 1], phase[:, 2 * s + 1 : 2 * s + 2]
-        rows.append(turn[0] * pair + turn[1] * half_swap(pair))
-    out[...] = jnp.where(low, rows[0], half_swap(rows[1]))
+def device_waves(waves, steps, place):
+    turns = (steps[0:1] * place[0] + steps[1:2] * place[1]) & 15
+    angle = turns.astype(F32) * (2.0 * math.pi / 16)
+    cos, sin = jnp.cos(angle), jnp.sin(angle)
+    return waves[0] * cos - waves[1] * sin, waves[1] * cos + waves[0] * sin
+
+
+def wave_rows(along_x, cos_y, sin_y, xs):
+    cos_x, sin_x = along_x
+    real = [cos_x[x : x + 1] * cos_y - sin_x[x : x + 1] * sin_y for x in xs]
+    imag = [sin_x[x : x + 1] * cos_y + cos_x[x : x + 1] * sin_y for x in xs]
+    return jnp.concatenate(real, axis=0), jnp.concatenate(imag, axis=0)
+
+
+def first_spectrum(place, fields, waves, steps, z_fwd, out, fields_v, sems):
+    copies = [
+        pltpu.make_async_copy(fields.at[ch], fields_v.at[ch], sems.at[ch]) for ch in range(CIN)
+    ]
+    for copy in copies:
+        copy.start()
+    along_x = device_waves(waves, steps, place)
+    real, imag = wave_rows(along_x, waves[2], waves[3], range(16))
+    nt = ((1,), (1,))
+    parts = [[], []]
+    for ch in range(CIN):
+        copies[ch].wait()
+        fh, fl = split(fields_v[ch].reshape(256, NZ))
+        both = mm(z_fwd[...], fh, nt)
+        made = both[:16] + both[16:] + mm(z_fwd[:16], fl, nt)
+        parts[0].append(made[:8])
+        parts[1].append(made[8:])
+    total = mm3(jnp.concatenate(parts[0], axis=0), real)
+    total += mm3(jnp.concatenate(parts[1], axis=0), imag)
+    total *= 1.0 / math.sqrt(TOTAL)
+    tiles = [total[:, 128 * t : 128 * t + 128] for t in range(4)]
+    out[...] = jnp.concatenate(tiles, axis=0).T
 
 
 def mixed_row(columns, weights, wide):
@@ -157,7 +157,8 @@
 
 def first_mix(arrived, lift_wide, bias_column, weights, out):
     row = jnp.sum(arrived[...], axis=0, keepdims=True)
-    source = lax.broadcasted_iota(jnp.int32, (128, 32), 0) // CIN
+    source = lax.broadcasted_iota(jnp.int32, (128, 32), 0)
+    source = source // 32 * 8 + source % 8
     pick = (source == lax.broadcasted_iota(jnp.int32, (128, 32), 1)).astype(F32)
     lifted = (
         lax.dot_general(
@@ -171,32 +172,43 @@
         at = s * 16 + part * 8 + k
         return lifted[:, at : at + 1]
 
-    for t, piece in enumerate(mixed_row(column, weights, C2)):
-        out[:, 128 * t : 128 * t + 128] = jnp.broadcast_to(piece, (OWNERS, 128))
+    block = jnp.concatenate(mixed_row(column, weights, C2), axis=0)
+    for n in range(OWNERS):
+        out[n] = block
 
 
 def second_mix(arrived, weights, out):
-    rows = [
-        jnp.sum(arrived[:, 128 * t : 128 * t + 128], axis=0, keepdims=True) for t in range(16)
-    ]
-    stacked = jnp.concatenate(rows + [jnp.zeros((112, 128), F32)], axis=0).T
+    rows = arrived[0]
+    for n in range(1, OWNERS):
+        rows += arrived[n]
+    stacked = jnp.concatenate([rows, jnp.zeros((112, 128), F32)], axis=0).T
 
     def column(s, part, k):
         at = (s * 2 + part) * 4 + k // 2
         return stacked[(k % 2) * 64 : (k % 2) * 64 + 64, at : at + 1]
 
-    for t, piece in enumerate(mixed_row(column, weights, C1)):
-        out[:, 128 * t : 128 * t + 128] = jnp.broadcast_to(piece, (OWNERS, 128))
+    block = jnp.concatenate(mixed_row(column, weights, C1), axis=0)
+    for n in range(OWNERS):
+        out[n] = block
 
 
 def coarse_level(
-    arrived, inv0, inv1, fwd0, fwd1, lane_phase, row_phase, fields, z_back, z_fwd,
+    place, arrived, waves, steps, fields, z_back, z_fwd,
     pool_mix, pool_bias, wide_mix, wide_bias, out, skip, y_s, rhs_s, g_s, t_s,
 ):
     low = lax.broadcasted_iota(jnp.int32, (16, 128), 1) < 64
-    table = inv0[...] * lane_phase[0:1] + inv1[...] * lane_phase[1:2]
-    modes = jnp.concatenate([arrived[:, 512 * t : 512 * t + 512] for t in range(4)], axis=0)
-    made = mm3(table, modes)
+    along_x = device_waves(waves, steps, place)
+    cos_y = jnp.concatenate([waves[2, 2 * q : 2 * q + 1] for q in range(8)], axis=0)
+    sin_y = jnp.concatenate([waves[3, 2 * q : 2 * q + 1] for q in range(8)], axis=0)
+    table = jnp.concatenate(wave_rows(along_x, cos_y, sin_y, range(0, 16, 2)), axis=0)
+    th, tl = split(table * BACK)
+    made = None
+    for t in range(4):
+        tiles = [arrived[pl.ds(4 * t + u, OWNERS, stride=16), :] for u in range(4)]
+        mh, ml = split(jnp.concatenate(tiles, axis=1))
+        at = slice(128 * t, 128 * t + 128)
+        term = mm(th[:, at], mh) + mm(th[:, at], ml) + mm(tl[:, at], mh)
+        made = term if made is None else made + term
     for t in range(4):
         y_s[t] = made[:, 128 * t : 128 * t + 128]
     for q in range(0, 8, 2):
@@ -230,7 +242,8 @@
             at = slice(128 * t, 128 * t + 128)
             wide = mm(vh[:, at], wide_h) + mm(vh[:, at], wide_l) + mm(vl[:, at], wide_h)
             skip[p, :, at] = wide + wide_bias[...]
-            g_s[t, pl.ds(pl.multiple_of(p * 16, 16), 16), :] = both[:, at]
+            g_s[t, pl.ds(pl.multiple_of(p * 8, 8), 8), :] = both[:8, at]
+            g_s[t, pl.ds(pl.multiple_of(p * 8 + 64, 8), 8), :] = both[8:, at]
         return carry
 
     lax.fori_loop(0, 8, step, 0)
@@ -238,29 +251,37 @@
         for k in range(0, 8, 2):
             first = g_s[q // 2, pl.ds(k, 16, stride=8), :]
             second = g_s[q // 2, pl.ds(k + 1, 16, stride=8), :]
-            at = slice(64 * k, 64 * k + 128)
-            t_s[16 * q : 16 * q + 16, at] = jnp.where(low, first, half_swap(second))
-            t_s[16 * q + 16 : 16 * q + 32, at] = jnp.where(low, half_swap(first), second)
-    th, tl = split(t_s[...])
+            t_s[k // 2, pl.ds(q, 16, stride=8), :] = jnp.where(low, first, half_swap(second))
+            t_s[k // 2, pl.ds(q + 1, 16, stride=8), :] = jnp.where(low, half_swap(first), second)
+    scale = 1.0 / math.sqrt(TOTAL / 4.0)
+    th, tl = split(jnp.concatenate([t_s[t] for t in range(4)], axis=1) * scale)
+    ah, al = split(table.T)
     for t in range(4):
         at = slice(128 * t, 128 * t + 128)
-        turn = row_phase[at]
-        ah, al = split(fwd0[at] * turn[:, 0:1] + fwd1[at] * turn[:, 1:2])
-        out[:, 512 * t : 512 * t + 512] = mm(ah, th) + mm(ah, tl) + mm(al, th)
+        made = mm(ah[at], th) + mm(ah[at], tl) + mm(al[at], th)
+        for u in range(4):
+            out[pl.ds(4 * t + u, OWNERS, stride=16), :] = made[:, 128 * u : 128 * u + 128]
 
 
 def fine_level(
-    through, constant, arrived, inv0, inv1, lane_phase, fields, z_back, skip, project_wide,
+    place, through, constant, arrived, waves, steps, fields, z_back, skip, project_wide,
     out, y_s, rhs_s,
 ):
-    modes = jnp.concatenate([arrived[:, 256 * t : 256 * t + 256] for t in range(4)], axis=0)
-    mh, ml = split(modes)
+    modes = []
     for t in range(4):
-        at = slice(128 * t, 128 * t + 128)
-        th, tl = split(inv0[at] * lane_phase[0:1] + inv1[at] * lane_phase[1:2])
-        made = mm(th, mh) + mm(th, ml) + mm(tl, mh)
-        y_s[0, at] = made[:, :128]
-        y_s[1, at] = made[:, 128:]
+        tiles = [arrived[pl.ds(2 * t + u, OWNERS, stride=8), :] for u in range(2)]
+        modes.append(jnp.concatenate(tiles, axis=1))
+    mh, ml = split(jnp.concatenate(modes, axis=0))
+    along_x = device_waves(waves, steps, place)
+    along_x = (along_x[0] * BACK, along_x[1] * BACK)
+    for x in range(0, 16, 8):
+        pair = wave_rows(along_x, waves[2], waves[3], range(x, x + 8))
+        for part in range(2):
+            th, tl = split(pair[part])
+            made = mm(th, mh) + mm(th, ml) + mm(tl, mh)
+            at = slice(256 * part + 16 * x, 256 * part + 16 * x + 128)
+            y_s[0, at] = made[:, :128]
+            y_s[1, at] = made[:, 128:]
     quarter = lax.broadcasted_iota(jnp.int32, (32, 128), 1) // 32
     for y in range(0, 16, 4):
         for k in range(0, 8, 4):
@@ -304,14 +325,9 @@
     project, project_bias,
 ):
     gx, gy = lax.axis_index("gx"), lax.axis_index("gy")
-    fx, fy = mode_frequencies()
-    turns = (jnp.asarray(2 * fx, jnp.int32) * gx + jnp.asarray(fy, jnp.int32) * gy) % 16
-    angle = turns.astype(F32) * (2.0 * math.pi / 16)
-    cos, sin = jnp.cos(angle), jnp.sin(angle)
-    first_phase = jnp.stack([cos[0], sin[0], cos[1], sin[1]], axis=1)
-    lanes = [jnp.repeat(v[:, None], 2, axis=1).reshape(1, 512) for v in (cos, sin)]
-    lane_phase = jnp.concatenate(lanes, axis=0)
-    row_phase = lane_phase.T
+    place = jnp.stack([gx, gy]).astype(jnp.int32)
+    waves, steps = wave_tables(), phase_steps()
+    z_back, z_fwd = inverse_z_table(), forward_z_table()
 
     eye8 = jnp.eye(8, dtype=F32)
     pool_mix = product("ed,dc->ce", bypass_in, lift)
@@ -328,48 +344,48 @@
     constant = project_bias + product("od,d->o", project, lift_bias)
     at_zero = ((gx == 0) & (gy == 0)).astype(F32) * math.sqrt(TOTAL)
     bias_column = lift_bias[:, None] * (jnp.arange(32) == 0).astype(F32)[None, :] * at_zero
-    lift_wide = jnp.tile(lift, (1, 32))
+    lift_wide = jnp.tile(jnp.repeat(lift, KZ, axis=1), (1, 4))
 
     call = functools.partial(pl.pallas_call, compiler_params=PARAMS)
     spectrum = call(
         first_spectrum,
         out_shape=jax.ShapeDtypeStruct((OWNERS, 128), F32),
-        in_specs=[VMEM] * 4, out_specs=VMEM, name="first_spectrum",
-    )(fields, first_z_table(), first_places_table(), first_phase)
+        in_specs=[SMEM, pl.BlockSpec(memory_space=pl.ANY)] + [VMEM] * 3, out_specs=VMEM,
+        scratch_shapes=[
+            pltpu.VMEM((CIN, 16, 16, NZ), F32), pltpu.SemaphoreType.DMA((CIN,)),
+        ],
+        name="first_spectrum",
+    )(place, fields, waves, steps, z_fwd)
     mixed = call(
         first_mix,
-        out_shape=jax.ShapeDtypeStruct((OWNERS, 2048), F32),
+        out_shape=jax.ShapeDtypeStruct((OWNERS, 16, 128), F32),
         in_specs=[VMEM] * 4, out_specs=VMEM, name="first_mix",
     )(exchange(spectrum), lift_wide, bias_column, spectral_in)
-    half = place_angles(np.arange(8), np.arange(8), NX // 2, NY // 2)
-    whole = place_angles(np.arange(16), np.arange(16), NX, NY)
-    z_back = inverse_z_table()
     spectrum, skip = call(
         coarse_level,
         out_shape=(
-            jax.ShapeDtypeStruct((OWNERS, 2048), F32),
+            jax.ShapeDtypeStruct((OWNERS * 16, 128), F32),
             jax.ShapeDtypeStruct((8, NZ, 512), F32),
         ),
-        in_specs=[VMEM] * 14, out_specs=(VMEM, VMEM), name="coarse_level",
-        scratch_shapes=[pltpu.VMEM((4, 128, 128), F32)] * 3 + [pltpu.VMEM((128, 512), F32)],
+        in_specs=[SMEM] + [VMEM] * 10, out_specs=(VMEM, VMEM), name="coarse_level",
+        scratch_shapes=[pltpu.VMEM((4, 128, 128), F32)] * 4,
     )(
-        exchange(mixed), *inverse_tables(half, BACK),
-        *forward_tables(half, 1.0 / math.sqrt(TOTAL / 4.0)), lane_phase, row_phase, fields,
-        z_back, forward_z_table(), pool_mix, pool_bias, wide_mix, wide_bias,
+        place, exchange(mixed).reshape(OWNERS * 16, 128), waves, steps, fields,
+        z_back, z_fwd, pool_mix, pool_bias, wide_mix, wide_bias,
     )
     mixed = call(
         second_mix,
-        out_shape=jax.ShapeDtypeStruct((OWNERS, 1024), F32),
+        out_shape=jax.ShapeDtypeStruct((OWNERS, 8, 128), F32),
         in_specs=[VMEM] * 2, out_specs=VMEM, name="second_mix",
-    )(exchange(spectrum), spectral_out)
+    )(exchange(spectrum.reshape(OWNERS, 16, 128)), spectral_out)
     return call(
         fine_level,
         out_shape=jax.ShapeDtypeStruct((CIN, 16, 16, NZ), F32),
-        in_specs=[SMEM] * 2 + [VMEM] * 8, out_specs=VMEM, name="fine_level",
+        in_specs=[SMEM] * 3 + [VMEM] * 7, out_specs=VMEM, name="fine_level",
         scratch_shapes=[pltpu.VMEM((2, 512, 128), F32), pltpu.VMEM((4, 256, 128), F32)],
     )(
-        through, constant, exchange(mixed), *inverse_tables(whole, BACK), lane_phase, fields,
-        z_back, skip, project_wide,
+        place, through, constant, exchange(mixed).reshape(OWNERS * 8, 128), waves, steps,
+        fields, z_back, skip, project_wide,
     )
 
 

time: 125 us -> 122 us (0.976)
  waiting for transfers between devices: 57.2 us -> 52 us
  Pallas kernels: 19.5 us -> 24 us
  local copies, waits for them, and re-layouts: 17.6 us -> 14.7 us
  matrix products: 0.52 us -> 3.1 us
  starting transfers between devices: 27.5 us -> 25.3 us
    all_to_all x3 -> x0, local copies, waits for them, and re-layouts: 5.43 us -> none  [exchange(): return lax.all_to_all(tiles, AXES, split_axis=0, concat_axis=0, tiled=True)]
    all_to_all x4, waiting for transfers between devices: 57.2 us -> 52 us  [exchange(): return lax.all_to_all(tiles, AXES, split_axis=0, concat_axis=0, tiled=True)]
    pallas_call x3, Pallas kernels: 7.83 us -> 10.8 us  [the longest x1 8.51 us: on_device(): call(coarse_level, out_shape=(jax.ShapeDtypeStruct((OWNERS * 16, 128), F3...]
    dot_general x4, matrix products: 0.52 us -> 3.1 us  [product(): return jnp.einsum(formula, left, right, precision=lax.Precision.HIGHEST)]
    mul x2, local copies, waits for them, and re-layouts: 0.35 us -> 2.92 us  [on_device(): project.T[None, :, :, None] * eye16[:, None, None, :]]
    all_to_all x4, starting transfers between devices: 27.5 us -> 25.3 us  [exchange(): return lax.all_to_all(tiles, AXES, split_axis=0, concat_axis=0, tiled=True)]
    pallas_call x1, Pallas kernels: 1.91 us -> 3.21 us  [on_device(): call(first_spectrum, out_shape=jax.ShapeDtypeStruct((OWNERS, 128), F32),...]
    unnamed x54 -> x57, local copies, waits for them, and re-layouts: 10.3 us -> 10.4 us
  transfers between devices with their start and end apart: 4 -> 4, of which waited for: 4 -> 4; matrix products, arithmetic and copies ran while one was open for 3% -> 8% of each run, Pallas kernels for 0% -> 0%
where the time goes in v1:
time: 122 us; the launch traced here: 121 us
  waiting for transfers between devices  52 us (43%)
  starting transfers between devices  25.3 us (21%)
  Pallas kernels  24 us (20%)
  local copies, waits for them, and re-layouts  14.7 us (12%)
  matrix products  3.1 us (3%)
  other arithmetic  1.92 us (2%)
    all_to_all x4, waiting for transfers between devices, exchange(): return lax.all_to_all(tiles, AXES, split_axis=0, concat_axis=0, tiled=True)  52 us
    all_to_all x4, starting transfers between devices, exchange(): return lax.all_to_all(tiles, AXES, split_axis=0, concat_axis=0, tiled=True)  25.3 us
    unnamed x57, local copies, waits for them, and re-layouts  10.4 us
    pallas_call x1, Pallas kernels, on_device(): call(fine_level, out_shape=jax.ShapeDtypeStruct((CIN, 16, 16, NZ), F32),...  9.96 us
    pallas_call x1, Pallas kernels, on_device(): call(coarse_level, out_shape=(jax.ShapeDtypeStruct((OWNERS * 16, 128), F3...  8.51 us
    pallas_call x1, Pallas kernels, on_device(): call(first_spectrum, out_shape=jax.ShapeDtypeStruct((OWNERS, 128), F32),...  3.21 us
    dot_general x4, matrix products, product(): return jnp.einsum(formula, left, right, precision=lax.Precision.HIGHEST)  3.1 us
    mul x2, local copies, waits for them, and re-layouts, on_device(): project.T[None, :, :, None] * eye16[:, None, None, :]  2.92 us
  transfers between devices with their start and end apart: 4, of which 4 were waited for; matrix products, arithmetic and copies ran while one was open for 8% of the time, Pallas kernels for 0%

profile of v1, /device:TPU:1, one launch (start us, length us, event | category | flops | bytes accessed | tf_op | source)
XLA Modules:
  0.0 121.4 jit_solution(15925320146047376468)
XLA Ops:
  0.1 1.0 copy-done.1
  1.1 0.9 copy-done.6
  3.4 3.2 %first_spectrum.1 = f32[128,128]{1,0:T(8,128)} custom-call(s32[2]{0:T(128)S(1)} %pad_add_fusion.place, f32[4,16,16,128]{3,2,1,0:T(8,128)S(1)} %copy-done.1, f32[4,16,512]{2,1,0:T(8,128)S(1)} %copy-done.6, s32[2,512]{1,0:T(2,128)S(1)} %copy-done.11, bf16[32,128]{1,0:T(8,128)(2,1)S(1)} %copy-done.14), custom_call_target="tpu_custom_call" | custom-call | tf_op jit(solution)/shard_map/first_spectrum/pallas_call | solution.py:350
  6.7 11.5 %all-to-all-start = ((f32[128,1,128]{2,1,0:T(1,128)}), f32[128,1,128]{2,1,0:T(1,128)S(1)}, u32[]{:S(2)}, u32[]{:S(2)}) async-start(f32[128,1,128]{2,1,0:T(1,128)} %bitcast.5), calls=%async_computation | async-start | bytes 131072 | tf_op jit(solution)/shard_map/all_to_all | solution.py:316
  19.8 8.1 %all-to-all-done = f32[128,1,128]{2,1,0:T(1,128)S(1)} async-done(((f32[128,1,128]{2,1,0:T(1,128)}), f32[128,1,128]{2,1,0:T(1,128)S(1)}, u32[]{:S(2)}, u32[]{:S(2)}) %all-to-all-start) | async-done | bytes 65568 | tf_op jit(solution)/shard_map/all_to_all | solution.py:316
  27.9 1.0 copy-done.8
  29.0 1.6 %first_mix.1 = f32[128,16,128]{2,1,0:T(8,128)} custom-call(f32[128,128]{1,0:T(8,128)S(1)} %bitcast.43, f32[32,128]{1,0:T(8,128)S(1)} %tile.24.lift_wide, f32[32,32]{1,0:T(8,128)S(1)} %multiply_multiply_fusion.bias_column, f32[2,2,8,32,64]{4,3,2,1,0:T(8,128)S(1)} %copy-done.8), custom_call_target="tpu_custom_call" | custom-call | tf_op jit(solution)/shard_map/first_mix/pallas_call | solution.py:359
  30.5 4.3 %all-to-all-start.1 = ((f32[128,16,128]{2,1,0:T(8,128)}), f32[128,16,128]{2,1,0:T(8,128)S(1)}, u32[]{:S(2)}, u32[]{:S(2)}) async-start(f32[128,16,128]{2,1,0:T(8,128)} %first_mix.1), calls=%async_computation.1 | async-start | bytes 2097152 | tf_op jit(solution)/shard_map/all_to_all | solution.py:316
  35.9 17.8 %all-to-all-done.1 = f32[128,16,128]{2,1,0:T(8,128)S(1)} async-done(((f32[128,16,128]{2,1,0:T(8,128)}), f32[128,16,128]{2,1,0:T(8,128)S(1)}, u32[]{:S(2)}, u32[]{:S(2)}) %all-to-all-start.1) | async-done | bytes 1048608 | tf_op jit(solution)/shard_map/all_to_all | solution.py:316
  53.7 8.5 %coarse_level.1 = (f32[2048,128]{1,0:T(8,128)}, f32[8,128,512]{2,1,0:T(8,128)S(1)}) custom-call(s32[2]{0:T(128)S(1)} %pad_add_fusion.place, f32[2048,128]{1,0:T(8,128)S(1)} %bitcast.41, f32[4,16,512]{2,1,0:T(8,128)S(1)} %copy-done.7, s32[2,512]{1,0:T(2,128)S(1)} %copy-done.12, f32[4,16,16,128]{3,2,1,0:T(8,128)S(1)} %copy-done.2, ...), custom_call_target="tpu_custom_call" | custom-call | tf_op jit(solution)/shard_map/coarse_level/pallas_call | solution.py:364
  62.3 1.3 %copy-done.3 = f32[8,128,512]{2,1,0:T(8,128)} copy-done((f32[8,128,512]{2,1,0:T(8,128)}, f32[8,128,512]{2,1,0:T(8,128)S(1)}, u32[]{:S(2)}) %copy-start.3) | copy-done | bytes 2097176
  63.6 4.7 %all-to-all-start.2 = ((f32[128,16,128]{2,1,0:T(8,128)}), f32[128,16,128]{2,1,0:T(8,128)S(1)}, u32[]{:S(2)}, u32[]{:S(2)}) async-start(f32[128,16,128]{2,1,0:T(8,128)} %bitcast.12), calls=%async_computation.2 | async-start | bytes 2097152 | tf_op jit(solution)/shard_map/all_to_all | solution.py:316
  68.7 18.6 %all-to-all-done.2.arrived = f32[128,16,128]{2,1,0:T(8,128)S(1)} async-done(((f32[128,16,128]{2,1,0:T(8,128)}), f32[128,16,128]{2,1,0:T(8,128)S(1)}, u32[]{:S(2)}, u32[]{:S(2)}) %all-to-all-start.2) | async-done | bytes 1048608 | tf_op jit(solution)/shard_map/all_to_all | solution.py:316
  87.3 0.8 second_mix.1
  88.1 0.8 copy-done.5
  88.9 4.8 %all-to-all-start.3 = ((f32[128,8,128]{2,1,0:T(8,128)}), f32[128,8,128]{2,1,0:T(8,128)S(1)}, u32[]{:S(2)}, u32[]{:S(2)}) async-start(f32[128,8,128]{2,1,0:T(8,128)} %copy-done.5), calls=%async_computation.3 | async-start | bytes 1048576 | tf_op jit(solution)/shard_map/all_to_all | solution.py:316
  93.7 0.9 broadcast_multiply_fusion
  94.6 1.9 %mul.90 = f32[512,64]{0,1:T(8,128)} reshape(f32[16,32,4,16]{1,0,3,2:T(8,128)} %broadcast_multiply_fusion) | data formatting | bytes 262144 | tf_op jit(solution)/shard_map/mul | solution.py:342
  96.5 1.0 copy.29.project_wide
  97.6 1.4 %fusion.1.constant = f32[4]{0:T(128)} fusion(f32[4]{0:T(128)} %param.26, f32[4,32]{1,0:T(4,128)} %param.25, f32[32]{0:T(128)} %param.18), kind=kOutput, calls=%fused_computation.3 | convolution fusion | flops 1540 | bytes 672 | tf_op jit(solution)/shard_map/od,d->o/dot_general | solution.py:320
  99.0 1.4 %fusion.6.through = f32[4,4]{1,0:T(4,128)} fusion(f32[4,32]{1,0:T(4,128)} %param.25, f32[32,4]{0,1:T(4,128)} %param.17), kind=kOutput, calls=%fused_computation.17 | convolution fusion | flops 6144 | bytes 1088 | tf_op jit(solution)/shard_map/od,dc->oc/dot_general | solution.py:320
  100.4 7.5 %all-to-all-done.3 = f32[128,8,128]{2,1,0:T(8,128)S(1)} async-done(((f32[128,8,128]{2,1,0:T(8,128)}), f32[128,8,128]{2,1,0:T(8,128)S(1)}, u32[]{:S(2)}, u32[]{:S(2)}) %all-to-all-start.3) | async-done | bytes 524320 | tf_op jit(solution)/shard_map/all_to_all | solution.py:316
  107.9 0.8 copy-done.10
  111.4 10.0 %fine_level.1 = f32[4,16,16,128]{3,2,1,0:T(8,128)} custom-call(s32[2]{0:T(128)S(1)} %copy-done.18, f32[4,4]{1,0:T(4,128)S(1)} %copy-done.16, f32[4]{0:T(128)S(1)} %copy-done.19, f32[1024,128]{1,0:T(8,128)S(1)} %bitcast.42, f32[4,16,512]{2,1,0:T(8,128)S(1)} %copy-done.7, s32[2,512]{1,0:T(2,128)S(1)} %copy-done.13, f32[4,16,16,128]{3,2,1,0:T(8,128)S(1)} %copy-done.2, ...), custom_call_target="tpu_custom_call" | custom-call | tf_op jit(solution)/shard_map/fine_level/pallas_call | solution.py:381
  (71 shorter events, 7.2 us)
Async XLA Ops:
  0.0 35.2 %copy-start = (f32[64,32]{0,1:T(8,128)S(1)}, f32[64,32]{0,1:T(8,128)}, u32[]{:S(2)}) copy-start(f32[64,32]{0,1:T(8,128)} %param.20) | copy-start | bytes 24580
  0.1 1.0 copy-start.1
  1.1 0.9 copy-start.6
  3.4 50.3 %copy-start.17 = (s32[2]{0:T(128)}, s32[2]{0:T(128)S(1)}, u32[]{:S(2)}) copy-start(s32[2]{0:T(128)S(1)} %pad_add_fusion.place) | copy-start | bytes 28
  6.6 28.2 %copy-start.22 = (f32[32,64]{1,0:T(8,128)S(1)}, f32[32,64]{1,0:T(8,128)}, u32[]{:S(2)}) copy-start(f32[32,64]{1,0:T(8,128)} %param.23) | copy-start | bytes 24580
  6.6 28.2 %copy-start.24 = (f32[2,4]{0,1:T(4,128)S(1)}, f32[2,4]{0,1:T(4,128)}, u32[]{:S(2)}) copy-start(f32[2,4]{0,1:T(4,128)} %constant.26.clone) | copy-start | bytes 100
  6.7 21.2 %all-to-all-start = ((f32[128,1,128]{2,1,0:T(1,128)}), f32[128,1,128]{2,1,0:T(1,128)S(1)}, u32[]{:S(2)}, u32[]{:S(2)}) async-start(f32[128,1,128]{2,1,0:T(1,128)} %bitcast.5), calls=%async_computation | async-start | bytes 131072 | tf_op jit(solution)/shard_map/all_to_all | solution.py:316
  27.9 1.0 copy-start.8
  28.9 6.3 %copy-start.21 = (f32[32,4]{0,1:T(4,128)S(1)}, f32[32,4]{0,1:T(4,128)}, u32[]{:S(2)}) copy-start(f32[32,4]{0,1:T(4,128)} %param.17) | copy-start | bytes 1540
  28.9 6.6 %copy-start.25 = (f32[32]{0:T(128)S(1)}, f32[32]{0:T(128)}, u32[]{:S(2)}) copy-start(f32[32]{0:T(128)} %param.18) | copy-start | bytes 388
  28.9 6.6 %copy-start.26 = (f32[64]{0:T(128)S(1)}, f32[64]{0:T(128)}, u32[]{:S(2)}) copy-start(f32[64]{0:T(128)} %param.21) | copy-start | bytes 772
  28.9 6.9 %copy-start.27 = (f32[32]{0:T(128)S(1)}, f32[32]{0:T(128)}, u32[]{:S(2)}) copy-start(f32[32]{0:T(128)} %param.24) | copy-start | bytes 388
  28.9 24.8 %copy-start.2 = (f32[4,16,16,128]{3,2,1,0:T(8,128)S(1)}, f32[4,16,16,128]{3,2,1,0:T(8,128)}, u32[]{:S(2)}) copy-start(f32[4,16,16,128]{3,2,1,0:T(8,128)} %fields.5) | copy-start | bytes 1572868
  28.9 24.8 %copy-start.7 = (f32[4,16,512]{2,1,0:T(8,128)S(1)}, f32[4,16,512]{2,1,0:T(8,128)}, u32[]{:S(2)}) copy-start(f32[4,16,512]{2,1,0:T(8,128)} %constant.27.clone.waves) | copy-start | bytes 393220
  28.9 24.8 %copy-start.9 = (bf16[128,48]{1,0:T(8,128)(2,1)S(1)}, bf16[128,48]{1,0:T(8,128)(2,1)}, u32[]{:S(2)}) copy-start(bf16[128,48]{1,0:T(8,128)(2,1)} %constant.30.clone.z_back) | copy-start | bytes 36868
  29.0 24.8 %copy-start.12 = (s32[2,512]{1,0:T(2,128)S(1)}, s32[2,512]{1,0:T(2,128)}, u32[]{:S(2)}) copy-start(s32[2,512]{1,0:T(2,128)} %constant.28.clone.steps) | copy-start | bytes 12292
  29.0 24.8 %copy-start.15 = (bf16[32,128]{1,0:T(8,128)(2,1)S(1)}, bf16[32,128]{1,0:T(8,128)(2,1)}, u32[]{:S(2)}) copy-start(bf16[32,128]{1,0:T(8,128)(2,1)} %constant.29.clone.z_fwd) | copy-start | bytes 24580
  30.5 23.2 %all-to-all-start.1 = ((f32[128,16,128]{2,1,0:T(8,128)}), f32[128,16,128]{2,1,0:T(8,128)S(1)}, u32[]{:S(2)}, u32[]{:S(2)}) async-start(f32[128,16,128]{2,1,0:T(8,128)} %first_mix.1), calls=%async_computation.1 | async-start | bytes 2097152 | tf_op jit(solution)/shard_map/all_to_all | solution.py:316
  35.4 32.9 %copy-start.20 = (f32[2,2,8,64,32]{3,4,2,1,0:T(8,128)S(1)}, f32[2,2,8,64,32]{3,4,2,1,0:T(8,128)}, u32[]{:S(2)}) copy-start(f32[2,2,8,64,32]{3,4,2,1,0:T(8,128)} %param.22) | copy-start | bytes 786436
  62.3 1.3 %copy-start.3 = (f32[8,128,512]{2,1,0:T(8,128)}, f32[8,128,512]{2,1,0:T(8,128)S(1)}, u32[]{:S(2)}) copy-start(f32[8,128,512]{2,1,0:T(8,128)S(1)} %get-tuple-element.8.skip) | copy-start | bytes 6291460
  63.6 23.7 %all-to-all-start.2 = ((f32[128,16,128]{2,1,0:T(8,128)}), f32[128,16,128]{2,1,0:T(8,128)S(1)}, u32[]{:S(2)}, u32[]{:S(2)}) async-start(f32[128,16,128]{2,1,0:T(8,128)} %bitcast.12), calls=%async_computation.2 | async-start | bytes 2097152 | tf_op jit(solution)/shard_map/all_to_all | solution.py:316
  68.7 25.0 %copy-start.23 = (f32[4,32]{1,0:T(4,128)S(1)}, f32[4,32]{1,0:T(4,128)}, u32[]{:S(2)}) copy-start(f32[4,32]{1,0:T(4,128)} %param.25) | copy-start | bytes 1540
  88.9 19.1 %copy-start.4 = (f32[8,128,512]{2,1,0:T(8,128)S(1)}, f32[8,128,512]{2,1,0:T(8,128)}, u32[]{:S(2)}) copy-start(f32[8,128,512]{2,1,0:T(8,128)} %copy-done.3) | copy-start | bytes 6291460
  88.9 19.1 %all-to-all-start.3 = ((f32[128,8,128]{2,1,0:T(8,128)}), f32[128,8,128]{2,1,0:T(8,128)S(1)}, u32[]{:S(2)}, u32[]{:S(2)}) async-start(f32[128,8,128]{2,1,0:T(8,128)} %copy-done.5), calls=%async_computation.3 | async-start | bytes 1048576 | tf_op jit(solution)/shard_map/all_to_all | solution.py:316
  (8 other events, 5.7 us)

commit v2 on v1

v2 whole, which is shorter than its diff:
```python
import functools
import math

import jax
import jax.numpy as jnp
import numpy as np
from jax import lax
from jax.experimental import pallas as pl
from jax.experimental.pallas import tpu as pltpu
from jax.sharding import PartitionSpec as P

KX, KY, KZ = 16, 16, 8
NX, NY, NZ = 128, 256, 128
CIN, C1, C2 = 4, 32, 64
AXES = ("gx", "gy")
OWNERS = 128
TOTAL = NX * NY * NZ
BACK = math.sqrt(2.0 / (KX * KY * KZ))
F32 = jnp.float32
BF16 = jnp.bfloat16
UNROLL = 2
VMEM = pl.BlockSpec(memory_space=pltpu.VMEM)
HBM = pl.BlockSpec(memory_space=pltpu.HBM)
PARAMS = pltpu.CompilerParams(vmem_limit_bytes=40 << 20)


def mode_frequencies():
    centered = np.where(np.arange(16) < 8, np.arange(16), np.arange(16) - 16)
    n = np.arange(OWNERS)
    fx = np.stack([centered[n // 8]] * 2)
    fy = np.stack([centered[2 * (n % 8) + s] for s in range(2)])
    return fx, fy


def place_angles(xs, ys, x_length, y_length):
    fx, fy = mode_frequencies()
    turns = (
        fx[:, :, None, None] * xs[None, None, :, None] / x_length
        + fy[:, :, None, None] * ys[None, None, None, :] / y_length
    )
    return 2.0 * np.pi * turns


def wave_tables():
    fx, fy = mode_frequencies()
    ahead = np.array([0.0, 0.5 * np.pi])[None, None, :, None]
    places = np.arange(16)[:, None, None, None]
    along_x = 2.0 * np.pi * places * fx[None, :, None, :] / NX + ahead
    along_y = 2.0 * np.pi * places * fy[None, :, None, :] / NY + 0.0 * ahead
    tables = [np.cos(along_x), np.sin(along_x), np.cos(along_y), np.sin(along_y)]
    return np.stack(tables).reshape(4, 16, 512).astype(np.float32)


def phase_steps():
    fx, fy = mode_frequencies()
    steps = np.stack([np.stack([2 * fx, 2 * fx], axis=1), np.stack([fy, fy], axis=1)])
    return steps.reshape(2, 512).astype(np.int32)


def z_angles():
    return 2.0 * np.pi * (np.arange(NZ)[:, None] * np.arange(KZ)[None, :] % NZ) / NZ


def split_np(table):
    high = table.astype(BF16)
    low = (table - high.astype(np.float32)).astype(BF16)
    return high, low


def inverse_z_table():
    table = np.stack([np.cos(z_angles()), -np.sin(z_angles())], axis=2)
    high, low = split_np(table.reshape(NZ, 16).astype(np.float32))
    return np.concatenate([high.T, high.T, low.T], axis=0)


def forward_z_table():
    table = np.stack([np.cos(z_angles()).T, -np.sin(z_angles()).T], axis=0)
    high, low = split_np(table.reshape(16, NZ).astype(np.float32))
    return np.block([[high, high], [low, np.zeros_like(low)]])


def split(x):
    high = x.astype(BF16)
    return high, (x - high.astype(F32)).astype(BF16)


def mm(a, b, dims=((1,), (0,))):
    return lax.dot_general(a, b, (dims, ((), ())), preferred_element_type=F32)


def mm3(a, b, dims=((1,), (0,))):
    ah, al = split(a)
    bh, bl = split(b)
    return mm(ah, bh, dims) + mm(ah, bl, dims) + mm(al, bh, dims)


def exact(a, b, dims=((1,), (0,))):
    return lax.dot_general(
        a, b, (dims, ((), ())), precision=lax.Precision.HIGHEST, preferred_element_type=F32
    )


def iota(shape, dim):
    return lax.broadcasted_iota(jnp.int32, shape, dim)


def ones_where(condition):
    return jnp.where(condition, 1.0, 0.0).astype(F32)


def gelu(x):
    return 0.5 * x * (1.0 + lax.erf(x * math.sqrt(0.5)))


def regroup(rows):
    group = iota(rows[0].shape, 1) // 32
    made = []
    for v in range(4):
        total = rows[v]
        for u in range(4):
            if u != v:
                moved = pltpu.roll(rows[u], ((u - v) % 4) * 32, 1)
                total = jnp.where(group == u, moved, total)
        made.append(total)
    return made


def my_place():
    return lax.axis_index("gx"), lax.axis_index("gy")


def device_waves(waves, steps, place):
    turns = (steps[0:1] * place[0] + steps[1:2] * place[1]) & 15
    angle = turns.astype(F32) * (2.0 * math.pi / 16)
    cos, sin = jnp.cos(angle), jnp.sin(angle)
    return waves[0] * cos - waves[1] * sin, waves[1] * cos + waves[0] * sin


def wave_rows(along_x, cos_y, sin_y, xs):
    cos_x, sin_x = along_x
    real = [cos_x[x : x + 1] * cos_y - sin_x[x : x + 1] * sin_y for x in xs]
    imag = [sin_x[x : x + 1] * cos_y + cos_x[x : x + 1] * sin_y for x in xs]
    return jnp.concatenate(real, axis=0), jnp.concatenate(imag, axis=0)


def first_spectrum(fields, waves_h, steps_h, z_fwd_h, out, fields_v, waves, steps, z_fwd, sems):
    pairs = [(waves_h, waves), (steps_h, steps), (z_fwd_h, z_fwd)]
    pairs += [(fields.at[ch], fields_v.at[ch]) for ch in range(CIN)]
    copies = [
        pltpu.make_async_copy(source, target, sems.at[i])
        for i, (source, target) in enumerate(pairs)
    ]
    for copy in copies:
        copy.start()
    for copy in copies[:3]:
        copy.wait()
    along_x = device_waves(waves, steps, my_place())
    real, imag = wave_rows(along_x, waves[2], waves[3], range(16))
    nt = ((1,), (1,))
    parts = [[], []]
    for ch in range(CIN):
        copies[3 + ch].wait()
        fh, fl = split(fields_v[ch].reshape(256, NZ))
        made = mm(z_fwd[...], jnp.concatenate([fh, fl], axis=1), nt)
        made = made[:16] + made[16:]
        parts[0].append(made[:8])
        parts[1].append(made[8:])
    total = mm3(jnp.concatenate(parts[0], axis=0), real)
    total += mm3(jnp.concatenate(parts[1], axis=0), imag)
    total *= 1.0 / math.sqrt(TOTAL)
    tiles = [total[:, 128 * t : 128 * t + 128] for t in range(4)]
    out[...] = jnp.concatenate(tiles, axis=0).T


def prepare(
    after, waves, steps, fields, lift, lift_bias, bypass_in, bias_in, bypass_out, bias_out,
    project, project_bias, coarse_t, spread_t, fine_t, pool_mix, pool_bias, wide_mix, wide_bias,
    project_mix, base,
):
    nt = ((1,), (1,))
    gx, gy = my_place()
    own = device_waves(waves, steps, (gx, gy))
    mate = device_waves(waves, steps, (gx + 1 - 2 * (gx % 2), gy))
    cos_y = jnp.concatenate([waves[2, 2 * q : 2 * q + 1] for q in range(8)], axis=0)
    sin_y = jnp.concatenate([waves[3, 2 * q : 2 * q + 1] for q in range(8)], axis=0)
    tables = [
        jnp.concatenate(wave_rows(along, cos_y, sin_y, range(0, 16, 2)), axis=0)
        for along in (own, mate)
    ]
    coarse_t[0], coarse_t[1] = split(tables[0] * BACK)
    scale = 1.0 / math.sqrt(TOTAL / 4.0)
    for patch in range(2):
        at = slice(128 * patch, 128 * patch + 128)
        high, less = split(tables[patch].T * scale)
        spread_t[0, :, at] = high
        spread_t[1, :, at] = less
    scaled = (own[0] * BACK, own[1] * BACK)
    for x in range(0, 16, 8):
        pair = wave_rows(scaled, waves[2], waves[3], range(x, x + 8))
        for part in range(2):
            at = slice(256 * part + 16 * x, 256 * part + 16 * x + 128)
            high, less = split(pair[part])
            fine_t[0, at] = high
            fine_t[1, at] = less

    lanes = [
        ones_where(iota((C2, 128), 0) == 32 * h + iota((C2, 128), 1) % 32) for h in range(2)
    ]
    through = exact(lift[...], bypass_in[...], ((0,), (1,)))
    through = exact(ones_where(iota((32, CIN), 0) // 8 == iota((32, CIN), 1)), through)
    offset = bias_in[...] + exact(lift_bias[...], bypass_in[...], nt)
    for t in range(4):
        at = slice(128 * t, 128 * t + 128)
        same = iota((32, 128), 0) % 8 == 4 * (t // 2) + iota((32, 128), 1) // 32
        high, less = split(jnp.where(same, exact(through, lanes[t % 2]), 0.0))
        pool_mix[:, at] = jnp.concatenate([high, less, high], axis=0)
        pool_bias[:, at] = exact(offset, lanes[t % 2])
    spread_d = ones_where(iota((C1, 256), 0) == iota((C1, 256), 1) % 32)
    same = iota((128, 256), 0) // 32 == iota((128, 256), 1) // 64
    for h in range(2):
        pick = ones_where(iota((128, C2), 1) == 32 * h + iota((128, C2), 0) % 32)
        wide = exact(exact(pick, bypass_out[...], nt), spread_d)
        high, less = split(jnp.where(same, wide, 0.0))
        wide_mix[0, 128 * h : 128 * h + 128] = high
        wide_mix[1, 128 * h : 128 * h + 128] = less
    wide_bias[...] = exact(bias_out[...], spread_d)
    pick = ones_where(iota((512, C1), 1) == iota((512, C1), 0) % 32)
    onto = ones_where(iota((CIN, 128), 0) == iota((CIN, 128), 1) % 64 // 16)
    made = exact(exact(pick, project[...], nt), onto)
    lane = iota((512, 128), 1)
    made = jnp.where(iota((512, 128), 0) // 32 == lane % 16, made, 0.0)
    high = made.astype(BF16).astype(F32)
    project_mix[0] = jnp.where(lane < 64, high, made - high).astype(BF16)
    project_mix[1] = jnp.where(lane < 64, high, 0.0).astype(BF16)
    across = exact(project[...], lift[...])
    constant = project_bias[...] + exact(project[...], lift_bias[...], nt)

    def step(x, carry):
        for o in range(CIN):
            total = jnp.broadcast_to(constant[o : o + 1], (16, NZ))
            for ch in range(CIN):
                total += across[o : o + 1, ch : ch + 1] * fields[ch, x]
            base[o, x] = total
        return carry

    lax.fori_loop(0, 16, step, 0)


def mixed_row(columns, weights, wide):
    pieces = [[[None] * KZ for _ in range(2)] for _ in range(2)]
    for s in range(2):
        for k in range(KZ):
            real, imag = columns(s, 0, k), columns(s, 1, k)
            wr, wi = weights[s, 0, k], weights[s, 1, k]
            pieces[s][0][k] = jnp.sum(real * wr - imag * wi, axis=0, keepdims=True)
            pieces[s][1][k] = jnp.sum(real * wi + imag * wr, axis=0, keepdims=True)
    per = 128 // wide
    return [
        jnp.concatenate(
            [
                jnp.concatenate(
                    [v[:, at : at + wide] for v in pieces[s][part][k : k + per]], axis=1
                )
                for s in range(2)
                for part in range(2)
                for k in range(0, KZ, per)
            ],
            axis=0,
        )
        for at in range(0, weights.shape[-1], wide)
    ]


def first_mix(arrived, lift_wide, bias_column, weights, out):
    row = jnp.sum(arrived[...], axis=0, keepdims=True)
    source = lax.broadcasted_iota(jnp.int32, (128, 32), 0)
    source = source // 32 * 8 + source % 8
    pick = (source == lax.broadcasted_iota(jnp.int32, (128, 32), 1)).astype(F32)
    lifted = (
        lax.dot_general(
            lift_wide[...] * row, pick, (((1,), (0,)), ((), ())),
            precision=lax.Precision.HIGHEST, preferred_element_type=F32,
        )
        + bias_column[...]
    )

    def column(s, part, k):
        at = s * 16 + part * 8 + k
        return lifted[:, at : at + 1]

    halves = mixed_row(column, weights, 32)
    for n in range(OWNERS):
        out[n] = halves[n // 16 % 2]


def second_mix(arrived, weights, out):
    sums = [None, None]
    for n in range(OWNERS):
        half = n // 16 % 2
        sums[half] = arrived[n] if sums[half] is None else sums[half] + arrived[n]
    stacked = jnp.concatenate(sums + [jnp.zeros((112, 128), F32)], axis=0).T

    def column(s, part, k):
        at = (s * 2 + part) * 2 + k // 4
        rows = slice(k % 4 * 32, k % 4 * 32 + 32)
        return jnp.concatenate([stacked[rows, at : at + 1], stacked[rows, at + 8 : at + 9]], axis=0)

    (block,) = mixed_row(column, weights, 32)
    for n in range(OWNERS):
        out[n] = block


def coarse_level(
    mine, other, table, fields, z_back, z_fwd, pool_mix, pool_bias, wide_mix, wide_bias,
    kept, sent, skip, y_s, rhs_s, g_s, t_s, skip_v, sems,
):
    core = lax.axis_index("gx") % 2
    modes = []
    for t in range(4):
        tiles = [
            ref[pl.ds(2 * t + u, OWNERS, stride=8), :] for ref in (mine, other) for u in range(2)
        ]
        modes.append(jnp.concatenate(tiles, axis=1))
    mh, ml = split(jnp.concatenate(modes, axis=0))
    made = mm(table[0], mh) + mm(table[1], mh) + mm(table[0], ml)
    for u in range(2):
        for t in range(2):
            at = 128 * (2 * u + t)
            y_s[2 * ((core + u) % 2) + t] = made[:, at : at + 128]
    for h in range(2):
        for t in range(2):
            for q in range(2):
                made = regroup(
                    [y_s[2 * h + t, pl.ds(4 * q + u, 16, stride=8), :] for u in range(4)]
                )
                for v in range(4):
                    rhs_s[2 * q + h, pl.ds(16 * (4 * t + v), 16), :] = made[v]

    def step(p, carry):
        rows = [rhs_s[t, pl.ds(p, 16, stride=8), :] for t in range(4)]
        high, less = split(jnp.concatenate(rows, axis=1))
        pooled = []
        for ch in range(CIN):
            total = jnp.zeros((8, 128), F32)
            for dx in range(2):
                for dy in range(2):
                    total += fields[ch, 2 * p + dx, pl.ds(dy, 8, stride=2), :]
            pooled.append(total * 0.25)
        ph, pll = split(jnp.concatenate(pooled, axis=0))
        left = jnp.concatenate([z_back[...], ph, ph, pll], axis=0)
        right = jnp.concatenate([high, less, high, pool_mix[...]], axis=0)
        value = gelu(mm(left, right, ((0,), (0,))) + pool_bias[...])
        vh, vl = split(value)
        made = mm(z_fwd[...], jnp.concatenate([vh, vl], axis=0))
        made = made[:16] + made[16:]
        for t in range(4):
            at = slice(128 * t, 128 * t + 128)
            g_s[t, pl.ds(pl.multiple_of(p * 8, 8), 8), :] = made[:8, at]
            g_s[t, pl.ds(pl.multiple_of(p * 8 + 64, 8), 8), :] = made[8:, at]
        for q in range(2):
            at = slice(256 * q, 256 * q + 256)
            wide = mm(vh[:, at], wide_mix[0]) + mm(vh[:, at], wide_mix[1])
            skip_v[p, :, at] = wide + mm(vl[:, at], wide_mix[0]) + wide_bias[...]
        pltpu.make_async_copy(skip_v.at[p], skip.at[p], sems.at[p]).start()
        return carry

    lax.fori_loop(0, 8, step, 0, unroll=UNROLL)
    for h in range(2):
        for t in range(2):
            for q in range(2):
                made = regroup(
                    [g_s[2 * q + h, pl.ds(4 * t + v, 16, stride=8), :] for v in range(4)]
                )
                for u in range(4):
                    t_s[2 * h + t, pl.ds(4 * q + u, 16, stride=8), :] = made[u]
    for t in range(2):
        kept[t] = t_s[2 * core + t]
        sent[t] = t_s[2 * (1 - core) + t]
    for p in range(8):
        pltpu.make_async_copy(skip_v.at[p], skip.at[p], sems.at[p]).wait()


def spread(kept, got, table, out):
    rows = [jnp.concatenate([ref[0], ref[1]], axis=1) for ref in (kept, got)]
    th, tl = split(jnp.concatenate(rows, axis=0))
    for t in range(4):
        at = slice(128 * t, 128 * t + 128)
        made = mm(table[0, at], th) + mm(table[0, at], tl) + mm(table[1, at], th)
        for u in range(2):
            out[pl.ds(2 * t + u, OWNERS, stride=8), :] = made[:, 128 * u : 128 * u + 128]


def fine_level(
    arrived, table, z_back_h, skip, project_mix, base, out, y_s, rhs_s, skip_v, z_back, sems,
):
    copies = [pltpu.make_async_copy(skip.at[p], skip_v.at[p], sems.at[p]) for p in range(8)]
    copies.append(pltpu.make_async_copy(z_back_h, z_back, sems.at[8]))
    for copy in copies:
        copy.start()
    modes = []
    for t in range(4):
        tiles = [arrived[pl.ds(2 * t + u, OWNERS, stride=8), :] for u in range(2)]
        modes.append(jnp.concatenate(tiles, axis=1))
    mh, ml = split(jnp.concatenate(modes, axis=0))
    for t in range(4):
        at = slice(128 * t, 128 * t + 128)
        made = mm(table[0, at], mh) + mm(table[0, at], ml) + mm(table[1, at], mh)
        y_s[0, at] = made[:, :128]
        y_s[1, at] = made[:, 128:]
    for t in range(2):
        for y in range(4):
            made = regroup([y_s[t, pl.ds(4 * y + u, 32, stride=16), :] for u in range(4)])
            for v in range(4):
                rhs_s[y, pl.ds(32 * (4 * t + v), 32), :] = made[v]
    for copy in copies:
        copy.wait()

    def step(x, carry):
        rows = [rhs_s[t, pl.ds(x, 16, stride=16), :] for t in range(4)]
        high, less = split(jnp.concatenate(rows, axis=1))
        before = mm(z_back[...], jnp.concatenate([high, less, high], axis=0), ((0,), (0,)))
        vh, vl = split(gelu(before + skip_v[x // 2]))
        made = (mm(vh, project_mix[0]) + mm(vl, project_mix[1])).T
        made = made[:64] + made[64:]
        for o in range(CIN):
            out[o, x] = made[16 * o : 16 * o + 16] + base[o, x]
        return carry

    lax.fori_loop(0, 16, step, 0, unroll=UNROLL)


def exchange(tiles):
    return lax.all_to_all(tiles, AXES, split_axis=0, concat_axis=0, tiled=True)


def between_cores(array):
    return lax.ppermute(array, "gx", [(i, i ^ 1) for i in range(lax.axis_size("gx"))])


def on_device(
    fields, lift, lift_bias, spectral_in, bypass_in, bias_in, spectral_out, bypass_out, bias_out,
    project, project_bias,
):
    gx, gy = lax.axis_index("gx"), lax.axis_index("gy")
    waves, steps = wave_tables(), phase_steps()
    z_back, z_fwd = inverse_z_table(), forward_z_table()
    at_zero = ((gx == 0) & (gy == 0)).astype(F32) * math.sqrt(TOTAL)
    bias_column = lift_bias[:, None] * (jnp.arange(32) == 0).astype(F32)[None, :] * at_zero
    lift_wide = jnp.tile(jnp.repeat(lift, KZ, axis=1), (1, 4))

    call = functools.partial(pl.pallas_call, compiler_params=PARAMS)
    shape = jax.ShapeDtypeStruct
    dma = pltpu.SemaphoreType.DMA
    spectrum = call(
        first_spectrum,
        out_shape=shape((OWNERS, 128), F32),
        in_specs=[HBM] * 4, out_specs=VMEM,
        scratch_shapes=[
            pltpu.VMEM((CIN, 16, 16, NZ), F32), pltpu.VMEM((4, 16, 512), F32),
            pltpu.VMEM((2, 512), jnp.int32), pltpu.VMEM((32, 2 * NZ), BF16), dma((7,)),
        ],
        name="first_spectrum",
    )(fields, waves, steps, z_fwd)
    mixed = call(
        first_mix,
        out_shape=shape((OWNERS, 8, 128), F32),
        in_specs=[VMEM] * 4, out_specs=VMEM, name="first_mix",
    )(exchange(spectrum), lift_wide, bias_column, spectral_in)
    prepared = call(
        prepare,
        out_shape=(
            shape((2, 128, 512), BF16), shape((2, 512, 256), BF16), shape((2, 512, 512), BF16),
            shape((96, 512), BF16), shape((1, 512), F32), shape((2, 256, 256), BF16),
            shape((1, 256), F32), shape((2, 512, 128), BF16), shape((CIN, 16, 16, NZ), F32),
        ),
        in_specs=[HBM] + [VMEM] * 11, out_specs=(VMEM,) * 9, name="prepare",
        cost_estimate=pl.CostEstimate(
            flops=1 << 31, transcendentals=0, bytes_accessed=6 << 20
        ),
    )(
        mixed, waves, steps, fields, lift, lift_bias[None], bypass_in, bias_in[None], bypass_out,
        bias_out[None], project, project_bias[:, None],
    )
    coarse_t, spread_t, fine_t, pool_mix, pool_bias, wide_mix, wide_bias, project_mix, base = (
        prepared
    )
    mine = exchange(mixed)
    kept, sent, skip = call(
        coarse_level,
        out_shape=(
            shape((2, 128, 128), F32), shape((2, 128, 128), F32), shape((8, NZ, 512), F32),
        ),
        in_specs=[VMEM] * 10, out_specs=(VMEM, VMEM, HBM), name="coarse_level",
        scratch_shapes=[pltpu.VMEM((4, 128, 128), F32)] * 4
        + [pltpu.VMEM((8, NZ, 512), F32), dma((8,))],
    )(
        mine.reshape(OWNERS * 8, 128), between_cores(mine).reshape(OWNERS * 8, 128), coarse_t,
        fields, z_back, z_fwd, pool_mix, pool_bias, wide_mix, wide_bias,
    )
    spectrum = call(
        spread,
        out_shape=shape((OWNERS * 8, 128), F32),
        in_specs=[VMEM] * 3, out_specs=VMEM, name="spread",
    )(kept, between_cores(sent), spread_t)
    mixed = call(
        second_mix,
        out_shape=shape((OWNERS, 8, 128), F32),
        in_specs=[VMEM] * 2, out_specs=VMEM, name="second_mix",
    )(exchange(spectrum.reshape(OWNERS, 8, 128)), spectral_out)
    return call(
        fine_level,
        out_shape=shape((CIN, 16, 16, NZ), F32),
        in_specs=[VMEM, VMEM, HBM, HBM, VMEM, VMEM], out_specs=VMEM, name="fine_level",
        scratch_shapes=[
            pltpu.VMEM((2, 512, 128), F32), pltpu.VMEM((4, 256, 128), F32),
            pltpu.VMEM((8, NZ, 512), F32), pltpu.VMEM((48, NZ), BF16), dma((9,)),
        ],
    )(exchange(mixed).reshape(OWNERS * 8, 128), fine_t, z_back, skip, project_mix, base)


def solution(mesh):
    owned = P(AXES, None, None, None, None)
    grid = P(None, "gx", "gy", None)
    in_specs = (grid, P(), P(), owned, P(), P(), owned, P(), P(), P(), P())
    return jax.shard_map(
        on_device, mesh=mesh, in_specs=in_specs, out_specs=grid, check_vma=False
    )
```

time: 122 us -> 111 us (0.910)
  blocking collectives: 0 us -> 36 us
  waiting for transfers between devices: 52 us -> 21.8 us
  starting transfers between devices: 25.3 us -> 16.9 us
  local copies, waits for them, and re-layouts: 14.7 us -> 10.6 us
  matrix products: 3.1 us -> 0 us
    all_to_all x0 -> x2, blocking collectives: none -> 36 us  [exchange(): return lax.all_to_all(tiles, AXES, split_axis=0, concat_axis=0, tiled=True)]
    all_to_all x4 -> x2, waiting for transfers between devices: 52 us -> 20.5 us  [exchange(): return lax.all_to_all(tiles, AXES, split_axis=0, concat_axis=0, tiled=True)]
    all_to_all x4 -> x2, starting transfers between devices: 25.3 us -> 16.2 us  [exchange(): return lax.all_to_all(tiles, AXES, split_axis=0, concat_axis=0, tiled=True)]
    mul x5 -> x0, local copies, waits for them, and re-layouts: 3.23 us -> none  [the longest x2 2.92 us: on_device(): project.T[None, :, :, None] * eye16[:, None, None, :]]
    dot_general x4 -> x0, matrix products: 3.1 us -> none  [product(): return jnp.einsum(formula, left, right, precision=lax.Precision.HIGHEST)]
    ppermute x0 -> x2, waiting for transfers between devices: none -> 1.34 us  [between_cores(): lax.ppermute(array, 'gx', [(i, i ^ 1) for i in range(lax.axis_size('gx'))])]
    unnamed x57 -> x51, local copies, waits for them, and re-layouts: 10.4 us -> 9.66 us
    pallas_call x5 -> x7, Pallas kernels: 24 us -> 24.6 us  [the longest x1 7.82 us: on_device(): call(fine_level, out_shape=shape((CIN, 16, 16, NZ), F32), in_specs=[VMEM,...]
  transfers between devices with their start and end apart: 4 -> 4, of which waited for: 4 -> 3; matrix products, arithmetic and copies ran while one was open for 8% -> 3% of each run, Pallas kernels for 0% -> 4%
where the time goes in v2:
time: 111 us
  blocking collectives  36 us (32%)
  Pallas kernels  24.6 us (22%)
  waiting for transfers between devices  21.8 us (20%)
  starting transfers between devices  16.9 us (15%)
  local copies, waits for them, and re-layouts  10.6 us (10%)
    all_to_all x2, blocking collectives, exchange(): return lax.all_to_all(tiles, AXES, split_axis=0, concat_axis=0, tiled=True)  36 us
    all_to_all x2, waiting for transfers between devices, exchange(): return lax.all_to_all(tiles, AXES, split_axis=0, concat_axis=0, tiled=True)  20.5 us
    all_to_all x2, starting transfers between devices, exchange(): return lax.all_to_all(tiles, AXES, split_axis=0, concat_axis=0, tiled=True)  16.2 us
    unnamed x51, local copies, waits for them, and re-layouts  9.66 us
    pallas_call x1, Pallas kernels, on_device(): call(fine_level, out_shape=shape((CIN, 16, 16, NZ), F32), in_specs=[VMEM,...  7.82 us
    pallas_call x1, Pallas kernels, on_device(): call(coarse_level, out_shape=(shape((2, 128, 128), F32), shape((2, 128, 1...  5.96 us
    pallas_call x1, Pallas kernels, on_device(): call(prepare, out_shape=(shape((2, 128, 512), BF16), shape((2, 512, 256),...  4.16 us
    pallas_call x1, Pallas kernels, on_device(): call(first_spectrum, out_shape=shape((OWNERS, 128), F32), in_specs=[HBM]...  2.95 us
  transfers between devices with their start and end apart: 4, of which 3 were waited for; matrix products, arithmetic and copies ran while one was open for 3% of the time, Pallas kernels for 4%

profile of v2, /device:TPU:1, one launch (start us, length us, event | category | flops | bytes accessed | tf_op | source)
XLA Modules:
  0.0 110.9 jit_solution(11569480995221974459)
XLA Ops:
  0.0 1.1 copy-done
  1.1 0.9 copy-done.9
  2.0 0.7 copy-done.11
  3.4 3.0 %first_spectrum.1 = f32[128,128]{1,0:T(8,128)} custom-call(f32[4,16,16,128]{3,2,1,0:T(8,128)S(1)} %copy-done, f32[4,16,512]{2,1,0:T(8,128)S(1)} %copy-done.9, s32[2,512]{1,0:T(2,128)S(1)} %copy-done.14, bf16[32,256]{1,0:T(8,128)(2,1)S(1)} %copy-done.11), custom_call_target="tpu_custom_call" | custom-call | tf_op jit(solution)/shard_map/first_spectrum/pallas_call | solution.py:454
  6.4 11.5 %all-to-all-start = ((f32[128,1,128]{2,1,0:T(1,128)}), f32[128,1,128]{2,1,0:T(1,128)S(1)}, u32[]{:S(2)}, u32[]{:S(2)}) async-start(f32[128,1,128]{2,1,0:T(1,128)} %bitcast.1), calls=%async_computation | async-start | bytes 131072 | tf_op jit(solution)/shard_map/all_to_all | solution.py:433
  17.9 0.7 broadcast_bitcast_fusion
  18.6 0.7 multiply_multiply_fusion.bias_column
  19.5 8.1 %all-to-all-done = f32[128,1,128]{2,1,0:T(1,128)S(1)} async-done(((f32[128,1,128]{2,1,0:T(1,128)}), f32[128,1,128]{2,1,0:T(1,128)S(1)}, u32[]{:S(2)}, u32[]{:S(2)}) %all-to-all-start) | async-done | bytes 65568 | tf_op jit(solution)/shard_map/all_to_all | solution.py:433
  27.6 1.0 copy-done.6
  29.3 18.2 %all_to_all.26 = f32[128,8,128]{2,1,0:T(8,128)S(1)} all-to-all(f32[128,8,128]{2,1,0:T(8,128)S(1)} %first_mix.1.after), channel_id=1, replica_groups=mesh['gx'=8,'gy'=16] {'gx','gy'}, dimensions={0} | all-to-all | bytes 1048576 | tf_op jit(solution)/shard_map/all_to_all | solution.py:433
  48.4 4.2 %prepare.1 = (bf16[2,128,512]{2,1,0:T(8,128)(2,1)S(1)}, bf16[2,512,256]{2,1,0:T(8,128)(2,1)S(1)}, bf16[2,512,512]{2,1,0:T(8,128)(2,1)S(1)}, bf16[96,512]{1,0:T(8...) custom-call(f32[128,8,128]{2,1,0:T(8,128)S(1)} %first_mix.1.after, ...), custom_call_target="tpu_custom_call" | custom-call | flops 2147483648 | bytes 6291456 | tf_op jit(solution)/shard_map/prepare/pallas_call | solution.py:469
  52.6 1.0 copy-done.2
  53.5 0.8 copy-done.7
  54.3 0.8 copy-done.4
  55.1 1.0 copy-done.5
  56.2 6.0 %coarse_level.1 = (f32[2,128,128]{2,1,0:T(8,128)S(1)}, f32[2,128,128]{2,1,0:T(8,128)S(1)}, f32[8,128,512]{2,1,0:T(8,128)S(1)}) custom-call(f32[1024,128]{1,0:T(8,128)S(1)} %bitcast.14, f32[1024,128]{1,0:T(8,128)S(1)} %bitcast.16, bf16[2,128,512]{2,1,0:T(8,128)(2,1)S(1)} %get-tuple-element.17.table, f32[4,16,16,128]{3,2,1,0:T(8,128)S(1)} %copy-done.1, ...), custom_call_target="tpu_custom_call" | custom-call | tf_op jit(solution)/shard_map/coarse_level/pallas_call | solution.py:488
  62.2 1.3 %collective-permute-done.1.got = f32[2,128,128]{2,1,0:T(8,128)S(1)} collective-permute-done((f32[2,128,128]{2,1,0:T(8,128)S(1)}, f32[2,128,128]{2,1,0:T(8,128)S(1)}, u32[]{:S(2)}, u32[]{:S(2)}) %collective-permute-start.1) | collective-permute-done | bytes 131104 | tf_op jit(solution)/shard_map/ppermute | solution.py:437
  63.6 1.2 %spread.1 = f32[1024,128]{1,0:T(8,128)} custom-call(f32[2,128,128]{2,1,0:T(8,128)S(1)} %get-tuple-element.22.kept, f32[2,128,128]{2,1,0:T(8,128)S(1)} %collective-permute-done.1.got, bf16[2,512,256]{2,1,0:T(8,128)(2,1)S(1)} %get-tuple-element.24.table), custom_call_target="tpu_custom_call" | custom-call | tf_op jit(solution)/shard_map/spread/pallas_call | solution.py:500
  64.8 4.7 %all-to-all-start.2 = ((f32[128,8,128]{2,1,0:T(8,128)}), f32[128,8,128]{2,1,0:T(8,128)}, u32[]{:S(2)}, u32[]{:S(2)}) async-start(f32[128,8,128]{2,1,0:T(8,128)} %bitcast.10), calls=%async_computation.2 | async-start | bytes 1048576 | tf_op jit(solution)/shard_map/all_to_all | solution.py:433
  69.5 1.4 %copy.31.weights = f32[2,2,8,64,32]{4,3,2,1,0:T(8,128)S(1)} copy(f32[2,2,8,64,32]{3,4,2,1,0:T(8,128)} %param.21) | data formatting | bytes 524288 | tf_op args[6]
  70.9 12.4 %all-to-all-done.2.arrived = f32[128,8,128]{2,1,0:T(8,128)} async-done(((f32[128,8,128]{2,1,0:T(8,128)}), f32[128,8,128]{2,1,0:T(8,128)}, u32[]{:S(2)}, u32[]{:S(2)}) %all-to-all-start.2) | async-done | bytes 524320 | tf_op jit(solution)/shard_map/all_to_all | solution.py:433
  83.3 1.9 %second_mix.1 = f32[128,8,128]{2,1,0:T(8,128)S(1)} custom-call(f32[128,8,128]{2,1,0:T(8,128)} %all-to-all-done.2.arrived, f32[2,2,8,64,32]{4,3,2,1,0:T(8,128)S(1)} %copy.31.weights), custom_call_target="tpu_custom_call" | custom-call | tf_op jit(solution)/shard_map/second_mix/pallas_call | solution.py:505
  85.2 17.9 %all_to_all.27 = f32[128,8,128]{2,1,0:T(8,128)S(1)} all-to-all(f32[128,8,128]{2,1,0:T(8,128)S(1)} %second_mix.1), channel_id=1, replica_groups=mesh['gx'=8,'gy'=16] {'gx','gy'}, dimensions={0} | all-to-all | bytes 1048576 | tf_op jit(solution)/shard_map/all_to_all | solution.py:433
  103.0 7.8 %fine_level.1 = f32[4,16,16,128]{3,2,1,0:T(8,128)} custom-call(f32[1024,128]{1,0:T(8,128)S(1)} %bitcast.15, bf16[2,512,512]{2,1,0:T(8,128)(2,1)S(1)} %copy-done.3, bf16[48,128]{1,0:T(8,128)(2,1)S(1)} %copy-done.13, f32[8,128,512]{2,1,0:T(8,128)S(1)} %get-tuple-element.26.skip, bf16[2,512,128]{2,1,0:T(8,128)(2,1)S(1)} %get-tuple-element.27.project_mix, ...), custom_call_target="tpu_custom_call" | custom-call | tf_op jit(solution)/shard_map/fine_level/pallas_call | solution.py:510
  (51 shorter events, 2.5 us)
Async XLA Ops:
  0.0 48.3 %copy-start.15 = (s32[2,512]{1,0:T(2,128)S(1)}, s32[2,512]{1,0:T(2,128)}, u32[]{:S(2)}) copy-start(s32[2,512]{1,0:T(2,128)} %constant.25.clone.steps_h.steps) | copy-start | bytes 12292
  0.0 1.1 copy-start
  1.1 0.9 copy-start.9
  3.4 44.7 %copy-start.22 = (f32[32,4]{0,1:T(4,128)S(1)}, f32[32,4]{0,1:T(4,128)}, u32[]{:S(2)}) copy-start(f32[32,4]{0,1:T(4,128)} %param.16) | copy-start | bytes 1540
  3.4 44.7 %copy-start.21 = (f32[64,32]{0,1:T(8,128)S(1)}, f32[64,32]{0,1:T(8,128)}, u32[]{:S(2)}) copy-start(f32[64,32]{0,1:T(8,128)} %param.19) | copy-start | bytes 24580
  3.4 44.8 %copy-start.23 = (f32[4]{0:T(128)S(1)}, f32[4]{0:T(128)}, u32[]{:S(2)}) copy-start(f32[4]{0:T(128)} %param.25) | copy-start | bytes 52
  3.4 44.9 %copy-start.1 = (f32[4,16,16,128]{3,2,1,0:T(8,128)S(1)}, f32[4,16,16,128]{3,2,1,0:T(8,128)}, u32[]{:S(2)}) copy-start(f32[4,16,16,128]{3,2,1,0:T(8,128)} %fields.5) | copy-start | bytes 1572868
  3.4 44.9 %copy-start.10 = (f32[4,16,512]{2,1,0:T(8,128)S(1)}, f32[4,16,512]{2,1,0:T(8,128)}, u32[]{:S(2)}) copy-start(f32[4,16,512]{2,1,0:T(8,128)} %constant.24.clone.waves_h.waves) | copy-start | bytes 393220
  3.4 44.9 %copy-start.16 = (f32[32]{0:T(128)S(1)}, f32[32]{0:T(128)}, u32[]{:S(2)}) copy-start(f32[32]{0:T(128)} %param.17) | copy-start | bytes 388
  3.4 44.9 %copy-start.17 = (f32[32,64]{1,0:T(8,128)S(1)}, f32[32,64]{1,0:T(8,128)}, u32[]{:S(2)}) copy-start(f32[32,64]{1,0:T(8,128)} %bypass_out.1) | copy-start | bytes 24580
  3.4 44.9 %copy-start.18 = (f32[4,32]{1,0:T(4,128)S(1)}, f32[4,32]{1,0:T(4,128)}, u32[]{:S(2)}) copy-start(f32[4,32]{1,0:T(4,128)} %project.1) | copy-start | bytes 1540
  3.4 44.9 %copy-start.19 = (f32[64]{0:T(128)S(1)}, f32[64]{0:T(128)}, u32[]{:S(2)}) copy-start(f32[64]{0:T(128)} %param.20) | copy-start | bytes 772
  3.4 44.9 %copy-start.20 = (f32[32]{0:T(128)S(1)}, f32[32]{0:T(128)}, u32[]{:S(2)}) copy-start(f32[32]{0:T(128)} %param.23) | copy-start | bytes 388
  6.4 21.2 %all-to-all-start = ((f32[128,1,128]{2,1,0:T(1,128)}), f32[128,1,128]{2,1,0:T(1,128)S(1)}, u32[]{:S(2)}, u32[]{:S(2)}) async-start(f32[128,1,128]{2,1,0:T(1,128)} %bitcast.1), calls=%async_computation | async-start | bytes 131072 | tf_op jit(solution)/shard_map/all_to_all | solution.py:433
  27.6 1.0 copy-start.6
  47.4 6.9 %collective-permute-start = (f32[128,8,128]{2,1,0:T(8,128)S(1)}, f32[128,8,128]{2,1,0:T(8,128)S(1)}, u32[]{:S(2)}, u32[]{:S(2)}) collective-permute-start(f32[128,8,128]{2,1,0:T(8,128)S(1)} %all_to_all.26), channel_id=1, source_target_pairs={{0,16},{16,0},{32,48},{48,32},{64,80},{80,64},{96,112},{112,96},{1... | collective-permute-start | bytes 1572872 | tf_op jit(solution)/shard_map/ppermute | solution.py:437
  48.3 6.8 %copy-start.12 = (bf16[32,256]{1,0:T(8,128)(2,1)S(1)}, bf16[32,256]{1,0:T(8,128)(2,1)}, u32[]{:S(2)}) copy-start(bf16[32,256]{1,0:T(8,128)(2,1)} %constant.26.clone.z_fwd_h.z_fwd) | copy-start | bytes 49156
  48.4 6.8 %copy-start.13 = (bf16[48,128]{1,0:T(8,128)(2,1)S(1)}, bf16[48,128]{1,0:T(8,128)(2,1)}, u32[]{:S(2)}) copy-start(bf16[48,128]{1,0:T(8,128)(2,1)} %constant.27.clone.z_back.z_back_h) | copy-start | bytes 36868
  52.5 1.0 copy-start.2
  55.1 1.0 copy-start.5
  62.2 1.4 %collective-permute-start.1 = (f32[2,128,128]{2,1,0:T(8,128)S(1)}, f32[2,128,128]{2,1,0:T(8,128)S(1)}, u32[]{:S(2)}, u32[]{:S(2)}) collective-permute-start(f32[2,128,128]{2,1,0:T(8,128)S(1)} %get-tuple-element.23), channel_id=1, source_target_pairs={{0,16},{16,0},{32,48},{48,32},{64,80},{80,64},{96,112},{112,96},{1... | collective-permute-start | bytes 393224 | tf_op jit(solution)/shard_map/ppermute | solution.py:437
  64.8 18.5 %all-to-all-start.2 = ((f32[128,8,128]{2,1,0:T(8,128)}), f32[128,8,128]{2,1,0:T(8,128)}, u32[]{:S(2)}, u32[]{:S(2)}) async-start(f32[128,8,128]{2,1,0:T(8,128)} %bitcast.10), calls=%async_computation.2 | async-start | bytes 1048576 | tf_op jit(solution)/shard_map/all_to_all | solution.py:433
  83.3 19.8 %copy-start.3 = (bf16[2,512,512]{2,1,0:T(8,128)(2,1)S(1)}, bf16[2,512,512]{2,1,0:T(8,128)(2,1)}, u32[]{:S(2)}) copy-start(bf16[2,512,512]{2,1,0:T(8,128)(2,1)} %copy-done.2) | copy-start | bytes 3145732
  83.3 19.8 %copy-start.8 = (f32[4,16,16,128]{3,2,1,0:T(8,128)S(1)}, f32[4,16,16,128]{3,2,1,0:T(8,128)}, u32[]{:S(2)}) copy-start(f32[4,16,16,128]{3,2,1,0:T(8,128)} %copy-done.7) | copy-start | bytes 1572868
  (4 other events, 3.0 us)

commit v3 on v2

--- a/solution.py
+++ b/solution.py
@@ -21,7 +21,8 @@
 UNROLL = 2
 VMEM = pl.BlockSpec(memory_space=pltpu.VMEM)
 HBM = pl.BlockSpec(memory_space=pltpu.HBM)
-PARAMS = pltpu.CompilerParams(vmem_limit_bytes=40 << 20)
+PARAMS = pltpu.CompilerParams(vmem_limit_bytes=16 << 20)
+ALONE = pltpu.CompilerParams(vmem_limit_bytes=60 << 20)
 
 
 def mode_frequencies():
@@ -67,10 +68,33 @@
     return high, low
 
 
+def first_z_table():
+    c, s = np.cos(z_angles()), np.sin(z_angles())
+    parts = np.array([[c, -s], [-s, -c]])
+    table = np.zeros((CIN, NZ, 2, 2, KZ, CIN))
+    for ch in range(CIN):
+        table[ch, :, :, :, :, ch] = parts.transpose(2, 0, 1, 3)
+    high, low = split_np(table.reshape(CIN, NZ, 128).astype(np.float32))
+    return np.concatenate([high, high, low], axis=1)
+
+
+def first_places_table():
+    fx, fy = mode_frequencies()
+    places = np.arange(16)
+    turns = (
+        fx[:, :, None, None] * places[:, None] / NX + fy[:, :, None, None] * places[None, :] / NY
+    )
+    angles = 2.0 * np.pi * turns
+    table = np.stack([np.cos(angles), np.sin(angles)], axis=1) / math.sqrt(TOTAL)
+    return np.stack(split_np(table.reshape(512, 256).astype(np.float32)))
+
+
 def inverse_z_table():
     table = np.stack([np.cos(z_angles()), -np.sin(z_angles())], axis=2)
     high, low = split_np(table.reshape(NZ, 16).astype(np.float32))
-    return np.concatenate([high.T, high.T, low.T], axis=0)
+    ones = np.zeros((16, NZ), BF16)
+    ones[:3] = 1.0
+    return np.concatenate([high.T, high.T, low.T, ones], axis=0)
 
 
 def forward_z_table():
@@ -82,6 +106,15 @@
 def split(x):
     high = x.astype(BF16)
     return high, (x - high.astype(F32)).astype(BF16)
+
+
+def bias_rows(bias):
+    high, less = split(bias)
+    least = (bias - high.astype(F32) - less.astype(F32)).astype(BF16)
+    row = iota((16, bias.shape[1]), 0)
+    rows = [v.astype(F32) for v in (high, less, least)]
+    total = jnp.where(row == 0, rows[0], jnp.where(row == 1, rows[1], rows[2]))
+    return jnp.where(row < 3, total, 0.0).astype(BF16)
 
 
 def mm(a, b, dims=((1,), (0,))):
@@ -129,10 +162,14 @@
     return lax.axis_index("gx"), lax.axis_index("gy")
 
 
-def device_waves(waves, steps, place):
+def phases(steps, place):
     turns = (steps[0:1] * place[0] + steps[1:2] * place[1]) & 15
     angle = turns.astype(F32) * (2.0 * math.pi / 16)
-    cos, sin = jnp.cos(angle), jnp.sin(angle)
+    return jnp.cos(angle), jnp.sin(angle)
+
+
+def device_waves(waves, steps, place):
+    cos, sin = phases(steps, place)
     return waves[0] * cos - waves[1] * sin, waves[1] * cos + waves[0] * sin
 
 
@@ -143,39 +180,57 @@
     return jnp.concatenate(real, axis=0), jnp.concatenate(imag, axis=0)
 
 
-def first_spectrum(fields, waves_h, steps_h, z_fwd_h, out, fields_v, waves, steps, z_fwd, sems):
-    pairs = [(waves_h, waves), (steps_h, steps), (z_fwd_h, z_fwd)]
-    pairs += [(fields.at[ch], fields_v.at[ch]) for ch in range(CIN)]
+def first_spectrum(
+    fields, ztab_h, ptab_h, steps_h, out, fields_v, ztab, ptab, steps, sems,
+):
+    pairs = [(steps_h, steps)]
+    for ch in range(CIN):
+        pairs += [(fields.at[ch], fields_v.at[ch]), (ztab_h.at[ch], ztab.at[ch])]
+    pairs.append((ptab_h, ptab))
     copies = [
         pltpu.make_async_copy(source, target, sems.at[i])
         for i, (source, target) in enumerate(pairs)
     ]
     for copy in copies:
         copy.start()
-    for copy in copies[:3]:
-        copy.wait()
-    along_x = device_waves(waves, steps, my_place())
-    real, imag = wave_rows(along_x, waves[2], waves[3], range(16))
-    nt = ((1,), (1,))
-    parts = [[], []]
+    copies[0].wait()
+    cos, sin = phases(steps, my_place())
+    turn = [v[:, at : at + 128] for at in (0, 256) for v in (cos, sin)]
+    turn = jnp.concatenate(turn + [jnp.zeros((124, 128), F32)], axis=0).T
+    total = None
     for ch in range(CIN):
-        copies[3 + ch].wait()
+        copies[1 + 2 * ch].wait()
+        copies[2 + 2 * ch].wait()
         fh, fl = split(fields_v[ch].reshape(256, NZ))
-        made = mm(z_fwd[...], jnp.concatenate([fh, fl], axis=1), nt)
-        made = made[:16] + made[16:]
-        parts[0].append(made[:8])
-        parts[1].append(made[8:])
-    total = mm3(jnp.concatenate(parts[0], axis=0), real)
-    total += mm3(jnp.concatenate(parts[1], axis=0), imag)
-    total *= 1.0 / math.sqrt(TOTAL)
-    tiles = [total[:, 128 * t : 128 * t + 128] for t in range(4)]
-    out[...] = jnp.concatenate(tiles, axis=0).T
-
-
-def prepare(
-    after, waves, steps, fields, lift, lift_bias, bypass_in, bias_in, bypass_out, bias_out,
-    project, project_bias, coarse_t, spread_t, fine_t, pool_mix, pool_bias, wide_mix, wide_bias,
-    project_mix, base,
+        term = mm(jnp.concatenate([fh, fl], axis=1), ztab[ch, :256]) + mm(fh, ztab[ch, 256:])
+        total = term if total is None else total + term
+    copies[-1].wait()
+    th, tl = split(total)
+    both = mm(ptab[0], th) + mm(ptab[0], tl) + mm(ptab[1], th)
+    low = iota((128, 128), 1) < 64
+    rows = []
+    for s in range(2):
+        part_cos = both[256 * s : 256 * s + 128]
+        part_sin = both[256 * s + 128 : 256 * s + 256]
+        part_sin = pltpu.roll(part_sin, 64, 1)
+        pair = jnp.where(low, part_cos + part_sin, part_cos - part_sin)
+        cos_s, sin_s = turn[:, 2 * s : 2 * s + 1], turn[:, 2 * s + 1 : 2 * s + 2]
+        rows.append(cos_s * pair + sin_s * pltpu.roll(pair, 64, 1))
+    out[...] = jnp.where(low, rows[0], pltpu.roll(rows[1], 64, 1))
+
+
+def prepare_mix(after, weights, lift, lift_bias, weights_v, lift_wide, bias_column, sem):
+    copy = pltpu.make_async_copy(weights, weights_v, sem)
+    copy.start()
+    lift_wide[...] = exact(lift[...], ones_where(iota((CIN, 128), 0) == iota((CIN, 128), 1) % 4))
+    gx, gy = my_place()
+    at_zero = (iota((C1, 32), 1) + gx + gy) == 0
+    bias_column[...] = jnp.where(at_zero, lift_bias[...] * math.sqrt(TOTAL), 0.0)
+    copy.wait()
+
+
+def prepare_coarse(
+    after, waves, steps, lift, lift_bias, bypass_in, bias_in, bypass_out, spread_t, pack,
 ):
     nt = ((1,), (1,))
     gx, gy = my_place()
@@ -187,22 +242,13 @@
         jnp.concatenate(wave_rows(along, cos_y, sin_y, range(0, 16, 2)), axis=0)
         for along in (own, mate)
     ]
-    coarse_t[0], coarse_t[1] = split(tables[0] * BACK)
+    pack[0:128], pack[128:256] = split(tables[0] * BACK)
     scale = 1.0 / math.sqrt(TOTAL / 4.0)
     for patch in range(2):
         at = slice(128 * patch, 128 * patch + 128)
         high, less = split(tables[patch].T * scale)
         spread_t[0, :, at] = high
         spread_t[1, :, at] = less
-    scaled = (own[0] * BACK, own[1] * BACK)
-    for x in range(0, 16, 8):
-        pair = wave_rows(scaled, waves[2], waves[3], range(x, x + 8))
-        for part in range(2):
-            at = slice(256 * part + 16 * x, 256 * part + 16 * x + 128)
-            high, less = split(pair[part])
-            fine_t[0, at] = high
-            fine_t[1, at] = less
-
     lanes = [
         ones_where(iota((C2, 128), 0) == 32 * h + iota((C2, 128), 1) % 32) for h in range(2)
     ]
@@ -213,17 +259,33 @@
         at = slice(128 * t, 128 * t + 128)
         same = iota((32, 128), 0) % 8 == 4 * (t // 2) + iota((32, 128), 1) // 32
         high, less = split(jnp.where(same, exact(through, lanes[t % 2]), 0.0))
-        pool_mix[:, at] = jnp.concatenate([high, less, high], axis=0)
-        pool_bias[:, at] = exact(offset, lanes[t % 2])
+        rows = bias_rows(exact(offset, lanes[t % 2]))
+        pack[256:368, at] = jnp.concatenate([rows, high, less, high], axis=0)
     spread_d = ones_where(iota((C1, 256), 0) == iota((C1, 256), 1) % 32)
     same = iota((128, 256), 0) // 32 == iota((128, 256), 1) // 64
     for h in range(2):
         pick = ones_where(iota((128, C2), 1) == 32 * h + iota((128, C2), 0) % 32)
         wide = exact(exact(pick, bypass_out[...], nt), spread_d)
         high, less = split(jnp.where(same, wide, 0.0))
-        wide_mix[0, 128 * h : 128 * h + 128] = high
-        wide_mix[1, 128 * h : 128 * h + 128] = less
-    wide_bias[...] = exact(bias_out[...], spread_d)
+        pack[368 + 128 * h : 496 + 128 * h] = jnp.concatenate([high, less], axis=1)
+
+
+def prepare_fine(
+    after, waves, steps, fields, lift, lift_bias, bias_out, project, project_bias,
+    fine_t, project_mix, bias_mix, base,
+):
+    nt = ((1,), (1,))
+    own = device_waves(waves, steps, my_place())
+    scaled = (own[0] * BACK, own[1] * BACK)
+    for x in range(0, 16, 8):
+        pair = wave_rows(scaled, waves[2], waves[3], range(x, x + 8))
+        for part in range(2):
+            at = slice(256 * part + 16 * x, 256 * part + 16 * x + 128)
+            high, less = split(pair[part])
+            fine_t[0, at] = high
+            fine_t[1, at] = less
+    lanes = ones_where(iota((C1, 512), 0) == iota((C1, 512), 1) % 32)
+    bias_mix[...] = bias_rows(exact(bias_out[...], lanes))
     pick = ones_where(iota((512, C1), 1) == iota((512, C1), 0) % 32)
     onto = ones_where(iota((CIN, 128), 0) == iota((CIN, 128), 1) % 64 // 16)
     made = exact(exact(pick, project[...], nt), onto)
@@ -273,8 +335,7 @@
 
 def first_mix(arrived, lift_wide, bias_column, weights, out):
     row = jnp.sum(arrived[...], axis=0, keepdims=True)
-    source = lax.broadcasted_iota(jnp.int32, (128, 32), 0)
-    source = source // 32 * 8 + source % 8
+    source = lax.broadcasted_iota(jnp.int32, (128, 32), 0) // CIN
     pick = (source == lax.broadcasted_iota(jnp.int32, (128, 32), 1)).astype(F32)
     lifted = (
         lax.dot_general(
@@ -293,9 +354,19 @@
         out[n] = halves[n // 16 % 2]
 
 
-def second_mix(arrived, weights, out):
+def second_mix(arrived_h, weights, out, arrived, sems):
+    copies = [
+        pltpu.make_async_copy(
+            arrived_h.at[pl.ds(32 * i, 32)], arrived.at[pl.ds(32 * i, 32)], sems.at[i]
+        )
+        for i in range(4)
+    ]
+    for copy in copies:
+        copy.start()
     sums = [None, None]
     for n in range(OWNERS):
+        if n % 32 == 0:
+            copies[n // 32].wait()
         half = n // 16 % 2
         sums[half] = arrived[n] if sums[half] is None else sums[half] + arrived[n]
     stacked = jnp.concatenate(sums + [jnp.zeros((112, 128), F32)], axis=0).T
@@ -311,7 +382,7 @@
 
 
 def coarse_level(
-    mine, other, table, fields, z_back, z_fwd, pool_mix, pool_bias, wide_mix, wide_bias,
+    mine, other, pack, fields, z_back, z_fwd,
     kept, sent, skip, y_s, rhs_s, g_s, t_s, skip_v, sems,
 ):
     core = lax.axis_index("gx") % 2
@@ -322,7 +393,8 @@
         ]
         modes.append(jnp.concatenate(tiles, axis=1))
     mh, ml = split(jnp.concatenate(modes, axis=0))
-    made = mm(table[0], mh) + mm(table[1], mh) + mm(table[0], ml)
+    th, tl = pack[0:128], pack[128:256]
+    made = mm(th, mh) + mm(tl, mh) + mm(th, ml)
     for u in range(2):
         for t in range(2):
             at = 128 * (2 * u + t)
@@ -348,8 +420,8 @@
             pooled.append(total * 0.25)
         ph, pll = split(jnp.concatenate(pooled, axis=0))
         left = jnp.concatenate([z_back[...], ph, ph, pll], axis=0)
-        right = jnp.concatenate([high, less, high, pool_mix[...]], axis=0)
-        value = gelu(mm(left, right, ((0,), (0,))) + pool_bias[...])
+        right = jnp.concatenate([high, less, high, pack[256:368]], axis=0)
+        value = gelu(mm(left, right, ((0,), (0,))))
         vh, vl = split(value)
         made = mm(z_fwd[...], jnp.concatenate([vh, vl], axis=0))
         made = made[:16] + made[16:]
@@ -359,8 +431,8 @@
             g_s[t, pl.ds(pl.multiple_of(p * 8 + 64, 8), 8), :] = made[8:, at]
         for q in range(2):
             at = slice(256 * q, 256 * q + 256)
-            wide = mm(vh[:, at], wide_mix[0]) + mm(vh[:, at], wide_mix[1])
-            skip_v[p, :, at] = wide + mm(vl[:, at], wide_mix[0]) + wide_bias[...]
+            wide = mm(vh[:, at], pack[368:624, 0:256]) + mm(vh[:, at], pack[368:624, 256:512])
+            skip_v[p, :, at] = wide + mm(vl[:, at], pack[368:624, 0:256])
         pltpu.make_async_copy(skip_v.at[p], skip.at[p], sems.at[p]).start()
         return carry
 
@@ -391,10 +463,11 @@
 
 
 def fine_level(
-    arrived, table, z_back_h, skip, project_mix, base, out, y_s, rhs_s, skip_v, z_back, sems,
-):
+    arrived, table, z_back_h, skip, project_mix, bias_mix, base_h, out, base,
+    y_s, rhs_s, skip_v, z_back, sems,):
     copies = [pltpu.make_async_copy(skip.at[p], skip_v.at[p], sems.at[p]) for p in range(8)]
     copies.append(pltpu.make_async_copy(z_back_h, z_back, sems.at[8]))
+    copies.append(pltpu.make_async_copy(base_h, base, sems.at[9]))
     for copy in copies:
         copy.start()
     modes = []
@@ -418,7 +491,8 @@
     def step(x, carry):
         rows = [rhs_s[t, pl.ds(x, 16, stride=16), :] for t in range(4)]
         high, less = split(jnp.concatenate(rows, axis=1))
-        before = mm(z_back[...], jnp.concatenate([high, less, high], axis=0), ((0,), (0,)))
+        right = jnp.concatenate([high, less, high, bias_mix[...]], axis=0)
+        before = mm(z_back[...], right, ((0,), (0,)))
         vh, vl = split(gelu(before + skip_v[x // 2]))
         made = (mm(vh, project_mix[0]) + mm(vl, project_mix[1])).T
         made = made[:64] + made[64:]
@@ -437,85 +511,106 @@
     return lax.ppermute(array, "gx", [(i, i ^ 1) for i in range(lax.axis_size("gx"))])
 
 
+def stay(array):
+    return pltpu.with_memory_space_constraint(array, pltpu.HBM)
+
+
 def on_device(
     fields, lift, lift_bias, spectral_in, bypass_in, bias_in, spectral_out, bypass_out, bias_out,
     project, project_bias,
 ):
-    gx, gy = lax.axis_index("gx"), lax.axis_index("gy")
     waves, steps = wave_tables(), phase_steps()
     z_back, z_fwd = inverse_z_table(), forward_z_table()
-    at_zero = ((gx == 0) & (gy == 0)).astype(F32) * math.sqrt(TOTAL)
-    bias_column = lift_bias[:, None] * (jnp.arange(32) == 0).astype(F32)[None, :] * at_zero
-    lift_wide = jnp.tile(jnp.repeat(lift, KZ, axis=1), (1, 4))
-
     call = functools.partial(pl.pallas_call, compiler_params=PARAMS)
     shape = jax.ShapeDtypeStruct
     dma = pltpu.SemaphoreType.DMA
-    spectrum = call(
+    work = pl.CostEstimate(flops=1 << 31, transcendentals=0, bytes_accessed=6 << 20)
+    spectrum = pl.pallas_call(
         first_spectrum,
         out_shape=shape((OWNERS, 128), F32),
         in_specs=[HBM] * 4, out_specs=VMEM,
         scratch_shapes=[
-            pltpu.VMEM((CIN, 16, 16, NZ), F32), pltpu.VMEM((4, 16, 512), F32),
-            pltpu.VMEM((2, 512), jnp.int32), pltpu.VMEM((32, 2 * NZ), BF16), dma((7,)),
+            pltpu.VMEM((CIN, 16, 16, NZ), F32), pltpu.VMEM((CIN, 384, 128), BF16),
+            pltpu.VMEM((2, 512, 256), BF16), pltpu.VMEM((2, 512), jnp.int32), dma((10,)),
         ],
-        name="first_spectrum",
-    )(fields, waves, steps, z_fwd)
+        name="first_spectrum", compiler_params=ALONE,
+    )(fields, first_z_table(), first_places_table(), steps)
+    prepared = call(
+        prepare_mix,
+        out_shape=(
+            shape((2, 2, KZ, C1, C2), F32), shape((C1, 128), F32), shape((C1, 32), F32),
+        ),
+        in_specs=[HBM] * 2 + [VMEM] * 2, out_specs=(VMEM,) * 3, name="prepare_mix",
+        scratch_shapes=[dma(())], cost_estimate=work,
+    )(spectrum, spectral_in, lift, lift_bias[:, None])
+    arrived, prepared = lax.optimization_barrier((exchange(spectrum), prepared))
+    weights, lift_wide, bias_column = prepared
     mixed = call(
         first_mix,
         out_shape=shape((OWNERS, 8, 128), F32),
         in_specs=[VMEM] * 4, out_specs=VMEM, name="first_mix",
-    )(exchange(spectrum), lift_wide, bias_column, spectral_in)
+    )(arrived, lift_wide, bias_column, weights)
     prepared = call(
-        prepare,
-        out_shape=(
-            shape((2, 128, 512), BF16), shape((2, 512, 256), BF16), shape((2, 512, 512), BF16),
-            shape((96, 512), BF16), shape((1, 512), F32), shape((2, 256, 256), BF16),
-            shape((1, 256), F32), shape((2, 512, 128), BF16), shape((CIN, 16, 16, NZ), F32),
-        ),
-        in_specs=[HBM] + [VMEM] * 11, out_specs=(VMEM,) * 9, name="prepare",
-        cost_estimate=pl.CostEstimate(
-            flops=1 << 31, transcendentals=0, bytes_accessed=6 << 20
-        ),
-    )(
-        mixed, waves, steps, fields, lift, lift_bias[None], bypass_in, bias_in[None], bypass_out,
-        bias_out[None], project, project_bias[:, None],
-    )
-    coarse_t, spread_t, fine_t, pool_mix, pool_bias, wide_mix, wide_bias, project_mix, base = (
-        prepared
-    )
-    mine = exchange(mixed)
+        prepare_coarse,
+        out_shape=(shape((2, 512, 256), BF16), shape((624, 512), BF16)),
+        in_specs=[HBM] + [VMEM] * 7, out_specs=(VMEM,) * 2, name="prepare_coarse",
+        cost_estimate=work,
+    )(mixed, waves, steps, lift, lift_bias[None], bypass_in, bias_in[None], bypass_out)
+    mine, prepared = lax.optimization_barrier((exchange(mixed), prepared))
+    spread_t, pack = prepared
     kept, sent, skip = call(
         coarse_level,
         out_shape=(
-            shape((2, 128, 128), F32), shape((2, 128, 128), F32), shape((8, NZ, 512), F32),
+            shape((2, 128, 128), F32), shape((2, 128, 128), F32),
+            pltpu.HBM((8, NZ, 512), F32),
         ),
-        in_specs=[VMEM] * 10, out_specs=(VMEM, VMEM, HBM), name="coarse_level",
+        in_specs=[VMEM] * 6, out_specs=(VMEM, VMEM, HBM), name="coarse_level",
         scratch_shapes=[pltpu.VMEM((4, 128, 128), F32)] * 4
         + [pltpu.VMEM((8, NZ, 512), F32), dma((8,))],
     )(
-        mine.reshape(OWNERS * 8, 128), between_cores(mine).reshape(OWNERS * 8, 128), coarse_t,
-        fields, z_back, z_fwd, pool_mix, pool_bias, wide_mix, wide_bias,
+        mine.reshape(OWNERS * 8, 128), between_cores(mine).reshape(OWNERS * 8, 128), pack,
+        fields, z_back, z_fwd,
     )
     spectrum = call(
         spread,
         out_shape=shape((OWNERS * 8, 128), F32),
         in_specs=[VMEM] * 3, out_specs=VMEM, name="spread",
     )(kept, between_cores(sent), spread_t)
+    prepared = call(
+        prepare_fine,
+        out_shape=(
+            pltpu.HBM((2, 512, 512), BF16), shape((2, 512, 128), BF16), shape((16, 512), BF16),
+            pltpu.HBM((CIN, 16, 16, NZ), F32),
+        ),
+        in_specs=[HBM] + [VMEM] * 8, out_specs=(VMEM,) * 4, name="prepare_fine",
+        cost_estimate=work,
+    )(
+        spectrum, waves, steps, fields, lift, lift_bias[None], bias_out[None], project,
+        project_bias[:, None],
+    )
+    arrived, prepared = lax.optimization_barrier(
+        (exchange(spectrum.reshape(OWNERS, 8, 128)), prepared)
+    )
+    fine_t, project_mix, bias_mix, base = prepared
     mixed = call(
         second_mix,
         out_shape=shape((OWNERS, 8, 128), F32),
-        in_specs=[VMEM] * 2, out_specs=VMEM, name="second_mix",
-    )(exchange(spectrum.reshape(OWNERS, 8, 128)), spectral_out)
+        in_specs=[HBM, VMEM], out_specs=VMEM, name="second_mix",
+        scratch_shapes=[pltpu.VMEM((OWNERS, 8, 128), F32), dma((4,))],
+    )(arrived, spectral_out)
     return call(
         fine_level,
         out_shape=shape((CIN, 16, 16, NZ), F32),
-        in_specs=[VMEM, VMEM, HBM, HBM, VMEM, VMEM], out_specs=VMEM, name="fine_level",
+        in_specs=[VMEM, VMEM, HBM, HBM, VMEM, VMEM, HBM], out_specs=VMEM, name="fine_level",
         scratch_shapes=[
+            pltpu.VMEM((CIN, 16, 16, NZ), F32),
             pltpu.VMEM((2, 512, 128), F32), pltpu.VMEM((4, 256, 128), F32),
-            pltpu.VMEM((8, NZ, 512), F32), pltpu.VMEM((48, NZ), BF16), dma((9,)),
+            pltpu.VMEM((8, NZ, 512), F32), pltpu.VMEM((64, NZ), BF16), dma((10,)),
         ],
-    )(exchange(mixed).reshape(OWNERS * 8, 128), fine_t, z_back, skip, project_mix, base)
+    )(
+        exchange(mixed).reshape(OWNERS * 8, 128), fine_t, stay(jnp.asarray(z_back)), stay(skip),
+        project_mix, bias_mix, stay(base),
+    )
 
 
 def solution(mesh):

time: 111 us -> 101 us (0.910)
  blocking collectives: 36 us -> 17.9 us
  waiting for transfers between devices: 21.8 us -> 30.7 us
  local copies, waits for them, and re-layouts: 10.6 us -> 3.99 us
  starting transfers between devices: 16.9 us -> 20.6 us
  Pallas kernels: 24.6 us -> 27.4 us
    all_to_all x2 -> x1, blocking collectives: 36 us -> 17.9 us  [exchange(): return lax.all_to_all(tiles, AXES, split_axis=0, concat_axis=0, tiled=True)]
    all_to_all x2 -> x3, waiting for transfers between devices: 20.5 us -> 28.2 us  [exchange(): return lax.all_to_all(tiles, AXES, split_axis=0, concat_axis=0, tiled=True)]
    unnamed x51 -> x35, local copies, waits for them, and re-layouts: 9.66 us -> 3.16 us
    all_to_all x2 -> x3, starting transfers between devices: 16.2 us -> 19.6 us  [exchange(): return lax.all_to_all(tiles, AXES, split_axis=0, concat_axis=0, tiled=True)]
    pallas_call x1, Pallas kernels: 7.82 us -> 9.27 us  [on_device(): call(fine_level, out_shape=shape((CIN, 16, 16, NZ), F32), in_specs=[VMEM,...]
    pallas_call x3 -> x5, Pallas kernels: 9.01 us -> 10.3 us  [the longest x1 4.31 us: on_device(): call(prepare_fine, out_shape=(pltpu.HBM((2, 512, 512), BF16), shape((2, 5...]
    ppermute x2, waiting for transfers between devices: 1.34 us -> 2.52 us  [between_cores(): lax.ppermute(array, 'gx', [(i, i ^ 1) for i in range(lax.axis_size('gx'))])]
  transfers between devices with their start and end apart: 4 -> 5, of which waited for: 3 -> 5; matrix products, arithmetic and copies ran while one was open for 3% -> 2% of each run, Pallas kernels for 4% -> 6%
where the time goes in v3:
time: 101 us
  waiting for transfers between devices  30.7 us (30%)
  Pallas kernels  27.4 us (27%)
  starting transfers between devices  20.6 us (20%)
  blocking collectives  17.9 us (18%)
  local copies, waits for them, and re-layouts  3.99 us (4%)
    all_to_all x3, waiting for transfers between devices, exchange(): return lax.all_to_all(tiles, AXES, split_axis=0, concat_axis=0, tiled=True)  28.2 us
    all_to_all x3, starting transfers between devices, exchange(): return lax.all_to_all(tiles, AXES, split_axis=0, concat_axis=0, tiled=True)  19.6 us
    all_to_all x1, blocking collectives, exchange(): return lax.all_to_all(tiles, AXES, split_axis=0, concat_axis=0, tiled=True)  17.9 us
    pallas_call x1, Pallas kernels, on_device(): call(fine_level, out_shape=shape((CIN, 16, 16, NZ), F32), in_specs=[VMEM,...  9.27 us
    pallas_call x1, Pallas kernels, on_device(): call(coarse_level, out_shape=(shape((2, 128, 128), F32), shape((2, 128, 1...  5.32 us
    pallas_call x1, Pallas kernels, on_device(): call(prepare_fine, out_shape=(pltpu.HBM((2, 512, 512), BF16), shape((2, 5...  4.31 us
    unnamed x35, local copies, waits for them, and re-layouts  3.16 us
    pallas_call x1, Pallas kernels, on_device(): pl.pallas_call(first_spectrum, out_shape=shape((OWNERS, 128), F32), in_sp...  3.14 us
  transfers between devices with their start and end apart: 5, of which 5 were waited for; matrix products, arithmetic and copies ran while one was open for 2% of the time, Pallas kernels for 6%

profile of v3, /device:TPU:1, one launch (start us, length us, event | category | flops | bytes accessed | tf_op | source)
XLA Modules:
  0.0 100.8 jit_solution(14943901666676868280)
XLA Ops:
  0.0 3.1 %first_spectrum.1.after = f32[128,128]{1,0:T(8,128)} custom-call(f32[4,16,16,128]{3,2,1,0:T(8,128)} %fields.5, bf16[4,384,128]{2,1,0:T(8,128)(2,1)} %constant.12.clone.ztab_h, bf16[2,512,256]{2,1,0:T(8,128)(2,1)} %constant.13.clone.ptab_h, s32[2,512]{1,0:T(2,128)} %constant.14.clone.steps_h.steps), custom_call_target="tpu_custom_call" | custom-call | tf_op jit(solution)/shard_map/first_spectrum/pallas_call | solution.py:528
  3.1 11.5 %all-to-all-start = ((f32[128,1,128]{2,1,0:T(1,128)}), f32[128,1,128]{2,1,0:T(1,128)S(1)}, u32[]{:S(2)}, u32[]{:S(2)}) async-start(f32[128,1,128]{2,1,0:T(1,128)} %bitcast.17), calls=%async_computation | async-start | bytes 131072 | tf_op jit(solution)/shard_map/all_to_all | solution.py:507
  14.7 0.8 copy.26.lift
  15.4 0.7 copy.27.lift_bias
  16.2 0.8 copy-done.2
  17.0 1.0 %copy-done.7 = f32[2,2,8,32,64]{4,3,2,1,0:T(8,128)S(1)} copy-done((f32[2,2,8,32,64]{4,3,2,1,0:T(8,128)S(1)}, f32[2,2,8,32,64]{4,3,2,1,0:T(8,128)}, u32[]{:S(2)}) %copy-start.7) | copy-done | bytes 262168
  18.3 6.1 %all-to-all-done = f32[128,1,128]{2,1,0:T(1,128)S(1)} async-done(((f32[128,1,128]{2,1,0:T(1,128)}), f32[128,1,128]{2,1,0:T(1,128)S(1)}, u32[]{:S(2)}, u32[]{:S(2)}) %all-to-all-start) | async-done | bytes 65568 | tf_op jit(solution)/shard_map/all_to_all | solution.py:507
  24.4 1.4 %first_mix.1.after = f32[128,8,128]{2,1,0:T(8,128)} custom-call(f32[128,128]{1,0:T(8,128)S(1)} %bitcast.16, f32[32,128]{1,0:T(8,128)S(1)} %get-tuple-element.33.lift_wide, f32[32,32]{1,0:T(8,128)S(1)} %get-tuple-element.34.bias_column, f32[2,2,8,32,64]{4,3,2,1,0:T(8,128)S(1)} %get-tuple-element.35.weights), custom_call_target="tpu_custom_call" | custom-call | tf_op jit(solution)/shard_map/first_mix/pallas_call | solution.py:548
  25.7 4.3 %all-to-all-start.1 = ((f32[128,8,128]{2,1,0:T(8,128)}), f32[128,8,128]{2,1,0:T(8,128)S(1)}, u32[]{:S(2)}, u32[]{:S(2)}) async-start(f32[128,8,128]{2,1,0:T(8,128)} %first_mix.1.after), calls=%async_computation.1 | async-start | bytes 1048576 | tf_op jit(solution)/shard_map/all_to_all | solution.py:507
  30.2 1.2 %prepare_coarse.1 = (bf16[2,512,256]{2,1,0:T(8,128)(2,1)S(1)}, bf16[624,512]{1,0:T(8,128)(2,1)S(1)}) custom-call(f32[128,8,128]{2,1,0:T(8,128)} %first_mix.1.after, f32[4,16,512]{2,1,0:T(8,128)S(1)} %copy-done.12, s32[2,512]{1,0:T(2,128)S(1)} %copy-done.5, f32[32,4]{1,0:T(8,128)S(1)} %copy.26.lift, f32[1,32]{1,0:T(1,128)S(1)} %bitcast.19, ...), custom_call_target="tpu_custom_call" | custom-call | flops 2147483648 | bytes 6291456 | tf_op jit(solution)/shard_map/prepare_coarse/pallas_call | solution.py:553
  31.4 12.7 %all-to-all-done.1 = f32[128,8,128]{2,1,0:T(8,128)S(1)} async-done(((f32[128,8,128]{2,1,0:T(8,128)}), f32[128,8,128]{2,1,0:T(8,128)S(1)}, u32[]{:S(2)}, u32[]{:S(2)}) %all-to-all-start.1) | async-done | bytes 524320 | tf_op jit(solution)/shard_map/all_to_all | solution.py:507
  44.1 0.6 collective-permute-start
  44.7 1.5 %collective-permute-done = f32[128,8,128]{2,1,0:T(8,128)S(1)} collective-permute-done((f32[128,8,128]{2,1,0:T(8,128)S(1)}, f32[128,8,128]{2,1,0:T(8,128)S(1)}, u32[]{:S(2)}, u32[]{:S(2)}) %collective-permute-start) | collective-permute-done | bytes 524320 | tf_op jit(solution)/shard_map/ppermute | solution.py:511
  46.3 5.3 %coarse_level.1 = (f32[2,128,128]{2,1,0:T(8,128)S(1)}, f32[2,128,128]{2,1,0:T(8,128)S(1)}, f32[8,128,512]{2,1,0:T(8,128)}) custom-call(f32[1024,128]{1,0:T(8,128)S(1)} %bitcast.13, f32[1024,128]{1,0:T(8,128)S(1)} %bitcast.15, bf16[624,512]{1,0:T(8,128)(2,1)S(1)} %get-tuple-element.39.pack, f32[4,16,16,128]{3,2,1,0:T(8,128)S(1)} %copy-done, ...), custom_call_target="tpu_custom_call" | custom-call | tf_op jit(solution)/shard_map/coarse_level/pallas_call | solution.py:561
  51.7 0.5 collective-permute-start.1
  52.1 1.0 collective-permute-done.1.got
  53.1 1.2 %spread.1.after = f32[1024,128]{1,0:T(8,128)} custom-call(f32[2,128,128]{2,1,0:T(8,128)S(1)} %get-tuple-element.40.kept, f32[2,128,128]{2,1,0:T(8,128)S(1)} %collective-permute-done.1.got, bf16[2,512,256]{2,1,0:T(8,128)(2,1)S(1)} %get-tuple-element.42.table), custom_call_target="tpu_custom_call" | custom-call | tf_op jit(solution)/shard_map/spread/pallas_call | solution.py:574
  54.3 3.8 %all-to-all-start.2 = ((f32[128,8,128]{2,1,0:T(8,128)}), f32[128,8,128]{2,1,0:T(8,128)S(1)}, u32[]{:S(2)}, u32[]{:S(2)}) async-start(f32[128,8,128]{2,1,0:T(8,128)} %bitcast.8), calls=%async_computation.2 | async-start | bytes 1048576 | tf_op jit(solution)/shard_map/all_to_all | solution.py:507
  58.2 0.4 copy.32.weights
  58.6 4.3 %prepare_fine.1 = (bf16[2,512,512]{2,1,0:T(8,128)(2,1)}, bf16[2,512,128]{2,1,0:T(8,128)(2,1)S(1)}, bf16[16,512]{1,0:T(8,128)(2,1)S(1)}, f32[4,16,16,128]{3,2,1,0:T(8,128)}) custom-call(f32[1024,128]{1,0:T(8,128)} %spread.1.after, f32[4,16,512]{2,1,0:T(8,128)S(1)} %copy-done.12, s32[2,512]{1,0:T(2,128)S(1)} %copy-done.5, f32[4,16,16,128]{3,2,1,0:T(8,128)S(1)} %copy-done, ...), custom_call_target="tpu_custom_call" | custom-call | flops 2147483648 | bytes 6291456 | tf_op jit(solution)/shard_map/prepare_fine/pallas_call | solution.py:579
  62.9 9.4 %all-to-all-done.2.arrived_h = f32[128,8,128]{2,1,0:T(8,128)S(1)} async-done(((f32[128,8,128]{2,1,0:T(8,128)}), f32[128,8,128]{2,1,0:T(8,128)S(1)}, u32[]{:S(2)}, u32[]{:S(2)}) %all-to-all-start.2) | async-done | bytes 524320 | tf_op jit(solution)/shard_map/all_to_all | solution.py:507
  72.3 1.4 %second_mix.1 = f32[128,8,128]{2,1,0:T(8,128)S(1)} custom-call(f32[128,8,128]{2,1,0:T(8,128)S(1)} %all-to-all-done.2.arrived_h, f32[2,2,8,64,32]{4,3,2,1,0:T(8,128)S(1)} %copy.32.weights), custom_call_target="tpu_custom_call" | custom-call | tf_op jit(solution)/shard_map/second_mix/pallas_call | solution.py:595
  73.7 17.9 %all_to_all.27 = f32[128,8,128]{2,1,0:T(8,128)S(1)} all-to-all(f32[128,8,128]{2,1,0:T(8,128)S(1)} %second_mix.1), channel_id=1, replica_groups=mesh['gx'=8,'gy'=16] {'gx','gy'}, dimensions={0} | all-to-all | bytes 1048576 | tf_op jit(solution)/shard_map/all_to_all | solution.py:507
  91.6 9.3 %fine_level.1 = f32[4,16,16,128]{3,2,1,0:T(8,128)} custom-call(f32[1024,128]{1,0:T(8,128)S(1)} %bitcast.14, bf16[2,512,512]{2,1,0:T(8,128)(2,1)S(1)} %copy-done.1, bf16[64,128]{1,0:T(8,128)(2,1)} %constant.16.clone.z_back.z_back_h, f32[8,128,512]{2,1,0:T(8,128)} %get-tuple-element.49.skip, bf16[2,512,128]{2,1,0:T(8,128)(2,1)S(1)} %get-tuple-element.50.project_mix, ...), custom_call_target="tpu_custom_call" | custom-call | tf_op jit(solution)/shard_map/fine_level/pallas_call | solution.py:601
  (33 shorter events, 0.5 us)
Async XLA Ops:
  3.1 21.2 %all-to-all-start = ((f32[128,1,128]{2,1,0:T(1,128)}), f32[128,1,128]{2,1,0:T(1,128)S(1)}, u32[]{:S(2)}, u32[]{:S(2)}) async-start(f32[128,1,128]{2,1,0:T(1,128)} %bitcast.17), calls=%async_computation | async-start | bytes 131072 | tf_op jit(solution)/shard_map/all_to_all | solution.py:507
  16.2 0.8 copy-start.2
  17.0 1.0 %copy-start.7 = (f32[2,2,8,32,64]{4,3,2,1,0:T(8,128)S(1)}, f32[2,2,8,32,64]{4,3,2,1,0:T(8,128)}, u32[]{:S(2)}) copy-start(f32[2,2,8,32,64]{4,3,2,1,0:T(8,128)} %weights.2) | copy-start | bytes 786436
  18.2 11.8 %copy-start.14 = (f32[64,32]{0,1:T(8,128)S(1)}, f32[64,32]{0,1:T(8,128)}, u32[]{:S(2)}) copy-start(f32[64,32]{0,1:T(8,128)} %param.21) | copy-start | bytes 24580
  18.3 11.9 %copy-start.5 = (s32[2,512]{1,0:T(2,128)S(1)}, s32[2,512]{1,0:T(2,128)}, u32[]{:S(2)}) copy-start(s32[2,512]{1,0:T(2,128)} %constant.14.clone.steps_h.steps) | copy-start | bytes 12292
  18.3 11.9 %copy-start.6 = (f32[32]{0:T(128)S(1)}, f32[32]{0:T(128)}, u32[]{:S(2)}) copy-start(f32[32]{0:T(128)} %param.19) | copy-start | bytes 388
  18.3 11.9 %copy-start.8 = (f32[32,64]{1,0:T(8,128)S(1)}, f32[32,64]{1,0:T(8,128)}, u32[]{:S(2)}) copy-start(f32[32,64]{1,0:T(8,128)} %bypass_out.1) | copy-start | bytes 24580
  18.3 11.9 %copy-start.10 = (f32[64]{0:T(128)S(1)}, f32[64]{0:T(128)}, u32[]{:S(2)}) copy-start(f32[64]{0:T(128)} %param.22) | copy-start | bytes 772
  18.3 11.9 %copy-start.12 = (f32[4,16,512]{2,1,0:T(8,128)S(1)}, f32[4,16,512]{2,1,0:T(8,128)}, u32[]{:S(2)}) copy-start(f32[4,16,512]{2,1,0:T(8,128)} %constant.15.clone.waves) | copy-start | bytes 393220
  25.7 18.4 %all-to-all-start.1 = ((f32[128,8,128]{2,1,0:T(8,128)}), f32[128,8,128]{2,1,0:T(8,128)S(1)}, u32[]{:S(2)}, u32[]{:S(2)}) async-start(f32[128,8,128]{2,1,0:T(8,128)} %first_mix.1.after), calls=%async_computation.1 | async-start | bytes 1048576 | tf_op jit(solution)/shard_map/all_to_all | solution.py:507
  30.2 16.1 %copy-start = (f32[4,16,16,128]{3,2,1,0:T(8,128)S(1)}, f32[4,16,16,128]{3,2,1,0:T(8,128)}, u32[]{:S(2)}) copy-start(f32[4,16,16,128]{3,2,1,0:T(8,128)} %fields.5) | copy-start | bytes 1572868
  30.2 16.1 %copy-start.3 = (bf16[64,128]{1,0:T(8,128)(2,1)S(1)}, bf16[64,128]{1,0:T(8,128)(2,1)}, u32[]{:S(2)}) copy-start(bf16[64,128]{1,0:T(8,128)(2,1)} %constant.16.clone.z_back.z_back_h) | copy-start | bytes 49156
  30.2 16.1 %copy-start.4 = (bf16[32,256]{1,0:T(8,128)(2,1)S(1)}, bf16[32,256]{1,0:T(8,128)(2,1)}, u32[]{:S(2)}) copy-start(bf16[32,256]{1,0:T(8,128)(2,1)} %constant.17.clone.z_fwd) | copy-start | bytes 49156
  44.1 2.1 %collective-permute-start = (f32[128,8,128]{2,1,0:T(8,128)S(1)}, f32[128,8,128]{2,1,0:T(8,128)S(1)}, u32[]{:S(2)}, u32[]{:S(2)}) collective-permute-start(f32[128,8,128]{2,1,0:T(8,128)S(1)} %all-to-all-done.1), channel_id=1, source_target_pairs={{0,16},{16,0},{32,48},{48,32},{64,80},{80,64},{96,112},{112,96},{1... | collective-permute-start | bytes 1572872 | tf_op jit(solution)/shard_map/ppermute | solution.py:511
  46.3 11.8 %copy-start.15 = (f32[4]{0:T(128)S(1)}, f32[4]{0:T(128)}, u32[]{:S(2)}) copy-start(f32[4]{0:T(128)} %param.27) | copy-start | bytes 52
  51.6 6.6 %copy-start.13 = (f32[2,2,8,64,32]{3,4,2,1,0:T(8,128)S(1)}, f32[2,2,8,64,32]{3,4,2,1,0:T(8,128)}, u32[]{:S(2)}) copy-start(f32[2,2,8,64,32]{3,4,2,1,0:T(8,128)} %param.23) | copy-start | bytes 786436
  51.6 6.9 %copy-start.9 = (f32[4,32]{1,0:T(4,128)S(1)}, f32[4,32]{1,0:T(4,128)}, u32[]{:S(2)}) copy-start(f32[4,32]{1,0:T(4,128)} %project.1) | copy-start | bytes 1540
  51.6 6.9 %copy-start.11 = (f32[32]{0:T(128)S(1)}, f32[32]{0:T(128)}, u32[]{:S(2)}) copy-start(f32[32]{0:T(128)} %param.25) | copy-start | bytes 388
  51.7 1.4 %collective-permute-start.1 = (f32[2,128,128]{2,1,0:T(8,128)S(1)}, f32[2,128,128]{2,1,0:T(8,128)S(1)}, u32[]{:S(2)}, u32[]{:S(2)}) collective-permute-start(f32[2,128,128]{2,1,0:T(8,128)S(1)} %get-tuple-element.41), channel_id=1, source_target_pairs={{0,16},{16,0},{32,48},{48,32},{64,80},{80,64},{96,112},{112,96},{1... | collective-permute-start | bytes 393224 | tf_op jit(solution)/shard_map/ppermute | solution.py:511
  54.3 18.0 %all-to-all-start.2 = ((f32[128,8,128]{2,1,0:T(8,128)}), f32[128,8,128]{2,1,0:T(8,128)S(1)}, u32[]{:S(2)}, u32[]{:S(2)}) async-start(f32[128,8,128]{2,1,0:T(8,128)} %bitcast.8), calls=%async_computation.2 | async-start | bytes 1048576 | tf_op jit(solution)/shard_map/all_to_all | solution.py:507
  62.9 28.7 %copy-start.1 = (bf16[2,512,512]{2,1,0:T(8,128)(2,1)S(1)}, bf16[2,512,512]{2,1,0:T(8,128)(2,1)}, u32[]{:S(2)}) copy-start(bf16[2,512,512]{2,1,0:T(8,128)(2,1)} %get-tuple-element.48.table) | copy-start | bytes 3145732

commit v4 on v3

--- a/solution.py
+++ b/solution.py
@@ -18,7 +18,8 @@
 BACK = math.sqrt(2.0 / (KX * KY * KZ))
 F32 = jnp.float32
 BF16 = jnp.bfloat16
-UNROLL = 2
+UNROLL = 8
+FINE_UNROLL = 1
 VMEM = pl.BlockSpec(memory_space=pltpu.VMEM)
 HBM = pl.BlockSpec(memory_space=pltpu.HBM)
 PARAMS = pltpu.CompilerParams(vmem_limit_bytes=16 << 20)
@@ -181,7 +182,7 @@
 
 
 def first_spectrum(
-    fields, ztab_h, ptab_h, steps_h, out, fields_v, ztab, ptab, steps, sems,
+    fields, ztab_h, ptab_h, steps_h, out, token, fields_v, ztab, ptab, steps, sems,
 ):
     pairs = [(steps_h, steps)]
     for ch in range(CIN):
@@ -217,6 +218,7 @@
         cos_s, sin_s = turn[:, 2 * s : 2 * s + 1], turn[:, 2 * s + 1 : 2 * s + 2]
         rows.append(cos_s * pair + sin_s * pltpu.roll(pair, 64, 1))
     out[...] = jnp.where(low, rows[0], pltpu.roll(rows[1], 64, 1))
+    token[...] = rows[0][:8]
 
 
 def prepare_mix(after, weights, lift, lift_bias, weights_v, lift_wide, bias_column, sem):
@@ -229,8 +231,9 @@
     copy.wait()
 
 
-def prepare_coarse(
-    after, waves, steps, lift, lift_bias, bypass_in, bias_in, bypass_out, spread_t, pack,
+def prepare(
+    after, waves, steps, lift, lift_bias, bypass_in, bias_in, bypass_out, bias_out, project,
+    spread_t, pack, fine_t, wide_mix, project_mix, bias_mix,
 ):
     nt = ((1,), (1,))
     gx, gy = my_place()
@@ -267,15 +270,7 @@
         pick = ones_where(iota((128, C2), 1) == 32 * h + iota((128, C2), 0) % 32)
         wide = exact(exact(pick, bypass_out[...], nt), spread_d)
         high, less = split(jnp.where(same, wide, 0.0))
-        pack[368 + 128 * h : 496 + 128 * h] = jnp.concatenate([high, less], axis=1)
-
-
-def prepare_fine(
-    after, waves, steps, fields, lift, lift_bias, bias_out, project, project_bias,
-    fine_t, project_mix, bias_mix, base,
-):
-    nt = ((1,), (1,))
-    own = device_waves(waves, steps, my_place())
+        wide_mix[128 * h : 128 * h + 128] = jnp.concatenate([high, less], axis=1)
     scaled = (own[0] * BACK, own[1] * BACK)
     for x in range(0, 16, 8):
         pair = wave_rows(scaled, waves[2], waves[3], range(x, x + 8))
@@ -294,8 +289,25 @@
     high = made.astype(BF16).astype(F32)
     project_mix[0] = jnp.where(lane < 64, high, made - high).astype(BF16)
     project_mix[1] = jnp.where(lane < 64, high, 0.0).astype(BF16)
+
+
+def bypass(
+    after, values, wide_mix_h, fields, lift, lift_bias, project, project_bias, skip, base,
+    values_v, skip_v, wide_mix, in_sems, out_sems,
+):
+    def taken(p):
+        return pltpu.make_async_copy(values.at[p], values_v.at[p], in_sems.at[p])
+
+    def given(p):
+        return pltpu.make_async_copy(skip_v.at[p], skip.at[p], out_sems.at[p])
+
+    mix_copy = pltpu.make_async_copy(wide_mix_h, wide_mix, in_sems.at[8])
+    mix_copy.start()
+    for p in range(8):
+        taken(p).start()
     across = exact(project[...], lift[...])
-    constant = project_bias[...] + exact(project[...], lift_bias[...], nt)
+    constant = project_bias[...] + exact(project[...], lift_bias[...], ((1,), (1,)))
+    mix_copy.wait()
 
     def step(x, carry):
         for o in range(CIN):
@@ -306,6 +318,20 @@
         return carry
 
     lax.fori_loop(0, 16, step, 0)
+
+    def wide_step(p, carry):
+        taken(p).wait()
+        for q in range(2):
+            at = slice(256 * q, 256 * q + 256)
+            high, less = values_v[p, 0, :, at], values_v[p, 1, :, at]
+            wide = mm(high, wide_mix[:, :256]) + mm(high, wide_mix[:, 256:])
+            skip_v[p, :, at] = wide + mm(less, wide_mix[:, :256])
+        given(p).start()
+        return carry
+
+    lax.fori_loop(0, 8, wide_step, 0, unroll=2)
+    for p in range(8):
+        given(p).wait()
 
 
 def mixed_row(columns, weights, wide):
@@ -333,7 +359,7 @@
     ]
 
 
-def first_mix(arrived, lift_wide, bias_column, weights, out):
+def first_mix(arrived, lift_wide, bias_column, weights, out, token):
     row = jnp.sum(arrived[...], axis=0, keepdims=True)
     source = lax.broadcasted_iota(jnp.int32, (128, 32), 0) // CIN
     pick = (source == lax.broadcasted_iota(jnp.int32, (128, 32), 1)).astype(F32)
@@ -350,23 +376,14 @@
         return lifted[:, at : at + 1]
 
     halves = mixed_row(column, weights, 32)
+    token[...] = halves[0]
     for n in range(OWNERS):
         out[n] = halves[n // 16 % 2]
 
 
-def second_mix(arrived_h, weights, out, arrived, sems):
-    copies = [
-        pltpu.make_async_copy(
-            arrived_h.at[pl.ds(32 * i, 32)], arrived.at[pl.ds(32 * i, 32)], sems.at[i]
-        )
-        for i in range(4)
-    ]
-    for copy in copies:
-        copy.start()
+def second_mix(arrived, weights, out):
     sums = [None, None]
     for n in range(OWNERS):
-        if n % 32 == 0:
-            copies[n // 32].wait()
         half = n // 16 % 2
         sums[half] = arrived[n] if sums[half] is None else sums[half] + arrived[n]
     stacked = jnp.concatenate(sums + [jnp.zeros((112, 128), F32)], axis=0).T
@@ -383,7 +400,7 @@
 
 def coarse_level(
     mine, other, pack, fields, z_back, z_fwd,
-    kept, sent, skip, y_s, rhs_s, g_s, t_s, skip_v, sems,
+    kept, sent, values, y_s, rhs_s, g_s, t_s, values_v, sems,
 ):
     core = lax.axis_index("gx") % 2
     modes = []
@@ -429,11 +446,9 @@
             at = slice(128 * t, 128 * t + 128)
             g_s[t, pl.ds(pl.multiple_of(p * 8, 8), 8), :] = made[:8, at]
             g_s[t, pl.ds(pl.multiple_of(p * 8 + 64, 8), 8), :] = made[8:, at]
-        for q in range(2):
-            at = slice(256 * q, 256 * q + 256)
-            wide = mm(vh[:, at], pack[368:624, 0:256]) + mm(vh[:, at], pack[368:624, 256:512])
-            skip_v[p, :, at] = wide + mm(vl[:, at], pack[368:624, 0:256])
-        pltpu.make_async_copy(skip_v.at[p], skip.at[p], sems.at[p]).start()
+        values_v[p, 0] = vh
+        values_v[p, 1] = vl
+        pltpu.make_async_copy(values_v.at[p], values.at[p], sems.at[p]).start()
         return carry
 
     lax.fori_loop(0, 8, step, 0, unroll=UNROLL)
@@ -449,10 +464,10 @@
         kept[t] = t_s[2 * core + t]
         sent[t] = t_s[2 * (1 - core) + t]
     for p in range(8):
-        pltpu.make_async_copy(skip_v.at[p], skip.at[p], sems.at[p]).wait()
-
-
-def spread(kept, got, table, out):
+        pltpu.make_async_copy(values_v.at[p], values.at[p], sems.at[p]).wait()
+
+
+def spread(kept, got, table, out, token):
     rows = [jnp.concatenate([ref[0], ref[1]], axis=1) for ref in (kept, got)]
     th, tl = split(jnp.concatenate(rows, axis=0))
     for t in range(4):
@@ -460,16 +475,34 @@
         made = mm(table[0, at], th) + mm(table[0, at], tl) + mm(table[1, at], th)
         for u in range(2):
             out[pl.ds(2 * t + u, OWNERS, stride=8), :] = made[:, 128 * u : 128 * u + 128]
+    token[...] = made[:8, :128]
 
 
 def fine_level(
-    arrived, table, z_back_h, skip, project_mix, bias_mix, base_h, out, base,
-    y_s, rhs_s, skip_v, z_back, sems,):
-    copies = [pltpu.make_async_copy(skip.at[p], skip_v.at[p], sems.at[p]) for p in range(8)]
-    copies.append(pltpu.make_async_copy(z_back_h, z_back, sems.at[8]))
-    copies.append(pltpu.make_async_copy(base_h, base, sems.at[9]))
-    for copy in copies:
+    arrived, table, z_back_h, skip, project_h, bias_h, base_h, out, base, out_v,
+    y_s, rhs_s, skip_v, z_back, project_mix, bias_mix, sems, base_sems, out_sems,):
+    def taken(p):
+        rows = pl.ds(2 * p, 2)
+        return (
+            pltpu.make_async_copy(skip.at[p], skip_v.at[p], sems.at[p]),
+            pltpu.make_async_copy(base_h.at[:, rows], base.at[:, rows], base_sems.at[p]),
+        )
+
+    def given(p):
+        rows = pl.ds(2 * p, 2)
+        return pltpu.make_async_copy(out_v.at[:, rows], out.at[:, rows], out_sems.at[p])
+
+    small = [
+        pltpu.make_async_copy(source, target, sems.at[i])
+        for i, source, target in (
+            (8, z_back_h, z_back), (9, project_h, project_mix), (10, bias_h, bias_mix)
+        )
+    ]
+    for copy in small:
         copy.start()
+    for p in range(8):
+        for copy in taken(p):
+            copy.start()
     modes = []
     for t in range(4):
         tiles = [arrived[pl.ds(2 * t + u, OWNERS, stride=8), :] for u in range(2)]
@@ -485,22 +518,28 @@
             made = regroup([y_s[t, pl.ds(4 * y + u, 32, stride=16), :] for u in range(4)])
             for v in range(4):
                 rhs_s[y, pl.ds(32 * (4 * t + v), 32), :] = made[v]
-    for copy in copies:
+    for copy in small:
         copy.wait()
 
-    def step(x, carry):
-        rows = [rhs_s[t, pl.ds(x, 16, stride=16), :] for t in range(4)]
-        high, less = split(jnp.concatenate(rows, axis=1))
-        right = jnp.concatenate([high, less, high, bias_mix[...]], axis=0)
-        before = mm(z_back[...], right, ((0,), (0,)))
-        vh, vl = split(gelu(before + skip_v[x // 2]))
-        made = (mm(vh, project_mix[0]) + mm(vl, project_mix[1])).T
-        made = made[:64] + made[64:]
-        for o in range(CIN):
-            out[o, x] = made[16 * o : 16 * o + 16] + base[o, x]
+    def step(p, carry):
+        for copy in taken(p):
+            copy.wait()
+        for x in (2 * p, 2 * p + 1):
+            rows = [rhs_s[t, pl.ds(x, 16, stride=16), :] for t in range(4)]
+            high, less = split(jnp.concatenate(rows, axis=1))
+            right = jnp.concatenate([high, less, high, bias_mix[...]], axis=0)
+            before = mm(z_back[...], right, ((0,), (0,)))
+            vh, vl = split(gelu(before + skip_v[p]))
+            made = (mm(vh, project_mix[0]) + mm(vl, project_mix[1])).T
+            made = made[:64] + made[64:]
+            for o in range(CIN):
+                out_v[o, x] = made[16 * o : 16 * o + 16] + base[o, x]
+        given(p).start()
         return carry
 
-    lax.fori_loop(0, 16, step, 0, unroll=UNROLL)
+    lax.fori_loop(0, 8, step, 0, unroll=FINE_UNROLL)
+    for p in range(8):
+        given(p).wait()
 
 
 def exchange(tiles):
@@ -525,10 +564,10 @@
     shape = jax.ShapeDtypeStruct
     dma = pltpu.SemaphoreType.DMA
     work = pl.CostEstimate(flops=1 << 31, transcendentals=0, bytes_accessed=6 << 20)
-    spectrum = pl.pallas_call(
+    spectrum, token = pl.pallas_call(
         first_spectrum,
-        out_shape=shape((OWNERS, 128), F32),
-        in_specs=[HBM] * 4, out_specs=VMEM,
+        out_shape=(shape((OWNERS, 128), F32), shape((8, 128), F32)),
+        in_specs=[HBM] * 4, out_specs=(VMEM, VMEM),
         scratch_shapes=[
             pltpu.VMEM((CIN, 16, 16, NZ), F32), pltpu.VMEM((CIN, 384, 128), BF16),
             pltpu.VMEM((2, 512, 256), BF16), pltpu.VMEM((2, 512), jnp.int32), dma((10,)),
@@ -540,76 +579,84 @@
         out_shape=(
             shape((2, 2, KZ, C1, C2), F32), shape((C1, 128), F32), shape((C1, 32), F32),
         ),
-        in_specs=[HBM] * 2 + [VMEM] * 2, out_specs=(VMEM,) * 3, name="prepare_mix",
+        in_specs=[VMEM, HBM, VMEM, VMEM], out_specs=(VMEM,) * 3, name="prepare_mix",
         scratch_shapes=[dma(())], cost_estimate=work,
-    )(spectrum, spectral_in, lift, lift_bias[:, None])
+    )(token, stay(spectral_in), lift, lift_bias[:, None])
     arrived, prepared = lax.optimization_barrier((exchange(spectrum), prepared))
     weights, lift_wide, bias_column = prepared
-    mixed = call(
+    mixed, token = call(
         first_mix,
-        out_shape=shape((OWNERS, 8, 128), F32),
-        in_specs=[VMEM] * 4, out_specs=VMEM, name="first_mix",
+        out_shape=(shape((OWNERS, 8, 128), F32), shape((8, 128), F32)),
+        in_specs=[VMEM] * 4, out_specs=(VMEM, VMEM), name="first_mix",
     )(arrived, lift_wide, bias_column, weights)
     prepared = call(
-        prepare_coarse,
-        out_shape=(shape((2, 512, 256), BF16), shape((624, 512), BF16)),
-        in_specs=[HBM] + [VMEM] * 7, out_specs=(VMEM,) * 2, name="prepare_coarse",
-        cost_estimate=work,
-    )(mixed, waves, steps, lift, lift_bias[None], bypass_in, bias_in[None], bypass_out)
+        prepare,
+        out_shape=(
+            shape((2, 512, 256), BF16), shape((368, 512), BF16), pltpu.HBM((2, 512, 512), BF16),
+            pltpu.HBM((256, 512), BF16), pltpu.HBM((2, 512, 128), BF16),
+            pltpu.HBM((16, 512), BF16),
+        ),
+        in_specs=[VMEM] * 10, out_specs=(VMEM,) * 6, name="prepare", cost_estimate=work,
+    )(
+        token, waves, steps, lift, lift_bias[None], bypass_in, bias_in[None], bypass_out,
+        bias_out[None], project,
+    )
     mine, prepared = lax.optimization_barrier((exchange(mixed), prepared))
-    spread_t, pack = prepared
-    kept, sent, skip = call(
+    spread_t, pack, fine_t, wide_mix, project_mix, bias_mix = prepared
+    kept, sent, values = call(
         coarse_level,
         out_shape=(
             shape((2, 128, 128), F32), shape((2, 128, 128), F32),
-            pltpu.HBM((8, NZ, 512), F32),
+            pltpu.HBM((8, 2, NZ, 512), BF16),
         ),
         in_specs=[VMEM] * 6, out_specs=(VMEM, VMEM, HBM), name="coarse_level",
         scratch_shapes=[pltpu.VMEM((4, 128, 128), F32)] * 4
-        + [pltpu.VMEM((8, NZ, 512), F32), dma((8,))],
+        + [pltpu.VMEM((8, 2, NZ, 512), BF16), dma((8,))],
     )(
         mine.reshape(OWNERS * 8, 128), between_cores(mine).reshape(OWNERS * 8, 128), pack,
         fields, z_back, z_fwd,
     )
-    spectrum = call(
+    spectrum, token = call(
         spread,
-        out_shape=shape((OWNERS * 8, 128), F32),
-        in_specs=[VMEM] * 3, out_specs=VMEM, name="spread",
+        out_shape=(shape((OWNERS * 8, 128), F32), shape((8, 128), F32)),
+        in_specs=[VMEM] * 3, out_specs=(VMEM, VMEM), name="spread",
     )(kept, between_cores(sent), spread_t)
     prepared = call(
-        prepare_fine,
-        out_shape=(
-            pltpu.HBM((2, 512, 512), BF16), shape((2, 512, 128), BF16), shape((16, 512), BF16),
-            pltpu.HBM((CIN, 16, 16, NZ), F32),
-        ),
-        in_specs=[HBM] + [VMEM] * 8, out_specs=(VMEM,) * 4, name="prepare_fine",
+        bypass,
+        out_shape=(pltpu.HBM((8, NZ, 512), F32), pltpu.HBM((CIN, 16, 16, NZ), F32)),
+        in_specs=[VMEM, HBM, HBM] + [VMEM] * 5, out_specs=(HBM, VMEM), name="bypass",
+        scratch_shapes=[
+            pltpu.VMEM((8, 2, NZ, 512), BF16), pltpu.VMEM((8, NZ, 512), F32),
+            pltpu.VMEM((256, 512), BF16), dma((9,)), dma((8,)),
+        ],
         cost_estimate=work,
     )(
-        spectrum, waves, steps, fields, lift, lift_bias[None], bias_out[None], project,
+        token, stay(values), stay(wide_mix), fields, lift, lift_bias[None], project,
         project_bias[:, None],
     )
     arrived, prepared = lax.optimization_barrier(
         (exchange(spectrum.reshape(OWNERS, 8, 128)), prepared)
     )
-    fine_t, project_mix, bias_mix, base = prepared
+    skip, base = prepared
     mixed = call(
         second_mix,
         out_shape=shape((OWNERS, 8, 128), F32),
-        in_specs=[HBM, VMEM], out_specs=VMEM, name="second_mix",
-        scratch_shapes=[pltpu.VMEM((OWNERS, 8, 128), F32), dma((4,))],
+        in_specs=[VMEM, VMEM], out_specs=VMEM, name="second_mix",
     )(arrived, spectral_out)
     return call(
         fine_level,
         out_shape=shape((CIN, 16, 16, NZ), F32),
-        in_specs=[VMEM, VMEM, HBM, HBM, VMEM, VMEM, HBM], out_specs=VMEM, name="fine_level",
+        in_specs=[VMEM, VMEM] + [HBM] * 5, out_specs=HBM, name="fine_level",
         scratch_shapes=[
-            pltpu.VMEM((CIN, 16, 16, NZ), F32),
+            pltpu.VMEM((CIN, 16, 16, NZ), F32), pltpu.VMEM((CIN, 16, 16, NZ), F32),
             pltpu.VMEM((2, 512, 128), F32), pltpu.VMEM((4, 256, 128), F32),
-            pltpu.VMEM((8, NZ, 512), F32), pltpu.VMEM((64, NZ), BF16), dma((10,)),
+            pltpu.VMEM((8, NZ, 512), F32), pltpu.VMEM((64, NZ), BF16),
+            pltpu.VMEM((2, 512, 128), BF16), pltpu.VMEM((16, 512), BF16), dma((11,)), dma((8,)),
+            dma((8,)),
         ],
     )(
         exchange(mixed).reshape(OWNERS * 8, 128), fine_t, stay(jnp.asarray(z_back)), stay(skip),
-        project_mix, bias_mix, stay(base),
+        stay(project_mix), stay(bias_mix), stay(base),
     )
 
 

time: 101 us -> 97.9 us (0.969)
  waiting for transfers between devices: 30.7 us -> 26.6 us
  Pallas kernels: 27.4 us -> 29.4 us
  local copies, waits for them, and re-layouts: 3.99 us -> 2.78 us
    all_to_all x3, waiting for transfers between devices: 28.2 us -> 24.1 us  [exchange(): return lax.all_to_all(tiles, AXES, split_axis=0, concat_axis=0, tiled=True)]
    pallas_call x6, Pallas kernels: 12.6 us -> 16.3 us  [the longest x1 6.67 us: on_device(): call(bypass, out_shape=(pltpu.HBM((8, NZ, 512), F32), pltpu.HBM((CIN, 16,...]
    pallas_call x1, Pallas kernels: 5.32 us -> 3.37 us  [on_device(): call(coarse_level, out_shape=(shape((2, 128, 128), F32), shape((2, 128, 1...]
    unnamed x35 -> x33, local copies, waits for them, and re-layouts: 3.16 us -> 1.95 us
  transfers between devices with their start and end apart: 5 -> 5, of which waited for: 5 -> 5; matrix products, arithmetic and copies ran while one was open for 2% -> 2% of each run, Pallas kernels for 6% -> 11%
where the time goes in v4:
time: 97.9 us; the launch traced here: 97.5 us
  Pallas kernels  29.4 us (30%)
  waiting for transfers between devices  26.6 us (27%)
  starting transfers between devices  20.6 us (21%)
  blocking collectives  17.9 us (18%)
  local copies, waits for them, and re-layouts  2.78 us (3%)
    all_to_all x3, waiting for transfers between devices, exchange(): return lax.all_to_all(tiles, AXES, split_axis=0, concat_axis=0, tiled=True)  24.1 us
    all_to_all x3, starting transfers between devices, exchange(): return lax.all_to_all(tiles, AXES, split_axis=0, concat_axis=0, tiled=True)  19.6 us
    all_to_all x1, blocking collectives, exchange(): return lax.all_to_all(tiles, AXES, split_axis=0, concat_axis=0, tiled=True)  17.9 us
    pallas_call x1, Pallas kernels, on_device(): call(fine_level, out_shape=shape((CIN, 16, 16, NZ), F32), in_specs=[VMEM,...  8.52 us
    pallas_call x1, Pallas kernels, on_device(): call(bypass, out_shape=(pltpu.HBM((8, NZ, 512), F32), pltpu.HBM((CIN, 16,...  6.67 us
    pallas_call x1, Pallas kernels, on_device(): call(coarse_level, out_shape=(shape((2, 128, 128), F32), shape((2, 128, 1...  3.37 us
    pallas_call x1, Pallas kernels, on_device(): call(prepare, out_shape=(shape((2, 512, 256), BF16), shape((368, 512), BF...  3.2 us
    pallas_call x1, Pallas kernels, on_device(): pl.pallas_call(first_spectrum, out_shape=(shape((OWNERS, 128), F32), shap...  3.14 us
  transfers between devices with their start and end apart: 5, of which 5 were waited for; matrix products, arithmetic and copies ran while one was open for 2% of the time, Pallas kernels for 11%

profile of v4, /device:TPU:1, one launch (start us, length us, event | category | flops | bytes accessed | tf_op | source)
XLA Modules:
  0.0 97.5 jit_solution(7542266118023371782)
XLA Ops:
  0.0 3.1 %first_spectrum.1 = (f32[128,128]{1,0:T(8,128)}, f32[8,128]{1,0:T(8,128)}) custom-call(f32[4,16,16,128]{3,2,1,0:T(8,128)} %fields.5, bf16[4,384,128]{2,1,0:T(8,128)(2,1)} %constant.12.clone.ztab_h, bf16[2,512,256]{2,1,0:T(8,128)(2,1)} %constant.13.clone.ptab_h, s32[2,512]{1,0:T(2,128)} %constant.14.clone.steps_h.steps), custom_call_target="tpu_custom_call" | custom-call | tf_op jit(solution)/shard_map/first_spectrum/pallas_call | solution.py:567
  3.2 11.5 %all-to-all-start = ((f32[128,1,128]{2,1,0:T(1,128)}), f32[128,1,128]{2,1,0:T(1,128)S(1)}, u32[]{:S(2)}, u32[]{:S(2)}) async-start(f32[128,1,128]{2,1,0:T(1,128)} %bitcast.22), calls=%async_computation | async-start | bytes 131072 | tf_op jit(solution)/shard_map/all_to_all | solution.py:546
  14.7 0.8 copy.26.lift
  15.4 0.7 copy.27.lift_bias
  16.2 0.7 copy-done.7
  16.9 1.1 %prepare_mix.1 = (f32[2,2,8,32,64]{4,3,2,1,0:T(8,128)S(1)}, f32[32,128]{1,0:T(8,128)S(1)}, f32[32,32]{1,0:T(8,128)S(1)}) custom-call(f32[8,128]{1,0:T(8,128)S(1)} %copy-done.7, f32[2,2,8,32,64]{4,3,2,1,0:T(8,128)} %weights.2, f32[32,4]{1,0:T(8,128)S(1)} %copy.26.lift, f32[32,1]{1,0:T(8,128)S(1)} %copy.27.lift_bias), custom_call_target="tpu_custom_call" | custom-call | flops 2147483648 | bytes 6291456 | tf_op jit(solution)/shard_map/prepare_mix/pallas_call | solution.py:577
  18.0 6.3 %all-to-all-done = f32[128,1,128]{2,1,0:T(1,128)S(1)} async-done(((f32[128,1,128]{2,1,0:T(1,128)}), f32[128,1,128]{2,1,0:T(1,128)S(1)}, u32[]{:S(2)}, u32[]{:S(2)}) %all-to-all-start) | async-done | bytes 65568 | tf_op jit(solution)/shard_map/all_to_all | solution.py:546
  24.4 1.4 %first_mix.1 = (f32[128,8,128]{2,1,0:T(8,128)}, f32[8,128]{1,0:T(8,128)S(1)}) custom-call(f32[128,128]{1,0:T(8,128)S(1)} %bitcast.16, f32[32,128]{1,0:T(8,128)S(1)} %get-tuple-element.45.lift_wide, f32[32,32]{1,0:T(8,128)S(1)} %get-tuple-element.46.bias_column, f32[2,2,8,32,64]{4,3,2,1,0:T(8,128)S(1)} %get-tuple-element.47.weights), custom_call_target="tpu_custom_call" | custom-call | tf_op jit(solution)/shard_map/first_mix/pallas_call | solution.py:587
  25.8 4.3 %all-to-all-start.1 = ((f32[128,8,128]{2,1,0:T(8,128)}), f32[128,8,128]{2,1,0:T(8,128)S(1)}, u32[]{:S(2)}, u32[]{:S(2)}) async-start(f32[128,8,128]{2,1,0:T(8,128)} %get-tuple-element.48), calls=%async_computation.1 | async-start | bytes 1048576 | tf_op jit(solution)/shard_map/all_to_all | solution.py:546
  30.2 3.2 %prepare.1 = (bf16[2,512,256]{2,1,0:T(8,128)(2,1)S(1)}, bf16[368,512]{1,0:T(8,128)(2,1)S(1)}, bf16[2,512,512]{2,1,0:T(8,128)(2,1)}, bf16[256,512]{1,0:T(8,128)(2...) custom-call(f32[8,128]{1,0:T(8,128)S(1)} %get-tuple-element.49.after, f32[4,16,512]{2,1,0:T(8,128)S(1)} %copy-done.11, ...), custom_call_target="tpu_custom_call" | custom-call | flops 2147483648 | bytes 6291456 | tf_op jit(solution)/shard_map/prepare/pallas_call | solution.py:592
  33.4 10.7 %all-to-all-done.1 = f32[128,8,128]{2,1,0:T(8,128)S(1)} async-done(((f32[128,8,128]{2,1,0:T(8,128)}), f32[128,8,128]{2,1,0:T(8,128)S(1)}, u32[]{:S(2)}, u32[]{:S(2)}) %all-to-all-start.1) | async-done | bytes 524320 | tf_op jit(solution)/shard_map/all_to_all | solution.py:546
  44.2 0.6 collective-permute-start
  44.8 1.5 %collective-permute-done = f32[128,8,128]{2,1,0:T(8,128)S(1)} collective-permute-done((f32[128,8,128]{2,1,0:T(8,128)S(1)}, f32[128,8,128]{2,1,0:T(8,128)S(1)}, u32[]{:S(2)}, u32[]{:S(2)}) %collective-permute-start) | collective-permute-done | bytes 524320 | tf_op jit(solution)/shard_map/ppermute | solution.py:550
  46.3 3.4 %coarse_level.1 = (f32[2,128,128]{2,1,0:T(8,128)S(1)}, f32[2,128,128]{2,1,0:T(8,128)S(1)}, bf16[8,2,128,512]{3,2,1,0:T(8,128)(2,1)}) custom-call(f32[1024,128]{1,0:T(8,128)S(1)} %bitcast.14, f32[1024,128]{1,0:T(8,128)S(1)} %bitcast.15, bf16[368,512]{1,0:T(8,128)(2,1)S(1)} %get-tuple-element.57.pack, f32[4,16,16,128]{3,2,1,0:T(8,128)S(1)} %copy-done, ...), custom_call_target="tpu_custom_call" | custom-call | tf_op jit(solution)/shard_map/coarse_level/pallas_call | solution.py:606
  49.7 0.5 collective-permute-start.1
  50.1 1.0 %collective-permute-done.1.got = f32[2,128,128]{2,1,0:T(8,128)S(1)} collective-permute-done((f32[2,128,128]{2,1,0:T(8,128)S(1)}, f32[2,128,128]{2,1,0:T(8,128)S(1)}, u32[]{:S(2)}, u32[]{:S(2)}) %collective-permute-start.1) | collective-permute-done | bytes 131104 | tf_op jit(solution)/shard_map/ppermute | solution.py:550
  51.1 1.2 %spread.1 = (f32[1024,128]{1,0:T(8,128)}, f32[8,128]{1,0:T(8,128)S(1)}) custom-call(f32[2,128,128]{2,1,0:T(8,128)S(1)} %get-tuple-element.58.kept, f32[2,128,128]{2,1,0:T(8,128)S(1)} %collective-permute-done.1.got, bf16[2,512,256]{2,1,0:T(8,128)(2,1)S(1)} %get-tuple-element.60.table), custom_call_target="tpu_custom_call" | custom-call | tf_op jit(solution)/shard_map/spread/pallas_call | solution.py:619
  52.3 3.8 %all-to-all-start.2 = ((f32[128,8,128]{2,1,0:T(8,128)}), f32[128,8,128]{2,1,0:T(8,128)S(1)}, u32[]{:S(2)}, u32[]{:S(2)}) async-start(f32[128,8,128]{2,1,0:T(8,128)} %bitcast.9), calls=%async_computation.2 | async-start | bytes 1048576 | tf_op jit(solution)/shard_map/all_to_all | solution.py:546
  56.2 0.4 copy.32.weights
  56.6 6.7 %bypass.1 = (f32[8,128,512]{2,1,0:T(8,128)}, f32[4,16,16,128]{3,2,1,0:T(8,128)}) custom-call(f32[8,128]{1,0:T(8,128)S(1)} %get-tuple-element.62.after, bf16[8,2,128,512]{3,2,1,0:T(8,128)(2,1)} %get-tuple-element.63.values, bf16[256,512]{1,0:T(8,128)(2,1)} %get-tuple-element.64.wide_mix_h, f32[4,16,16,128]{3,2,1,0:T(8,128)S(1)} %copy-done, ...), custom_call_target="tpu_custom_call" | custom-call | flops 2147483648 | bytes 6291456 | tf_op jit(solution)/shard_map/bypass/pallas_call | solution.py:624
  63.2 7.1 %all-to-all-done.2.arrived = f32[128,8,128]{2,1,0:T(8,128)S(1)} async-done(((f32[128,8,128]{2,1,0:T(8,128)}), f32[128,8,128]{2,1,0:T(8,128)S(1)}, u32[]{:S(2)}, u32[]{:S(2)}) %all-to-all-start.2) | async-done | bytes 524320 | tf_op jit(solution)/shard_map/all_to_all | solution.py:546
  70.3 0.8 second_mix.1
  71.1 17.9 %all_to_all.27 = f32[128,8,128]{2,1,0:T(8,128)S(1)} all-to-all(f32[128,8,128]{2,1,0:T(8,128)S(1)} %second_mix.1), channel_id=1, replica_groups=mesh['gx'=8,'gy'=16] {'gx','gy'}, dimensions={0} | all-to-all | bytes 1048576 | tf_op jit(solution)/shard_map/all_to_all | solution.py:546
  88.9 8.5 %fine_level.1 = f32[4,16,16,128]{3,2,1,0:T(8,128)} custom-call(f32[1024,128]{1,0:T(8,128)S(1)} %bitcast.13, bf16[2,512,512]{2,1,0:T(8,128)(2,1)S(1)} %copy-done.1, bf16[64,128]{1,0:T(8,128)(2,1)} %constant.16.clone.z_back.z_back_h, f32[8,128,512]{2,1,0:T(8,128)} %get-tuple-element.69.skip, bf16[2,512,128]{2,1,0:T(8,128)(2,1)} %get-tuple-element.70.project_h, ...), custom_call_target="tpu_custom_call" | custom-call | tf_op jit(solution)/shard_map/fine_level/pallas_call | solution.py:646
  (31 shorter events, 0.2 us)
Async XLA Ops:
  3.2 21.2 %all-to-all-start = ((f32[128,1,128]{2,1,0:T(1,128)}), f32[128,1,128]{2,1,0:T(1,128)S(1)}, u32[]{:S(2)}, u32[]{:S(2)}) async-start(f32[128,1,128]{2,1,0:T(1,128)} %bitcast.22), calls=%async_computation | async-start | bytes 131072 | tf_op jit(solution)/shard_map/all_to_all | solution.py:546
  16.2 0.7 copy-start.7
  16.8 13.2 %copy-start.13 = (f32[64,32]{0,1:T(8,128)S(1)}, f32[64,32]{0,1:T(8,128)}, u32[]{:S(2)}) copy-start(f32[64,32]{0,1:T(8,128)} %param.21) | copy-start | bytes 24580
  16.8 13.3 %copy-start.4 = (s32[2,512]{1,0:T(2,128)S(1)}, s32[2,512]{1,0:T(2,128)}, u32[]{:S(2)}) copy-start(s32[2,512]{1,0:T(2,128)} %constant.14.clone.steps_h.steps) | copy-start | bytes 12292
  16.8 13.3 %copy-start.5 = (f32[32]{0:T(128)S(1)}, f32[32]{0:T(128)}, u32[]{:S(2)}) copy-start(f32[32]{0:T(128)} %param.19) | copy-start | bytes 388
  16.8 13.3 %copy-start.6 = (f32[32,64]{1,0:T(8,128)S(1)}, f32[32,64]{1,0:T(8,128)}, u32[]{:S(2)}) copy-start(f32[32,64]{1,0:T(8,128)} %bypass_out.1) | copy-start | bytes 24580
  16.9 13.3 %copy-start.8 = (f32[4,32]{1,0:T(4,128)S(1)}, f32[4,32]{1,0:T(4,128)}, u32[]{:S(2)}) copy-start(f32[4,32]{1,0:T(4,128)} %project.3) | copy-start | bytes 1540
  16.9 13.3 %copy-start.9 = (f32[64]{0:T(128)S(1)}, f32[64]{0:T(128)}, u32[]{:S(2)}) copy-start(f32[64]{0:T(128)} %param.22) | copy-start | bytes 772
  16.9 13.3 %copy-start.10 = (f32[32]{0:T(128)S(1)}, f32[32]{0:T(128)}, u32[]{:S(2)}) copy-start(f32[32]{0:T(128)} %param.25) | copy-start | bytes 388
  16.9 13.3 %copy-start.11 = (f32[4,16,512]{2,1,0:T(8,128)S(1)}, f32[4,16,512]{2,1,0:T(8,128)}, u32[]{:S(2)}) copy-start(f32[4,16,512]{2,1,0:T(8,128)} %constant.15.clone.waves) | copy-start | bytes 393220
  25.8 18.4 %all-to-all-start.1 = ((f32[128,8,128]{2,1,0:T(8,128)}), f32[128,8,128]{2,1,0:T(8,128)S(1)}, u32[]{:S(2)}, u32[]{:S(2)}) async-start(f32[128,8,128]{2,1,0:T(8,128)} %get-tuple-element.48), calls=%async_computation.1 | async-start | bytes 1048576 | tf_op jit(solution)/shard_map/all_to_all | solution.py:546
  30.2 16.1 %copy-start = (f32[4,16,16,128]{3,2,1,0:T(8,128)S(1)}, f32[4,16,16,128]{3,2,1,0:T(8,128)}, u32[]{:S(2)}) copy-start(f32[4,16,16,128]{3,2,1,0:T(8,128)} %fields.5) | copy-start | bytes 1572868
  30.2 16.1 %copy-start.2 = (bf16[64,128]{1,0:T(8,128)(2,1)S(1)}, bf16[64,128]{1,0:T(8,128)(2,1)}, u32[]{:S(2)}) copy-start(bf16[64,128]{1,0:T(8,128)(2,1)} %constant.16.clone.z_back.z_back_h) | copy-start | bytes 49156
  30.2 16.1 %copy-start.3 = (bf16[32,256]{1,0:T(8,128)(2,1)S(1)}, bf16[32,256]{1,0:T(8,128)(2,1)}, u32[]{:S(2)}) copy-start(bf16[32,256]{1,0:T(8,128)(2,1)} %constant.17.clone.z_fwd) | copy-start | bytes 49156
  33.4 22.7 %copy-start.14 = (f32[4]{0:T(128)S(1)}, f32[4]{0:T(128)}, u32[]{:S(2)}) copy-start(f32[4]{0:T(128)} %param.27) | copy-start | bytes 52
  33.4 22.8 %copy-start.12 = (f32[2,2,8,64,32]{3,4,2,1,0:T(8,128)S(1)}, f32[2,2,8,64,32]{3,4,2,1,0:T(8,128)}, u32[]{:S(2)}) copy-start(f32[2,2,8,64,32]{3,4,2,1,0:T(8,128)} %param.23) | copy-start | bytes 786436
  44.2 2.1 %collective-permute-start = (f32[128,8,128]{2,1,0:T(8,128)S(1)}, f32[128,8,128]{2,1,0:T(8,128)S(1)}, u32[]{:S(2)}, u32[]{:S(2)}) collective-permute-start(f32[128,8,128]{2,1,0:T(8,128)S(1)} %all-to-all-done.1), channel_id=1, source_target_pairs={{0,16},{16,0},{32,48},{48,32},{64,80},{80,64},{96,112},{112,96},{1... | collective-permute-start | bytes 1572872 | tf_op jit(solution)/shard_map/ppermute | solution.py:550
  49.7 1.4 %collective-permute-start.1 = (f32[2,128,128]{2,1,0:T(8,128)S(1)}, f32[2,128,128]{2,1,0:T(8,128)S(1)}, u32[]{:S(2)}, u32[]{:S(2)}) collective-permute-start(f32[2,128,128]{2,1,0:T(8,128)S(1)} %get-tuple-element.59), channel_id=1, source_target_pairs={{0,16},{16,0},{32,48},{48,32},{64,80},{80,64},{96,112},{112,96},{1... | collective-permute-start | bytes 393224 | tf_op jit(solution)/shard_map/ppermute | solution.py:550
  52.3 18.0 %all-to-all-start.2 = ((f32[128,8,128]{2,1,0:T(8,128)}), f32[128,8,128]{2,1,0:T(8,128)S(1)}, u32[]{:S(2)}, u32[]{:S(2)}) async-start(f32[128,8,128]{2,1,0:T(8,128)} %bitcast.9), calls=%async_computation.2 | async-start | bytes 1048576 | tf_op jit(solution)/shard_map/all_to_all | solution.py:546
  63.2 25.7 %copy-start.1 = (bf16[2,512,512]{2,1,0:T(8,128)(2,1)S(1)}, bf16[2,512,512]{2,1,0:T(8,128)(2,1)}, u32[]{:S(2)}) copy-start(bf16[2,512,512]{2,1,0:T(8,128)(2,1)} %get-tuple-element.68.table) | copy-start | bytes 3145732

commit v5 on v4

--- a/solution.py
+++ b/solution.py
@@ -233,7 +233,7 @@
 
 def prepare(
     after, waves, steps, lift, lift_bias, bypass_in, bias_in, bypass_out, bias_out, project,
-    spread_t, pack, fine_t, wide_mix, project_mix, bias_mix,
+    own_t, mate_t, spread_t, pack, fine_t, wide_mix, project_mix, bias_mix,
 ):
     nt = ((1,), (1,))
     gx, gy = my_place()
@@ -245,7 +245,8 @@
         jnp.concatenate(wave_rows(along, cos_y, sin_y, range(0, 16, 2)), axis=0)
         for along in (own, mate)
     ]
-    pack[0:128], pack[128:256] = split(tables[0] * BACK)
+    own_t[0:128], own_t[128:256] = split(tables[0] * BACK)
+    mate_t[0:128], mate_t[128:256] = split(tables[1] * BACK)
     scale = 1.0 / math.sqrt(TOTAL / 4.0)
     for patch in range(2):
         at = slice(128 * patch, 128 * patch + 128)
@@ -263,7 +264,7 @@
         same = iota((32, 128), 0) % 8 == 4 * (t // 2) + iota((32, 128), 1) // 32
         high, less = split(jnp.where(same, exact(through, lanes[t % 2]), 0.0))
         rows = bias_rows(exact(offset, lanes[t % 2]))
-        pack[256:368, at] = jnp.concatenate([rows, high, less, high], axis=0)
+        pack[:, at] = jnp.concatenate([rows, high, less, high], axis=0)
     spread_d = ones_where(iota((C1, 256), 0) == iota((C1, 256), 1) % 32)
     same = iota((128, 256), 0) // 32 == iota((128, 256), 1) // 64
     for h in range(2):
@@ -287,8 +288,7 @@
     lane = iota((512, 128), 1)
     made = jnp.where(iota((512, 128), 0) // 32 == lane % 16, made, 0.0)
     high = made.astype(BF16).astype(F32)
-    project_mix[0] = jnp.where(lane < 64, high, made - high).astype(BF16)
-    project_mix[1] = jnp.where(lane < 64, high, 0.0).astype(BF16)
+    project_mix[...] = jnp.where(lane < 64, high, made - high).T.astype(BF16)
 
 
 def bypass(
@@ -359,7 +359,7 @@
     ]
 
 
-def first_mix(arrived, lift_wide, bias_column, weights, out, token):
+def first_mix(arrived, lift_wide, bias_column, weights, out, token, blocks, sems):
     row = jnp.sum(arrived[...], axis=0, keepdims=True)
     source = lax.broadcasted_iota(jnp.int32, (128, 32), 0) // CIN
     pick = (source == lax.broadcasted_iota(jnp.int32, (128, 32), 1)).astype(F32)
@@ -377,8 +377,17 @@
 
     halves = mixed_row(column, weights, 32)
     token[...] = halves[0]
-    for n in range(OWNERS):
-        out[n] = halves[n // 16 % 2]
+    copies = []
+    for half in range(2):
+        for i in range(16):
+            blocks[half, i] = halves[half]
+        for i in range(half, 8, 2):
+            copies.append(
+                pltpu.make_async_copy(blocks.at[half], out.at[pl.ds(16 * i, 16)], sems.at[i])
+            )
+            copies[-1].start()
+    for copy in copies:
+        copy.wait()
 
 
 def second_mix(arrived, weights, out):
@@ -398,24 +407,26 @@
         out[n] = block
 
 
+def invert(arrived, table, out):
+    modes = []
+    for t in range(4):
+        tiles = [arrived[pl.ds(2 * t + u, OWNERS, stride=8), :] for u in range(2)]
+        modes.append(jnp.concatenate(tiles, axis=1))
+    mh, ml = split(jnp.concatenate(modes, axis=0))
+    made = mm(table[...], mh)
+    made = made[:128] + made[128:] + mm(table[:128], ml)
+    out[0] = made[:, :128]
+    out[1] = made[:, 128:]
+
+
 def coarse_level(
-    mine, other, pack, fields, z_back, z_fwd,
+    own, got, pack, fields, z_back, z_fwd,
     kept, sent, values, y_s, rhs_s, g_s, t_s, values_v, sems,
 ):
     core = lax.axis_index("gx") % 2
-    modes = []
-    for t in range(4):
-        tiles = [
-            ref[pl.ds(2 * t + u, OWNERS, stride=8), :] for ref in (mine, other) for u in range(2)
-        ]
-        modes.append(jnp.concatenate(tiles, axis=1))
-    mh, ml = split(jnp.concatenate(modes, axis=0))
-    th, tl = pack[0:128], pack[128:256]
-    made = mm(th, mh) + mm(tl, mh) + mm(th, ml)
-    for u in range(2):
-        for t in range(2):
-            at = 128 * (2 * u + t)
-            y_s[2 * ((core + u) % 2) + t] = made[:, at : at + 128]
+    for t in range(2):
+        y_s[2 * core + t] = own[t]
+        y_s[2 * (1 - core) + t] = got[t]
     for h in range(2):
         for t in range(2):
             for q in range(2):
@@ -437,7 +448,7 @@
             pooled.append(total * 0.25)
         ph, pll = split(jnp.concatenate(pooled, axis=0))
         left = jnp.concatenate([z_back[...], ph, ph, pll], axis=0)
-        right = jnp.concatenate([high, less, high, pack[256:368]], axis=0)
+        right = jnp.concatenate([high, less, high, pack[...]], axis=0)
         value = gelu(mm(left, right, ((0,), (0,))))
         vh, vl = split(value)
         made = mm(z_fwd[...], jnp.concatenate([vh, vl], axis=0))
@@ -467,15 +478,26 @@
         pltpu.make_async_copy(values_v.at[p], values.at[p], sems.at[p]).wait()
 
 
-def spread(kept, got, table, out, token):
+def spread(kept, got, table, out, token, out_v, sems):
     rows = [jnp.concatenate([ref[0], ref[1]], axis=1) for ref in (kept, got)]
     th, tl = split(jnp.concatenate(rows, axis=0))
-    for t in range(4):
-        at = slice(128 * t, 128 * t + 128)
-        made = mm(table[0, at], th) + mm(table[0, at], tl) + mm(table[1, at], th)
-        for u in range(2):
-            out[pl.ds(2 * t + u, OWNERS, stride=8), :] = made[:, 128 * u : 128 * u + 128]
-    token[...] = made[:8, :128]
+    copies = []
+    for j in range(4):
+        ah, al = [
+            jnp.concatenate([table[i, pl.ds(128 * t + 32 * j, 32)] for t in range(4)], axis=0)
+            for i in range(2)
+        ]
+        made = mm(ah, th) + mm(ah, tl) + mm(al, th)
+        for t in range(4):
+            for u in range(2):
+                piece = made[32 * t : 32 * t + 32, 128 * u : 128 * u + 128]
+                out_v[pl.ds(256 * j + 2 * t + u, 32, stride=8), :] = piece
+        rows = pl.ds(256 * j, 256)
+        copies.append(pltpu.make_async_copy(out_v.at[rows], out.at[rows], sems.at[j]))
+        copies[-1].start()
+    token[...] = out_v[:8]
+    for copy in copies:
+        copy.wait()
 
 
 def fine_level(
@@ -528,10 +550,10 @@
             rows = [rhs_s[t, pl.ds(x, 16, stride=16), :] for t in range(4)]
             high, less = split(jnp.concatenate(rows, axis=1))
             right = jnp.concatenate([high, less, high, bias_mix[...]], axis=0)
-            before = mm(z_back[...], right, ((0,), (0,)))
+            before = mm(z_back[...], right)
             vh, vl = split(gelu(before + skip_v[p]))
-            made = (mm(vh, project_mix[0]) + mm(vl, project_mix[1])).T
-            made = made[:64] + made[64:]
+            made = mm(project_mix[...], vh, ((1,), (1,)))
+            made = made[:64] + made[64:] + mm(project_mix[:64], vl, ((1,), (1,)))
             for o in range(CIN):
                 out_v[o, x] = made[16 * o : 16 * o + 16] + base[o, x]
         given(p).start()
@@ -586,23 +608,32 @@
     weights, lift_wide, bias_column = prepared
     mixed, token = call(
         first_mix,
-        out_shape=(shape((OWNERS, 8, 128), F32), shape((8, 128), F32)),
-        in_specs=[VMEM] * 4, out_specs=(VMEM, VMEM), name="first_mix",
+        out_shape=(pltpu.HBM((OWNERS, 8, 128), F32), shape((8, 128), F32)),
+        in_specs=[VMEM] * 4, out_specs=(HBM, VMEM), name="first_mix",
+        scratch_shapes=[pltpu.VMEM((2, 16, 8, 128), F32), dma((8,))],
     )(arrived, lift_wide, bias_column, weights)
     prepared = call(
         prepare,
         out_shape=(
-            shape((2, 512, 256), BF16), shape((368, 512), BF16), pltpu.HBM((2, 512, 512), BF16),
-            pltpu.HBM((256, 512), BF16), pltpu.HBM((2, 512, 128), BF16),
-            pltpu.HBM((16, 512), BF16),
+            shape((256, 512), BF16), shape((256, 512), BF16), shape((2, 512, 256), BF16),
+            shape((112, 512), BF16), pltpu.HBM((2, 512, 512), BF16), pltpu.HBM((256, 512), BF16),
+            pltpu.HBM((128, 512), BF16), pltpu.HBM((16, 512), BF16),
         ),
-        in_specs=[VMEM] * 10, out_specs=(VMEM,) * 6, name="prepare", cost_estimate=work,
+        in_specs=[VMEM] * 10, out_specs=(VMEM,) * 8, name="prepare", cost_estimate=work,
     )(
         token, waves, steps, lift, lift_bias[None], bypass_in, bias_in[None], bypass_out,
         bias_out[None], project,
     )
     mine, prepared = lax.optimization_barrier((exchange(mixed), prepared))
-    spread_t, pack, fine_t, wide_mix, project_mix, bias_mix = prepared
+    own_t, mate_t, spread_t, pack, fine_t, wide_mix, project_mix, bias_mix = prepared
+    mine = mine.reshape(OWNERS * 8, 128)
+    own, got = [
+        call(
+            invert, out_shape=shape((2, 128, 128), F32), in_specs=[VMEM] * 2, out_specs=VMEM,
+            name=name, cost_estimate=work,
+        )(mine, table)
+        for name, table in (("invert_own", own_t), ("invert_mate", mate_t))
+    ]
     kept, sent, values = call(
         coarse_level,
         out_shape=(
@@ -613,13 +644,13 @@
         scratch_shapes=[pltpu.VMEM((4, 128, 128), F32)] * 4
         + [pltpu.VMEM((8, 2, NZ, 512), BF16), dma((8,))],
     )(
-        mine.reshape(OWNERS * 8, 128), between_cores(mine).reshape(OWNERS * 8, 128), pack,
-        fields, z_back, z_fwd,
+        own, between_cores(got), pack, fields, z_back, z_fwd,
     )
     spectrum, token = call(
         spread,
-        out_shape=(shape((OWNERS * 8, 128), F32), shape((8, 128), F32)),
-        in_specs=[VMEM] * 3, out_specs=(VMEM, VMEM), name="spread",
+        out_shape=(pltpu.HBM((OWNERS * 8, 128), F32), shape((8, 128), F32)),
+        in_specs=[VMEM] * 3, out_specs=(HBM, VMEM), name="spread",
+        scratch_shapes=[pltpu.VMEM((OWNERS * 8, 128), F32), dma((4,))],
     )(kept, between_cores(sent), spread_t)
     prepared = call(
         bypass,
@@ -650,12 +681,12 @@
         scratch_shapes=[
             pltpu.VMEM((CIN, 16, 16, NZ), F32), pltpu.VMEM((CIN, 16, 16, NZ), F32),
             pltpu.VMEM((2, 512, 128), F32), pltpu.VMEM((4, 256, 128), F32),
-            pltpu.VMEM((8, NZ, 512), F32), pltpu.VMEM((64, NZ), BF16),
-            pltpu.VMEM((2, 512, 128), BF16), pltpu.VMEM((16, 512), BF16), dma((11,)), dma((8,)),
+            pltpu.VMEM((8, NZ, 512), F32), pltpu.VMEM((NZ, 64), BF16),
+            pltpu.VMEM((128, 512), BF16), pltpu.VMEM((16, 512), BF16), dma((11,)), dma((8,)),
             dma((8,)),
         ],
     )(
-        exchange(mixed).reshape(OWNERS * 8, 128), fine_t, stay(jnp.asarray(z_back)), stay(skip),
+        exchange(mixed).reshape(OWNERS * 8, 128), fine_t, stay(jnp.asarray(z_back.T)), stay(skip),
         stay(project_mix), stay(bias_mix), stay(base),
     )
 

time: 97.9 us -> 96.6 us (0.987)
    pallas_call x3 -> x5, Pallas kernels: 5.77 us -> 6.51 us  [the longest x1 3.33 us: on_device(): call(prepare, out_shape=(shape((256, 512), BF16), shape((256, 512), BF16)...]
  transfers between devices with their start and end apart: 5 -> 5, of which waited for: 5 -> 5; matrix products, arithmetic and copies ran while one was open for 2% -> 2% of each run, Pallas kernels for 11% -> 12%
where the time goes in v5:
time: 96.6 us; the launch traced here: 96.2 us
  Pallas kernels  29 us (30%)
  waiting for transfers between devices  25.7 us (27%)
  starting transfers between devices  20.7 us (21%)
  blocking collectives  17.9 us (19%)
  local copies, waits for them, and re-layouts  2.78 us (3%)
    all_to_all x3, waiting for transfers between devices, exchange(): return lax.all_to_all(tiles, AXES, split_axis=0, concat_axis=0, tiled=True)  24 us
    all_to_all x3, starting transfers between devices, exchange(): return lax.all_to_all(tiles, AXES, split_axis=0, concat_axis=0, tiled=True)  19.6 us
    all_to_all x1, blocking collectives, exchange(): return lax.all_to_all(tiles, AXES, split_axis=0, concat_axis=0, tiled=True)  17.9 us
    pallas_call x1, Pallas kernels, on_device(): call(fine_level, out_shape=shape((CIN, 16, 16, NZ), F32), in_specs=[VMEM,...  7.92 us
    pallas_call x1, Pallas kernels, on_device(): call(bypass, out_shape=(pltpu.HBM((8, NZ, 512), F32), pltpu.HBM((CIN, 16,...  6.66 us
    pallas_call x1, Pallas kernels, on_device(): call(prepare, out_shape=(shape((256, 512), BF16), shape((256, 512), BF16)...  3.33 us
    pallas_call x1, Pallas kernels, on_device(): pl.pallas_call(first_spectrum, out_shape=(shape((OWNERS, 128), F32), shap...  3.14 us
    pallas_call x1, Pallas kernels, on_device(): call(coarse_level, out_shape=(shape((2, 128, 128), F32), shape((2, 128, 1...  2.84 us
  transfers between devices with their start and end apart: 5, of which 5 were waited for; matrix products, arithmetic and copies ran while one was open for 2% of the time, Pallas kernels for 12%

profile of v5, /device:TPU:1, one launch (start us, length us, event | category | flops | bytes accessed | tf_op | source)
XLA Modules:
  0.0 96.2 jit_solution(17202296439138360944)
XLA Ops:
  0.0 3.1 %first_spectrum.1 = (f32[128,128]{1,0:T(8,128)}, f32[8,128]{1,0:T(8,128)}) custom-call(f32[4,16,16,128]{3,2,1,0:T(8,128)} %fields.5, bf16[4,384,128]{2,1,0:T(8,128)(2,1)} %constant.14.clone.ztab_h, bf16[2,512,256]{2,1,0:T(8,128)(2,1)} %constant.15.clone.ptab_h, s32[2,512]{1,0:T(2,128)} %constant.16.clone.steps_h.steps), custom_call_target="tpu_custom_call" | custom-call | tf_op jit(solution)/shard_map/first_spectrum/pallas_call | solution.py:589
  3.2 11.5 %all-to-all-start = ((f32[128,1,128]{2,1,0:T(1,128)}), f32[128,1,128]{2,1,0:T(1,128)S(1)}, u32[]{:S(2)}, u32[]{:S(2)}) async-start(f32[128,1,128]{2,1,0:T(1,128)} %bitcast.22), calls=%async_computation | async-start | bytes 131072 | tf_op jit(solution)/shard_map/all_to_all | solution.py:568
  14.7 0.8 copy.27.lift
  15.4 0.7 copy.28.lift_bias
  16.2 0.7 copy-done.7
  16.9 1.1 %prepare_mix.1 = (f32[2,2,8,32,64]{4,3,2,1,0:T(8,128)S(1)}, f32[32,128]{1,0:T(8,128)S(1)}, f32[32,32]{1,0:T(8,128)S(1)}) custom-call(f32[8,128]{1,0:T(8,128)S(1)} %copy-done.7, f32[2,2,8,32,64]{4,3,2,1,0:T(8,128)} %weights.2, f32[32,4]{1,0:T(8,128)S(1)} %copy.27.lift, f32[32,1]{1,0:T(8,128)S(1)} %copy.28.lift_bias), custom_call_target="tpu_custom_call" | custom-call | flops 2147483648 | bytes 6291456 | tf_op jit(solution)/shard_map/prepare_mix/pallas_call | solution.py:599
  18.0 6.3 %all-to-all-done = f32[128,1,128]{2,1,0:T(1,128)S(1)} async-done(((f32[128,1,128]{2,1,0:T(1,128)}), f32[128,1,128]{2,1,0:T(1,128)S(1)}, u32[]{:S(2)}, u32[]{:S(2)}) %all-to-all-start) | async-done | bytes 65568 | tf_op jit(solution)/shard_map/all_to_all | solution.py:568
  24.4 1.4 %first_mix.1 = (f32[128,8,128]{2,1,0:T(8,128)}, f32[8,128]{1,0:T(8,128)S(1)}) custom-call(f32[128,128]{1,0:T(8,128)S(1)} %bitcast.15, f32[32,128]{1,0:T(8,128)S(1)} %get-tuple-element.49.lift_wide, f32[32,32]{1,0:T(8,128)S(1)} %get-tuple-element.50.bias_column, f32[2,2,8,32,64]{4,3,2,1,0:T(8,128)S(1)} %get-tuple-element.51.weights), custom_call_target="tpu_custom_call" | custom-call | tf_op jit(solution)/shard_map/first_mix/pallas_call | solution.py:609
  25.8 4.3 %all-to-all-start.1 = ((f32[128,8,128]{2,1,0:T(8,128)}), f32[128,8,128]{2,1,0:T(8,128)S(1)}, u32[]{:S(2)}, u32[]{:S(2)}) async-start(f32[128,8,128]{2,1,0:T(8,128)} %get-tuple-element.52), calls=%async_computation.1 | async-start | bytes 1048576 | tf_op jit(solution)/shard_map/all_to_all | solution.py:568
  30.2 3.3 %prepare.1 = (bf16[256,512]{1,0:T(8,128)(2,1)S(1)}, bf16[256,512]{1,0:T(8,128)(2,1)S(1)}, bf16[2,512,256]{2,1,0:T(8,128)(2,1)S(1)}, bf16[112,512]{1,0:T(8,128)(2...) custom-call(f32[8,128]{1,0:T(8,128)S(1)} %get-tuple-element.53.after, ...), custom_call_target="tpu_custom_call" | custom-call | flops 2147483648 | bytes 6291456 | tf_op jit(solution)/shard_map/prepare/pallas_call | solution.py:615
  33.6 10.7 %all-to-all-done.1 = f32[128,8,128]{2,1,0:T(8,128)S(1)} async-done(((f32[128,8,128]{2,1,0:T(8,128)}), f32[128,8,128]{2,1,0:T(8,128)S(1)}, u32[]{:S(2)}, u32[]{:S(2)}) %all-to-all-start.1) | async-done | bytes 524320 | tf_op jit(solution)/shard_map/all_to_all | solution.py:568
  44.6 0.7 collective-permute-start
  45.6 0.6 collective-permute-done.got
  46.3 2.8 %coarse_level.1 = (f32[2,128,128]{2,1,0:T(8,128)S(1)}, f32[2,128,128]{2,1,0:T(8,128)S(1)}, bf16[8,2,128,512]{3,2,1,0:T(8,128)(2,1)}) custom-call(f32[2,128,128]{2,1,0:T(8,128)S(1)} %invert_own.1.own, f32[2,128,128]{2,1,0:T(8,128)S(1)} %collective-permute-done.got, bf16[112,512]{1,0:T(8,128)(2,1)S(1)} %get-tuple-element.65.pack, ...), custom_call_target="tpu_custom_call" | custom-call | tf_op jit(solution)/shard_map/coarse_level/pallas_call | solution.py:637
  49.1 0.5 collective-permute-start.1
  49.6 1.0 %collective-permute-done.1.got = f32[2,128,128]{2,1,0:T(8,128)S(1)} collective-permute-done((f32[2,128,128]{2,1,0:T(8,128)S(1)}, f32[2,128,128]{2,1,0:T(8,128)S(1)}, u32[]{:S(2)}, u32[]{:S(2)}) %collective-permute-start.1) | collective-permute-done | bytes 131104 | tf_op jit(solution)/shard_map/ppermute | solution.py:572
  50.5 1.1 %spread.1 = (f32[1024,128]{1,0:T(8,128)}, f32[8,128]{1,0:T(8,128)S(1)}) custom-call(f32[2,128,128]{2,1,0:T(8,128)S(1)} %get-tuple-element.66.kept, f32[2,128,128]{2,1,0:T(8,128)S(1)} %collective-permute-done.1.got, bf16[2,512,256]{2,1,0:T(8,128)(2,1)S(1)} %get-tuple-element.68.table), custom_call_target="tpu_custom_call" | custom-call | tf_op jit(solution)/shard_map/spread/pallas_call | solution.py:649
  51.7 3.8 %all-to-all-start.2 = ((f32[128,8,128]{2,1,0:T(8,128)}), f32[128,8,128]{2,1,0:T(8,128)S(1)}, u32[]{:S(2)}, u32[]{:S(2)}) async-start(f32[128,8,128]{2,1,0:T(8,128)} %bitcast.21), calls=%async_computation.2 | async-start | bytes 1048576 | tf_op jit(solution)/shard_map/all_to_all | solution.py:568
  55.6 0.4 copy.33.weights
  55.9 6.7 %bypass.1 = (f32[8,128,512]{2,1,0:T(8,128)}, f32[4,16,16,128]{3,2,1,0:T(8,128)}) custom-call(f32[8,128]{1,0:T(8,128)S(1)} %get-tuple-element.70.after, bf16[8,2,128,512]{3,2,1,0:T(8,128)(2,1)} %get-tuple-element.71.values, bf16[256,512]{1,0:T(8,128)(2,1)} %get-tuple-element.72.wide_mix_h, f32[4,16,16,128]{3,2,1,0:T(8,128)S(1)} %copy-done, ...), custom_call_target="tpu_custom_call" | custom-call | flops 2147483648 | bytes 6291456 | tf_op jit(solution)/shard_map/bypass/pallas_call | solution.py:655
  62.6 7.1 %all-to-all-done.2.arrived = f32[128,8,128]{2,1,0:T(8,128)S(1)} async-done(((f32[128,8,128]{2,1,0:T(8,128)}), f32[128,8,128]{2,1,0:T(8,128)S(1)}, u32[]{:S(2)}, u32[]{:S(2)}) %all-to-all-start.2) | async-done | bytes 524320 | tf_op jit(solution)/shard_map/all_to_all | solution.py:568
  69.7 0.8 second_mix.1
  70.4 17.9 %all_to_all.27 = f32[128,8,128]{2,1,0:T(8,128)S(1)} all-to-all(f32[128,8,128]{2,1,0:T(8,128)S(1)} %second_mix.1), channel_id=1, replica_groups=mesh['gx'=8,'gy'=16] {'gx','gy'}, dimensions={0} | all-to-all | bytes 1048576 | tf_op jit(solution)/shard_map/all_to_all | solution.py:568
  88.3 7.9 %fine_level.1 = f32[4,16,16,128]{3,2,1,0:T(8,128)} custom-call(f32[1024,128]{1,0:T(8,128)S(1)} %bitcast.12, bf16[2,512,512]{2,1,0:T(8,128)(2,1)S(1)} %copy-done.1, bf16[128,64]{1,0:T(8,128)(2,1)} %constant.20.clone.z_back_h, f32[8,128,512]{2,1,0:T(8,128)} %get-tuple-element.77.skip, bf16[128,512]{1,0:T(8,128)(2,1)} %get-tuple-element.78.project_h, ...), custom_call_target="tpu_custom_call" | custom-call | tf_op jit(solution)/shard_map/fine_level/pallas_call | solution.py:677
  (33 shorter events, 0.9 us)
Async XLA Ops:
  3.2 21.2 %all-to-all-start = ((f32[128,1,128]{2,1,0:T(1,128)}), f32[128,1,128]{2,1,0:T(1,128)S(1)}, u32[]{:S(2)}, u32[]{:S(2)}) async-start(f32[128,1,128]{2,1,0:T(1,128)} %bitcast.22), calls=%async_computation | async-start | bytes 131072 | tf_op jit(solution)/shard_map/all_to_all | solution.py:568
  16.2 0.7 copy-start.7
  16.8 13.2 %copy-start.13 = (f32[64,32]{0,1:T(8,128)S(1)}, f32[64,32]{0,1:T(8,128)}, u32[]{:S(2)}) copy-start(f32[64,32]{0,1:T(8,128)} %param.22) | copy-start | bytes 24580
  16.8 13.3 %copy-start.4 = (s32[2,512]{1,0:T(2,128)S(1)}, s32[2,512]{1,0:T(2,128)}, u32[]{:S(2)}) copy-start(s32[2,512]{1,0:T(2,128)} %constant.16.clone.steps_h.steps) | copy-start | bytes 12292
  16.8 13.3 %copy-start.5 = (f32[32]{0:T(128)S(1)}, f32[32]{0:T(128)}, u32[]{:S(2)}) copy-start(f32[32]{0:T(128)} %param.20) | copy-start | bytes 388
  16.8 13.3 %copy-start.6 = (f32[32,64]{1,0:T(8,128)S(1)}, f32[32,64]{1,0:T(8,128)}, u32[]{:S(2)}) copy-start(f32[32,64]{1,0:T(8,128)} %bypass_out.1) | copy-start | bytes 24580
  16.9 13.3 %copy-start.8 = (f32[4,32]{1,0:T(4,128)S(1)}, f32[4,32]{1,0:T(4,128)}, u32[]{:S(2)}) copy-start(f32[4,32]{1,0:T(4,128)} %project.3) | copy-start | bytes 1540
  16.9 13.3 %copy-start.9 = (f32[64]{0:T(128)S(1)}, f32[64]{0:T(128)}, u32[]{:S(2)}) copy-start(f32[64]{0:T(128)} %param.23) | copy-start | bytes 772
  16.9 13.3 %copy-start.10 = (f32[32]{0:T(128)S(1)}, f32[32]{0:T(128)}, u32[]{:S(2)}) copy-start(f32[32]{0:T(128)} %param.26) | copy-start | bytes 388
  16.9 13.3 %copy-start.11 = (f32[4,16,512]{2,1,0:T(8,128)S(1)}, f32[4,16,512]{2,1,0:T(8,128)}, u32[]{:S(2)}) copy-start(f32[4,16,512]{2,1,0:T(8,128)} %constant.17.clone.waves) | copy-start | bytes 393220
  25.8 18.4 %all-to-all-start.1 = ((f32[128,8,128]{2,1,0:T(8,128)}), f32[128,8,128]{2,1,0:T(8,128)S(1)}, u32[]{:S(2)}, u32[]{:S(2)}) async-start(f32[128,8,128]{2,1,0:T(8,128)} %get-tuple-element.52), calls=%async_computation.1 | async-start | bytes 1048576 | tf_op jit(solution)/shard_map/all_to_all | solution.py:568
  44.6 1.7 %copy-start = (f32[4,16,16,128]{3,2,1,0:T(8,128)S(1)}, f32[4,16,16,128]{3,2,1,0:T(8,128)}, u32[]{:S(2)}) copy-start(f32[4,16,16,128]{3,2,1,0:T(8,128)} %fields.5) | copy-start | bytes 1572868
  44.6 1.7 %copy-start.2 = (bf16[64,128]{1,0:T(8,128)(2,1)S(1)}, bf16[64,128]{1,0:T(8,128)(2,1)}, u32[]{:S(2)}) copy-start(bf16[64,128]{1,0:T(8,128)(2,1)} %constant.18.clone.z_back) | copy-start | bytes 49156
  44.6 1.7 %copy-start.3 = (bf16[32,256]{1,0:T(8,128)(2,1)S(1)}, bf16[32,256]{1,0:T(8,128)(2,1)}, u32[]{:S(2)}) copy-start(bf16[32,256]{1,0:T(8,128)(2,1)} %constant.19.clone.z_fwd) | copy-start | bytes 49156
  44.6 1.7 %collective-permute-start = (f32[2,128,128]{2,1,0:T(8,128)S(1)}, f32[2,128,128]{2,1,0:T(8,128)S(1)}, u32[]{:S(2)}, u32[]{:S(2)}) collective-permute-start(f32[2,128,128]{2,1,0:T(8,128)S(1)} %invert_mate.1), channel_id=1, source_target_pairs={{0,16},{16,0},{32,48},{48,32},{64,80},{80,64},{96,112},{112,96},{1... | collective-permute-start | bytes 393224 | tf_op jit(solution)/shard_map/ppermute | solution.py:572
  45.6 9.9 %copy-start.14 = (f32[4]{0:T(128)S(1)}, f32[4]{0:T(128)}, u32[]{:S(2)}) copy-start(f32[4]{0:T(128)} %param.28) | copy-start | bytes 52
  45.6 10.0 %copy-start.12 = (f32[2,2,8,64,32]{3,4,2,1,0:T(8,128)S(1)}, f32[2,2,8,64,32]{3,4,2,1,0:T(8,128)}, u32[]{:S(2)}) copy-start(f32[2,2,8,64,32]{3,4,2,1,0:T(8,128)} %param.24) | copy-start | bytes 786436
  49.1 1.4 %collective-permute-start.1 = (f32[2,128,128]{2,1,0:T(8,128)S(1)}, f32[2,128,128]{2,1,0:T(8,128)S(1)}, u32[]{:S(2)}, u32[]{:S(2)}) collective-permute-start(f32[2,128,128]{2,1,0:T(8,128)S(1)} %get-tuple-element.67), channel_id=1, source_target_pairs={{0,16},{16,0},{32,48},{48,32},{64,80},{80,64},{96,112},{112,96},{1... | collective-permute-start | bytes 393224 | tf_op jit(solution)/shard_map/ppermute | solution.py:572
  51.7 18.0 %all-to-all-start.2 = ((f32[128,8,128]{2,1,0:T(8,128)}), f32[128,8,128]{2,1,0:T(8,128)S(1)}, u32[]{:S(2)}, u32[]{:S(2)}) async-start(f32[128,8,128]{2,1,0:T(8,128)} %bitcast.21), calls=%async_computation.2 | async-start | bytes 1048576 | tf_op jit(solution)/shard_map/all_to_all | solution.py:568
  62.6 25.7 %copy-start.1 = (bf16[2,512,512]{2,1,0:T(8,128)(2,1)S(1)}, bf16[2,512,512]{2,1,0:T(8,128)(2,1)}, u32[]{:S(2)}) copy-start(bf16[2,512,512]{2,1,0:T(8,128)(2,1)} %get-tuple-element.76.table) | copy-start | bytes 3145732

commit v6 on v5

--- a/solution.py
+++ b/solution.py
@@ -19,7 +19,7 @@
 F32 = jnp.float32
 BF16 = jnp.bfloat16
 UNROLL = 8
-FINE_UNROLL = 1
+FINE_GROUP = 4
 VMEM = pl.BlockSpec(memory_space=pltpu.VMEM)
 HBM = pl.BlockSpec(memory_space=pltpu.HBM)
 PARAMS = pltpu.CompilerParams(vmem_limit_bytes=16 << 20)
@@ -96,6 +96,11 @@
     ones = np.zeros((16, NZ), BF16)
     ones[:3] = 1.0
     return np.concatenate([high.T, high.T, low.T, ones], axis=0)
+
+
+def fine_z_table():
+    table = np.kron(np.eye(FINE_GROUP), inverse_z_table().T.astype(np.float32))
+    return table.astype(BF16)
 
 
 def forward_z_table():
@@ -543,23 +548,32 @@
     for copy in small:
         copy.wait()
 
-    def step(p, carry):
-        for copy in taken(p):
-            copy.wait()
-        for x in (2 * p, 2 * p + 1):
+    def step(i, carry):
+        rights = []
+        for u in range(FINE_GROUP):
+            x = FINE_GROUP * i + u
             rows = [rhs_s[t, pl.ds(x, 16, stride=16), :] for t in range(4)]
             high, less = split(jnp.concatenate(rows, axis=1))
-            right = jnp.concatenate([high, less, high, bias_mix[...]], axis=0)
-            before = mm(z_back[...], right)
-            vh, vl = split(gelu(before + skip_v[p]))
-            made = mm(project_mix[...], vh, ((1,), (1,)))
-            made = made[:64] + made[64:] + mm(project_mix[:64], vl, ((1,), (1,)))
+            rights += [high, less, high, bias_mix[...]]
+        before = mm(z_back[...], jnp.concatenate(rights, axis=0))
+        for v in range(FINE_GROUP // 2):
+            p = FINE_GROUP // 2 * i + v
+            for copy in taken(p):
+                copy.wait()
+        skips = [skip_v[FINE_GROUP // 2 * i + u // 2] for u in range(FINE_GROUP)]
+        vh, vl = split(gelu(before + jnp.concatenate(skips, axis=0)))
+        made = mm(project_mix[...], vh, ((1,), (1,)))
+        made = made[:64] + made[64:] + mm(project_mix[:64], vl, ((1,), (1,)))
+        for u in range(FINE_GROUP):
+            x = FINE_GROUP * i + u
             for o in range(CIN):
-                out_v[o, x] = made[16 * o : 16 * o + 16] + base[o, x]
-        given(p).start()
+                piece = made[16 * o : 16 * o + 16, 128 * u : 128 * u + 128]
+                out_v[o, x] = piece + base[o, x]
+        for v in range(FINE_GROUP // 2):
+            given(FINE_GROUP // 2 * i + v).start()
         return carry
 
-    lax.fori_loop(0, 8, step, 0, unroll=FINE_UNROLL)
+    lax.fori_loop(0, 16 // FINE_GROUP, step, 0)
     for p in range(8):
         given(p).wait()
 
@@ -681,12 +695,12 @@
         scratch_shapes=[
             pltpu.VMEM((CIN, 16, 16, NZ), F32), pltpu.VMEM((CIN, 16, 16, NZ), F32),
             pltpu.VMEM((2, 512, 128), F32), pltpu.VMEM((4, 256, 128), F32),
-            pltpu.VMEM((8, NZ, 512), F32), pltpu.VMEM((NZ, 64), BF16),
+            pltpu.VMEM((8, NZ, 512), F32), pltpu.VMEM((NZ * FINE_GROUP, 64 * FINE_GROUP), BF16),
             pltpu.VMEM((128, 512), BF16), pltpu.VMEM((16, 512), BF16), dma((11,)), dma((8,)),
             dma((8,)),
         ],
     )(
-        exchange(mixed).reshape(OWNERS * 8, 128), fine_t, stay(jnp.asarray(z_back.T)), stay(skip),
+        exchange(mixed).reshape(OWNERS * 8, 128), fine_t, stay(jnp.asarray(fine_z_table())), stay(skip),
         stay(project_mix), stay(bias_mix), stay(base),
     )
 

time: 96.6 us -> 94.6 us (0.979)
  Pallas kernels: 29 us -> 27 us
    pallas_call x1, Pallas kernels: 7.92 us -> 5.92 us  [on_device(): call(fine_level, out_shape=shape((CIN, 16, 16, NZ), F32), in_specs=[VMEM,...]
where the time goes in v6:
time: 94.6 us; the launch traced here: 94.2 us
  Pallas kernels  27 us (29%)
  waiting for transfers between devices  25.7 us (27%)
  starting transfers between devices  20.7 us (22%)
  blocking collectives  17.9 us (19%)
  local copies, waits for them, and re-layouts  2.78 us (3%)
    all_to_all x3, waiting for transfers between devices, exchange(): return lax.all_to_all(tiles, AXES, split_axis=0, concat_axis=0, tiled=True)  24 us
    all_to_all x3, starting transfers between devices, exchange(): return lax.all_to_all(tiles, AXES, split_axis=0, concat_axis=0, tiled=True)  19.6 us
    all_to_all x1, blocking collectives, exchange(): return lax.all_to_all(tiles, AXES, split_axis=0, concat_axis=0, tiled=True)  17.9 us
    pallas_call x1, Pallas kernels, on_device(): call(bypass, out_shape=(pltpu.HBM((8, NZ, 512), F32), pltpu.HBM((CIN, 16,...  6.66 us
    pallas_call x1, Pallas kernels, on_device(): call(fine_level, out_shape=shape((CIN, 16, 16, NZ), F32), in_specs=[VMEM,...  5.92 us
    pallas_call x1, Pallas kernels, on_device(): call(prepare, out_shape=(shape((256, 512), BF16), shape((256, 512), BF16)...  3.33 us
    pallas_call x1, Pallas kernels, on_device(): pl.pallas_call(first_spectrum, out_shape=(shape((OWNERS, 128), F32), shap...  3.14 us
    pallas_call x1, Pallas kernels, on_device(): call(coarse_level, out_shape=(shape((2, 128, 128), F32), shape((2, 128, 1...  2.84 us
  transfers between devices with their start and end apart: 5, of which 5 were waited for; matrix products, arithmetic and copies ran while one was open for 2% of the time, Pallas kernels for 12%

profile of v6, /device:TPU:1, one launch (start us, length us, event | category | flops | bytes accessed | tf_op | source)
XLA Modules:
  0.0 94.2 jit_solution(13869620406065398868)
XLA Ops:
  0.0 3.1 %first_spectrum.1 = (f32[128,128]{1,0:T(8,128)}, f32[8,128]{1,0:T(8,128)}) custom-call(f32[4,16,16,128]{3,2,1,0:T(8,128)} %fields.5, bf16[4,384,128]{2,1,0:T(8,128)(2,1)} %constant.14.clone.ztab_h, bf16[2,512,256]{2,1,0:T(8,128)(2,1)} %constant.15.clone.ptab_h, s32[2,512]{1,0:T(2,128)} %constant.16.clone.steps_h.steps), custom_call_target="tpu_custom_call" | custom-call | tf_op jit(solution)/shard_map/first_spectrum/pallas_call | solution.py:603
  3.2 11.5 %all-to-all-start = ((f32[128,1,128]{2,1,0:T(1,128)}), f32[128,1,128]{2,1,0:T(1,128)S(1)}, u32[]{:S(2)}, u32[]{:S(2)}) async-start(f32[128,1,128]{2,1,0:T(1,128)} %bitcast.22), calls=%async_computation | async-start | bytes 131072 | tf_op jit(solution)/shard_map/all_to_all | solution.py:582
  14.7 0.8 copy.27.lift
  15.4 0.7 copy.28.lift_bias
  16.2 0.7 copy-done.7
  16.9 1.1 %prepare_mix.1 = (f32[2,2,8,32,64]{4,3,2,1,0:T(8,128)S(1)}, f32[32,128]{1,0:T(8,128)S(1)}, f32[32,32]{1,0:T(8,128)S(1)}) custom-call(f32[8,128]{1,0:T(8,128)S(1)} %copy-done.7, f32[2,2,8,32,64]{4,3,2,1,0:T(8,128)} %weights.2, f32[32,4]{1,0:T(8,128)S(1)} %copy.27.lift, f32[32,1]{1,0:T(8,128)S(1)} %copy.28.lift_bias), custom_call_target="tpu_custom_call" | custom-call | flops 2147483648 | bytes 6291456 | tf_op jit(solution)/shard_map/prepare_mix/pallas_call | solution.py:613
  18.0 6.3 %all-to-all-done = f32[128,1,128]{2,1,0:T(1,128)S(1)} async-done(((f32[128,1,128]{2,1,0:T(1,128)}), f32[128,1,128]{2,1,0:T(1,128)S(1)}, u32[]{:S(2)}, u32[]{:S(2)}) %all-to-all-start) | async-done | bytes 65568 | tf_op jit(solution)/shard_map/all_to_all | solution.py:582
  24.4 1.4 %first_mix.1 = (f32[128,8,128]{2,1,0:T(8,128)}, f32[8,128]{1,0:T(8,128)S(1)}) custom-call(f32[128,128]{1,0:T(8,128)S(1)} %bitcast.15, f32[32,128]{1,0:T(8,128)S(1)} %get-tuple-element.49.lift_wide, f32[32,32]{1,0:T(8,128)S(1)} %get-tuple-element.50.bias_column, f32[2,2,8,32,64]{4,3,2,1,0:T(8,128)S(1)} %get-tuple-element.51.weights), custom_call_target="tpu_custom_call" | custom-call | tf_op jit(solution)/shard_map/first_mix/pallas_call | solution.py:623
  25.8 4.3 %all-to-all-start.1 = ((f32[128,8,128]{2,1,0:T(8,128)}), f32[128,8,128]{2,1,0:T(8,128)S(1)}, u32[]{:S(2)}, u32[]{:S(2)}) async-start(f32[128,8,128]{2,1,0:T(8,128)} %get-tuple-element.52), calls=%async_computation.1 | async-start | bytes 1048576 | tf_op jit(solution)/shard_map/all_to_all | solution.py:582
  30.2 3.3 %prepare.1 = (bf16[256,512]{1,0:T(8,128)(2,1)S(1)}, bf16[256,512]{1,0:T(8,128)(2,1)S(1)}, bf16[2,512,256]{2,1,0:T(8,128)(2,1)S(1)}, bf16[112,512]{1,0:T(8,128)(2...) custom-call(f32[8,128]{1,0:T(8,128)S(1)} %get-tuple-element.53.after, ...), custom_call_target="tpu_custom_call" | custom-call | flops 2147483648 | bytes 6291456 | tf_op jit(solution)/shard_map/prepare/pallas_call | solution.py:629
  33.6 10.7 %all-to-all-done.1 = f32[128,8,128]{2,1,0:T(8,128)S(1)} async-done(((f32[128,8,128]{2,1,0:T(8,128)}), f32[128,8,128]{2,1,0:T(8,128)S(1)}, u32[]{:S(2)}, u32[]{:S(2)}) %all-to-all-start.1) | async-done | bytes 524320 | tf_op jit(solution)/shard_map/all_to_all | solution.py:582
  44.6 0.7 collective-permute-start
  45.6 0.6 collective-permute-done.got
  46.3 2.8 %coarse_level.1 = (f32[2,128,128]{2,1,0:T(8,128)S(1)}, f32[2,128,128]{2,1,0:T(8,128)S(1)}, bf16[8,2,128,512]{3,2,1,0:T(8,128)(2,1)}) custom-call(f32[2,128,128]{2,1,0:T(8,128)S(1)} %invert_own.1.own, f32[2,128,128]{2,1,0:T(8,128)S(1)} %collective-permute-done.got, bf16[112,512]{1,0:T(8,128)(2,1)S(1)} %get-tuple-element.65.pack, ...), custom_call_target="tpu_custom_call" | custom-call | tf_op jit(solution)/shard_map/coarse_level/pallas_call | solution.py:651
  49.1 0.5 collective-permute-start.1
  49.6 1.0 %collective-permute-done.1.got = f32[2,128,128]{2,1,0:T(8,128)S(1)} collective-permute-done((f32[2,128,128]{2,1,0:T(8,128)S(1)}, f32[2,128,128]{2,1,0:T(8,128)S(1)}, u32[]{:S(2)}, u32[]{:S(2)}) %collective-permute-start.1) | collective-permute-done | bytes 131104 | tf_op jit(solution)/shard_map/ppermute | solution.py:586
  50.5 1.1 %spread.1 = (f32[1024,128]{1,0:T(8,128)}, f32[8,128]{1,0:T(8,128)S(1)}) custom-call(f32[2,128,128]{2,1,0:T(8,128)S(1)} %get-tuple-element.66.kept, f32[2,128,128]{2,1,0:T(8,128)S(1)} %collective-permute-done.1.got, bf16[2,512,256]{2,1,0:T(8,128)(2,1)S(1)} %get-tuple-element.68.table), custom_call_target="tpu_custom_call" | custom-call | tf_op jit(solution)/shard_map/spread/pallas_call | solution.py:663
  51.7 3.8 %all-to-all-start.2 = ((f32[128,8,128]{2,1,0:T(8,128)}), f32[128,8,128]{2,1,0:T(8,128)S(1)}, u32[]{:S(2)}, u32[]{:S(2)}) async-start(f32[128,8,128]{2,1,0:T(8,128)} %bitcast.21), calls=%async_computation.2 | async-start | bytes 1048576 | tf_op jit(solution)/shard_map/all_to_all | solution.py:582
  55.6 0.4 copy.33.weights
  55.9 6.7 %bypass.1 = (f32[8,128,512]{2,1,0:T(8,128)}, f32[4,16,16,128]{3,2,1,0:T(8,128)}) custom-call(f32[8,128]{1,0:T(8,128)S(1)} %get-tuple-element.70.after, bf16[8,2,128,512]{3,2,1,0:T(8,128)(2,1)} %get-tuple-element.71.values, bf16[256,512]{1,0:T(8,128)(2,1)} %get-tuple-element.72.wide_mix_h, f32[4,16,16,128]{3,2,1,0:T(8,128)S(1)} %copy-done, ...), custom_call_target="tpu_custom_call" | custom-call | flops 2147483648 | bytes 6291456 | tf_op jit(solution)/shard_map/bypass/pallas_call | solution.py:669
  62.6 7.1 %all-to-all-done.2.arrived = f32[128,8,128]{2,1,0:T(8,128)S(1)} async-done(((f32[128,8,128]{2,1,0:T(8,128)}), f32[128,8,128]{2,1,0:T(8,128)S(1)}, u32[]{:S(2)}, u32[]{:S(2)}) %all-to-all-start.2) | async-done | bytes 524320 | tf_op jit(solution)/shard_map/all_to_all | solution.py:582
  69.7 0.8 second_mix.1
  70.4 17.9 %all_to_all.27 = f32[128,8,128]{2,1,0:T(8,128)S(1)} all-to-all(f32[128,8,128]{2,1,0:T(8,128)S(1)} %second_mix.1), channel_id=1, replica_groups=mesh['gx'=8,'gy'=16] {'gx','gy'}, dimensions={0} | all-to-all | bytes 1048576 | tf_op jit(solution)/shard_map/all_to_all | solution.py:582
  88.3 5.9 %fine_level.1 = f32[4,16,16,128]{3,2,1,0:T(8,128)} custom-call(f32[1024,128]{1,0:T(8,128)S(1)} %bitcast.12, bf16[2,512,512]{2,1,0:T(8,128)(2,1)S(1)} %copy-done.1, bf16[512,256]{1,0:T(8,128)(2,1)} %constant.20.clone.z_back_h, f32[8,128,512]{2,1,0:T(8,128)} %get-tuple-element.77.skip, bf16[128,512]{1,0:T(8,128)(2,1)} %get-tuple-element.78.project_h, ...), custom_call_target="tpu_custom_call" | custom-call | tf_op jit(solution)/shard_map/fine_level/pallas_call | solution.py:691
  (33 shorter events, 0.9 us)
Async XLA Ops:
  3.2 21.2 %all-to-all-start = ((f32[128,1,128]{2,1,0:T(1,128)}), f32[128,1,128]{2,1,0:T(1,128)S(1)}, u32[]{:S(2)}, u32[]{:S(2)}) async-start(f32[128,1,128]{2,1,0:T(1,128)} %bitcast.22), calls=%async_computation | async-start | bytes 131072 | tf_op jit(solution)/shard_map/all_to_all | solution.py:582
  16.2 0.7 copy-start.7
  16.8 13.2 %copy-start.13 = (f32[64,32]{0,1:T(8,128)S(1)}, f32[64,32]{0,1:T(8,128)}, u32[]{:S(2)}) copy-start(f32[64,32]{0,1:T(8,128)} %param.22) | copy-start | bytes 24580
  16.8 13.3 %copy-start.4 = (s32[2,512]{1,0:T(2,128)S(1)}, s32[2,512]{1,0:T(2,128)}, u32[]{:S(2)}) copy-start(s32[2,512]{1,0:T(2,128)} %constant.16.clone.steps_h.steps) | copy-start | bytes 12292
  16.8 13.3 %copy-start.5 = (f32[32]{0:T(128)S(1)}, f32[32]{0:T(128)}, u32[]{:S(2)}) copy-start(f32[32]{0:T(128)} %param.20) | copy-start | bytes 388
  16.8 13.3 %copy-start.6 = (f32[32,64]{1,0:T(8,128)S(1)}, f32[32,64]{1,0:T(8,128)}, u32[]{:S(2)}) copy-start(f32[32,64]{1,0:T(8,128)} %bypass_out.1) | copy-start | bytes 24580
  16.9 13.3 %copy-start.8 = (f32[4,32]{1,0:T(4,128)S(1)}, f32[4,32]{1,0:T(4,128)}, u32[]{:S(2)}) copy-start(f32[4,32]{1,0:T(4,128)} %project.3) | copy-start | bytes 1540
  16.9 13.3 %copy-start.9 = (f32[64]{0:T(128)S(1)}, f32[64]{0:T(128)}, u32[]{:S(2)}) copy-start(f32[64]{0:T(128)} %param.23) | copy-start | bytes 772
  16.9 13.3 %copy-start.10 = (f32[32]{0:T(128)S(1)}, f32[32]{0:T(128)}, u32[]{:S(2)}) copy-start(f32[32]{0:T(128)} %param.26) | copy-start | bytes 388
  16.9 13.3 %copy-start.11 = (f32[4,16,512]{2,1,0:T(8,128)S(1)}, f32[4,16,512]{2,1,0:T(8,128)}, u32[]{:S(2)}) copy-start(f32[4,16,512]{2,1,0:T(8,128)} %constant.17.clone.waves) | copy-start | bytes 393220
  25.8 18.4 %all-to-all-start.1 = ((f32[128,8,128]{2,1,0:T(8,128)}), f32[128,8,128]{2,1,0:T(8,128)S(1)}, u32[]{:S(2)}, u32[]{:S(2)}) async-start(f32[128,8,128]{2,1,0:T(8,128)} %get-tuple-element.52), calls=%async_computation.1 | async-start | bytes 1048576 | tf_op jit(solution)/shard_map/all_to_all | solution.py:582
  44.6 1.7 %copy-start = (f32[4,16,16,128]{3,2,1,0:T(8,128)S(1)}, f32[4,16,16,128]{3,2,1,0:T(8,128)}, u32[]{:S(2)}) copy-start(f32[4,16,16,128]{3,2,1,0:T(8,128)} %fields.5) | copy-start | bytes 1572868
  44.6 1.7 %copy-start.2 = (bf16[64,128]{1,0:T(8,128)(2,1)S(1)}, bf16[64,128]{1,0:T(8,128)(2,1)}, u32[]{:S(2)}) copy-start(bf16[64,128]{1,0:T(8,128)(2,1)} %constant.18.clone.z_back) | copy-start | bytes 49156
  44.6 1.7 %copy-start.3 = (bf16[32,256]{1,0:T(8,128)(2,1)S(1)}, bf16[32,256]{1,0:T(8,128)(2,1)}, u32[]{:S(2)}) copy-start(bf16[32,256]{1,0:T(8,128)(2,1)} %constant.19.clone.z_fwd) | copy-start | bytes 49156
  44.6 1.7 %collective-permute-start = (f32[2,128,128]{2,1,0:T(8,128)S(1)}, f32[2,128,128]{2,1,0:T(8,128)S(1)}, u32[]{:S(2)}, u32[]{:S(2)}) collective-permute-start(f32[2,128,128]{2,1,0:T(8,128)S(1)} %invert_mate.1), channel_id=1, source_target_pairs={{0,16},{16,0},{32,48},{48,32},{64,80},{80,64},{96,112},{112,96},{1... | collective-permute-start | bytes 393224 | tf_op jit(solution)/shard_map/ppermute | solution.py:586
  45.6 9.9 %copy-start.14 = (f32[4]{0:T(128)S(1)}, f32[4]{0:T(128)}, u32[]{:S(2)}) copy-start(f32[4]{0:T(128)} %param.28) | copy-start | bytes 52
  45.6 10.0 %copy-start.12 = (f32[2,2,8,64,32]{3,4,2,1,0:T(8,128)S(1)}, f32[2,2,8,64,32]{3,4,2,1,0:T(8,128)}, u32[]{:S(2)}) copy-start(f32[2,2,8,64,32]{3,4,2,1,0:T(8,128)} %param.24) | copy-start | bytes 786436
  49.1 1.4 %collective-permute-start.1 = (f32[2,128,128]{2,1,0:T(8,128)S(1)}, f32[2,128,128]{2,1,0:T(8,128)S(1)}, u32[]{:S(2)}, u32[]{:S(2)}) collective-permute-start(f32[2,128,128]{2,1,0:T(8,128)S(1)} %get-tuple-element.67), channel_id=1, source_target_pairs={{0,16},{16,0},{32,48},{48,32},{64,80},{80,64},{96,112},{112,96},{1... | collective-permute-start | bytes 393224 | tf_op jit(solution)/shard_map/ppermute | solution.py:586
  51.7 18.0 %all-to-all-start.2 = ((f32[128,8,128]{2,1,0:T(8,128)}), f32[128,8,128]{2,1,0:T(8,128)S(1)}, u32[]{:S(2)}, u32[]{:S(2)}) async-start(f32[128,8,128]{2,1,0:T(8,128)} %bitcast.21), calls=%async_computation.2 | async-start | bytes 1048576 | tf_op jit(solution)/shard_map/all_to_all | solution.py:582
  62.6 25.7 %copy-start.1 = (bf16[2,512,512]{2,1,0:T(8,128)(2,1)S(1)}, bf16[2,512,512]{2,1,0:T(8,128)(2,1)}, u32[]{:S(2)}) copy-start(bf16[2,512,512]{2,1,0:T(8,128)(2,1)} %get-tuple-element.76.table) | copy-start | bytes 3145732

commit v7 on v6

--- a/solution.py
+++ b/solution.py
@@ -19,7 +19,7 @@
 F32 = jnp.float32
 BF16 = jnp.bfloat16
 UNROLL = 8
-FINE_GROUP = 4
+FINE_GROUP = 16
 VMEM = pl.BlockSpec(memory_space=pltpu.VMEM)
 HBM = pl.BlockSpec(memory_space=pltpu.HBM)
 PARAMS = pltpu.CompilerParams(vmem_limit_bytes=16 << 20)
@@ -71,12 +71,9 @@
 
 def first_z_table():
     c, s = np.cos(z_angles()), np.sin(z_angles())
-    parts = np.array([[c, -s], [-s, -c]])
-    table = np.zeros((CIN, NZ, 2, 2, KZ, CIN))
-    for ch in range(CIN):
-        table[ch, :, :, :, :, ch] = parts.transpose(2, 0, 1, 3)
-    high, low = split_np(table.reshape(CIN, NZ, 128).astype(np.float32))
-    return np.concatenate([high, high, low], axis=1)
+    parts = np.array([[c, -s], [-s, -c]]).transpose(2, 0, 1, 3).reshape(NZ, 32)
+    high, low = split_np(np.repeat(parts, CIN, axis=1).astype(np.float32))
+    return np.concatenate([high, high, low], axis=0)
 
 
 def first_places_table():
@@ -99,7 +96,7 @@
 
 
 def fine_z_table():
-    table = np.kron(np.eye(FINE_GROUP), inverse_z_table().T.astype(np.float32))
+    table = np.kron(np.eye(4), inverse_z_table().T.astype(np.float32))
     return table.astype(BF16)
 
 
@@ -189,9 +186,8 @@
 def first_spectrum(
     fields, ztab_h, ptab_h, steps_h, out, token, fields_v, ztab, ptab, steps, sems,
 ):
-    pairs = [(steps_h, steps)]
-    for ch in range(CIN):
-        pairs += [(fields.at[ch], fields_v.at[ch]), (ztab_h.at[ch], ztab.at[ch])]
+    pairs = [(steps_h, steps), (ztab_h, ztab)]
+    pairs += [(fields.at[ch], fields_v.at[ch]) for ch in range(CIN)]
     pairs.append((ptab_h, ptab))
     copies = [
         pltpu.make_async_copy(source, target, sems.at[i])
@@ -203,16 +199,18 @@
     cos, sin = phases(steps, my_place())
     turn = [v[:, at : at + 128] for at in (0, 256) for v in (cos, sin)]
     turn = jnp.concatenate(turn + [jnp.zeros((124, 128), F32)], axis=0).T
-    total = None
+    channel = iota((256, 128), 1) % CIN
+    total = jnp.zeros((256, 128), F32)
+    copies[1].wait()
     for ch in range(CIN):
-        copies[1 + 2 * ch].wait()
-        copies[2 + 2 * ch].wait()
+        copies[2 + ch].wait()
         fh, fl = split(fields_v[ch].reshape(256, NZ))
-        term = mm(jnp.concatenate([fh, fl], axis=1), ztab[ch, :256]) + mm(fh, ztab[ch, 256:])
-        total = term if total is None else total + term
+        term = mm(jnp.concatenate([fh, fl], axis=1), ztab[:256]) + mm(fh, ztab[256:])
+        total = jnp.where(channel == ch, term, total)
     copies[-1].wait()
     th, tl = split(total)
-    both = mm(ptab[0], th) + mm(ptab[0], tl) + mm(ptab[1], th)
+    both = mm(ptab[0], jnp.concatenate([th, tl], axis=1))
+    both = both[:, :128] + both[:, 128:] + mm(ptab[1], th)
     low = iota((128, 128), 1) < 64
     rows = []
     for s in range(2):
@@ -324,17 +322,21 @@
 
     lax.fori_loop(0, 16, step, 0)
 
-    def wide_step(p, carry):
-        taken(p).wait()
+    for group in range(0, 8, 4):
+        ps = range(group, group + 4)
+        for p in ps:
+            taken(p).wait()
         for q in range(2):
             at = slice(256 * q, 256 * q + 256)
-            high, less = values_v[p, 0, :, at], values_v[p, 1, :, at]
+            high, less = [
+                jnp.concatenate([values_v[p, i, :, at] for p in ps], axis=0) for i in range(2)
+            ]
             wide = mm(high, wide_mix[:, :256]) + mm(high, wide_mix[:, 256:])
-            skip_v[p, :, at] = wide + mm(less, wide_mix[:, :256])
-        given(p).start()
-        return carry
-
-    lax.fori_loop(0, 8, wide_step, 0, unroll=2)
+            wide += mm(less, wide_mix[:, :256])
+            for u, p in enumerate(ps):
+                skip_v[p, :, at] = wide[128 * u : 128 * u + 128]
+        for p in ps:
+            given(p).start()
     for p in range(8):
         given(p).wait()
 
@@ -555,7 +557,13 @@
             rows = [rhs_s[t, pl.ds(x, 16, stride=16), :] for t in range(4)]
             high, less = split(jnp.concatenate(rows, axis=1))
             rights += [high, less, high, bias_mix[...]]
-        before = mm(z_back[...], jnp.concatenate(rights, axis=0))
+        before = jnp.concatenate(
+            [
+                mm(z_back[...], jnp.concatenate(rights[at : at + 16], axis=0))
+                for at in range(0, 4 * FINE_GROUP, 16)
+            ],
+            axis=0,
+        )
         for v in range(FINE_GROUP // 2):
             p = FINE_GROUP // 2 * i + v
             for copy in taken(p):
@@ -605,8 +613,8 @@
         out_shape=(shape((OWNERS, 128), F32), shape((8, 128), F32)),
         in_specs=[HBM] * 4, out_specs=(VMEM, VMEM),
         scratch_shapes=[
-            pltpu.VMEM((CIN, 16, 16, NZ), F32), pltpu.VMEM((CIN, 384, 128), BF16),
-            pltpu.VMEM((2, 512, 256), BF16), pltpu.VMEM((2, 512), jnp.int32), dma((10,)),
+            pltpu.VMEM((CIN, 16, 16, NZ), F32), pltpu.VMEM((384, 128), BF16),
+            pltpu.VMEM((2, 512, 256), BF16), pltpu.VMEM((2, 512), jnp.int32), dma((7,)),
         ],
         name="first_spectrum", compiler_params=ALONE,
     )(fields, first_z_table(), first_places_table(), steps)
@@ -688,14 +696,14 @@
         out_shape=shape((OWNERS, 8, 128), F32),
         in_specs=[VMEM, VMEM], out_specs=VMEM, name="second_mix",
     )(arrived, spectral_out)
-    return call(
-        fine_level,
+    return pl.pallas_call(
+        fine_level, compiler_params=pltpu.CompilerParams(vmem_limit_bytes=32 << 20),
         out_shape=shape((CIN, 16, 16, NZ), F32),
         in_specs=[VMEM, VMEM] + [HBM] * 5, out_specs=HBM, name="fine_level",
         scratch_shapes=[
             pltpu.VMEM((CIN, 16, 16, NZ), F32), pltpu.VMEM((CIN, 16, 16, NZ), F32),
             pltpu.VMEM((2, 512, 128), F32), pltpu.VMEM((4, 256, 128), F32),
-            pltpu.VMEM((8, NZ, 512), F32), pltpu.VMEM((NZ * FINE_GROUP, 64 * FINE_GROUP), BF16),
+            pltpu.VMEM((8, NZ, 512), F32), pltpu.VMEM((4 * NZ, 256), BF16),
             pltpu.VMEM((128, 512), BF16), pltpu.VMEM((16, 512), BF16), dma((11,)), dma((8,)),
             dma((8,)),
         ],

time: 94.6 us -> 94.1 us (level)
  Pallas kernels: 27 us -> 25.5 us
  transfers between devices with their start and end apart: 5 -> 5, of which waited for: 5 -> 5; matrix products, arithmetic and copies ran while one was open for 2% -> 2% of each run, Pallas kernels for 12% -> 11%
where the time goes in v7:
time: 94.1 us; the launch traced here: 93.7 us
  waiting for transfers between devices  26.4 us (28%)
  Pallas kernels  25.5 us (27%)
  starting transfers between devices  20.7 us (22%)
  blocking collectives  17.9 us (19%)
  local copies, waits for them, and re-layouts  2.78 us (3%)
    all_to_all x3, waiting for transfers between devices, exchange(): return lax.all_to_all(tiles, AXES, split_axis=0, concat_axis=0, tiled=True)  24.8 us
    all_to_all x3, starting transfers between devices, exchange(): return lax.all_to_all(tiles, AXES, split_axis=0, concat_axis=0, tiled=True)  19.6 us
    all_to_all x1, blocking collectives, exchange(): return lax.all_to_all(tiles, AXES, split_axis=0, concat_axis=0, tiled=True)  17.9 us
    pallas_call x1, Pallas kernels, on_device(): call(bypass, out_shape=(pltpu.HBM((8, NZ, 512), F32), pltpu.HBM((CIN, 16,...  5.91 us
    pallas_call x1, Pallas kernels, on_device(): pl.pallas_call(fine_level, compiler_params=pltpu.CompilerParams(vmem_limi...  5.2 us
    pallas_call x1, Pallas kernels, on_device(): call(prepare, out_shape=(shape((256, 512), BF16), shape((256, 512), BF16)...  3.33 us
    pallas_call x1, Pallas kernels, on_device(): pl.pallas_call(first_spectrum, out_shape=(shape((OWNERS, 128), F32), shap...  3.12 us
    pallas_call x1, Pallas kernels, on_device(): call(coarse_level, out_shape=(shape((2, 128, 128), F32), shape((2, 128, 1...  2.84 us
  transfers between devices with their start and end apart: 5, of which 5 were waited for; matrix products, arithmetic and copies ran while one was open for 2% of the time, Pallas kernels for 11%

profile of v7, /device:TPU:1, one launch (start us, length us, event | category | flops | bytes accessed | tf_op | source)
XLA Modules:
  0.0 93.7 jit_solution(10219653417365582180)
XLA Ops:
  0.0 3.1 %first_spectrum.1 = (f32[128,128]{1,0:T(8,128)}, f32[8,128]{1,0:T(8,128)}) custom-call(f32[4,16,16,128]{3,2,1,0:T(8,128)} %fields.5, bf16[384,128]{1,0:T(8,128)(2,1)} %constant.14.clone.ztab_h, bf16[2,512,256]{2,1,0:T(8,128)(2,1)} %constant.15.clone.ptab_h, s32[2,512]{1,0:T(2,128)} %constant.16.clone.steps_h.steps), custom_call_target="tpu_custom_call" | custom-call | tf_op jit(solution)/shard_map/first_spectrum/pallas_call | solution.py:611
  3.1 11.5 %all-to-all-start = ((f32[128,1,128]{2,1,0:T(1,128)}), f32[128,1,128]{2,1,0:T(1,128)S(1)}, u32[]{:S(2)}, u32[]{:S(2)}) async-start(f32[128,1,128]{2,1,0:T(1,128)} %bitcast.22), calls=%async_computation | async-start | bytes 131072 | tf_op jit(solution)/shard_map/all_to_all | solution.py:590
  14.6 0.8 copy.27.lift
  15.4 0.7 copy.28.lift_bias
  16.1 0.7 copy-done.7
  16.9 1.1 %prepare_mix.1 = (f32[2,2,8,32,64]{4,3,2,1,0:T(8,128)S(1)}, f32[32,128]{1,0:T(8,128)S(1)}, f32[32,32]{1,0:T(8,128)S(1)}) custom-call(f32[8,128]{1,0:T(8,128)S(1)} %copy-done.7, f32[2,2,8,32,64]{4,3,2,1,0:T(8,128)} %weights.2, f32[32,4]{1,0:T(8,128)S(1)} %copy.27.lift, f32[32,1]{1,0:T(8,128)S(1)} %copy.28.lift_bias), custom_call_target="tpu_custom_call" | custom-call | flops 2147483648 | bytes 6291456 | tf_op jit(solution)/shard_map/prepare_mix/pallas_call | solution.py:621
  18.0 6.3 %all-to-all-done = f32[128,1,128]{2,1,0:T(1,128)S(1)} async-done(((f32[128,1,128]{2,1,0:T(1,128)}), f32[128,1,128]{2,1,0:T(1,128)S(1)}, u32[]{:S(2)}, u32[]{:S(2)}) %all-to-all-start) | async-done | bytes 65568 | tf_op jit(solution)/shard_map/all_to_all | solution.py:590
  24.3 1.4 %first_mix.1 = (f32[128,8,128]{2,1,0:T(8,128)}, f32[8,128]{1,0:T(8,128)S(1)}) custom-call(f32[128,128]{1,0:T(8,128)S(1)} %bitcast.15, f32[32,128]{1,0:T(8,128)S(1)} %get-tuple-element.49.lift_wide, f32[32,32]{1,0:T(8,128)S(1)} %get-tuple-element.50.bias_column, f32[2,2,8,32,64]{4,3,2,1,0:T(8,128)S(1)} %get-tuple-element.51.weights), custom_call_target="tpu_custom_call" | custom-call | tf_op jit(solution)/shard_map/first_mix/pallas_call | solution.py:631
  25.8 4.3 %all-to-all-start.1 = ((f32[128,8,128]{2,1,0:T(8,128)}), f32[128,8,128]{2,1,0:T(8,128)S(1)}, u32[]{:S(2)}, u32[]{:S(2)}) async-start(f32[128,8,128]{2,1,0:T(8,128)} %get-tuple-element.52), calls=%async_computation.1 | async-start | bytes 1048576 | tf_op jit(solution)/shard_map/all_to_all | solution.py:590
  30.2 3.3 %prepare.1 = (bf16[256,512]{1,0:T(8,128)(2,1)S(1)}, bf16[256,512]{1,0:T(8,128)(2,1)S(1)}, bf16[2,512,256]{2,1,0:T(8,128)(2,1)S(1)}, bf16[112,512]{1,0:T(8,128)(2...) custom-call(f32[8,128]{1,0:T(8,128)S(1)} %get-tuple-element.53.after, ...), custom_call_target="tpu_custom_call" | custom-call | flops 2147483648 | bytes 6291456 | tf_op jit(solution)/shard_map/prepare/pallas_call | solution.py:637
  33.5 10.6 %all-to-all-done.1 = f32[128,8,128]{2,1,0:T(8,128)S(1)} async-done(((f32[128,8,128]{2,1,0:T(8,128)}), f32[128,8,128]{2,1,0:T(8,128)S(1)}, u32[]{:S(2)}, u32[]{:S(2)}) %all-to-all-start.1) | async-done | bytes 524320 | tf_op jit(solution)/shard_map/all_to_all | solution.py:590
  44.6 0.7 collective-permute-start
  45.6 0.6 collective-permute-done.got
  46.2 2.8 %coarse_level.1 = (f32[2,128,128]{2,1,0:T(8,128)S(1)}, f32[2,128,128]{2,1,0:T(8,128)S(1)}, bf16[8,2,128,512]{3,2,1,0:T(8,128)(2,1)}) custom-call(f32[2,128,128]{2,1,0:T(8,128)S(1)} %invert_own.1.own, f32[2,128,128]{2,1,0:T(8,128)S(1)} %collective-permute-done.got, bf16[112,512]{1,0:T(8,128)(2,1)S(1)} %get-tuple-element.65.pack, ...), custom_call_target="tpu_custom_call" | custom-call | tf_op jit(solution)/shard_map/coarse_level/pallas_call | solution.py:659
  49.1 0.4 collective-permute-start.1
  49.5 1.0 %collective-permute-done.1.got = f32[2,128,128]{2,1,0:T(8,128)S(1)} collective-permute-done((f32[2,128,128]{2,1,0:T(8,128)S(1)}, f32[2,128,128]{2,1,0:T(8,128)S(1)}, u32[]{:S(2)}, u32[]{:S(2)}) %collective-permute-start.1) | collective-permute-done | bytes 131104 | tf_op jit(solution)/shard_map/ppermute | solution.py:594
  50.5 1.1 %spread.1 = (f32[1024,128]{1,0:T(8,128)}, f32[8,128]{1,0:T(8,128)S(1)}) custom-call(f32[2,128,128]{2,1,0:T(8,128)S(1)} %get-tuple-element.66.kept, f32[2,128,128]{2,1,0:T(8,128)S(1)} %collective-permute-done.1.got, bf16[2,512,256]{2,1,0:T(8,128)(2,1)S(1)} %get-tuple-element.68.table), custom_call_target="tpu_custom_call" | custom-call | tf_op jit(solution)/shard_map/spread/pallas_call | solution.py:671
  51.6 3.8 %all-to-all-start.2 = ((f32[128,8,128]{2,1,0:T(8,128)}), f32[128,8,128]{2,1,0:T(8,128)S(1)}, u32[]{:S(2)}, u32[]{:S(2)}) async-start(f32[128,8,128]{2,1,0:T(8,128)} %bitcast.21), calls=%async_computation.2 | async-start | bytes 1048576 | tf_op jit(solution)/shard_map/all_to_all | solution.py:590
  55.5 0.4 copy.33.weights
  55.9 5.9 %bypass.1 = (f32[8,128,512]{2,1,0:T(8,128)}, f32[4,16,16,128]{3,2,1,0:T(8,128)}) custom-call(f32[8,128]{1,0:T(8,128)S(1)} %get-tuple-element.70.after, bf16[8,2,128,512]{3,2,1,0:T(8,128)(2,1)} %get-tuple-element.71.values, bf16[256,512]{1,0:T(8,128)(2,1)} %get-tuple-element.72.wide_mix_h, f32[4,16,16,128]{3,2,1,0:T(8,128)S(1)} %copy-done, ...), custom_call_target="tpu_custom_call" | custom-call | flops 2147483648 | bytes 6291456 | tf_op jit(solution)/shard_map/bypass/pallas_call | solution.py:677
  61.8 7.8 %all-to-all-done.2.arrived = f32[128,8,128]{2,1,0:T(8,128)S(1)} async-done(((f32[128,8,128]{2,1,0:T(8,128)}), f32[128,8,128]{2,1,0:T(8,128)S(1)}, u32[]{:S(2)}, u32[]{:S(2)}) %all-to-all-start.2) | async-done | bytes 524320 | tf_op jit(solution)/shard_map/all_to_all | solution.py:590
  69.7 0.8 second_mix.1
  70.4 17.9 %all_to_all.27 = f32[128,8,128]{2,1,0:T(8,128)S(1)} all-to-all(f32[128,8,128]{2,1,0:T(8,128)S(1)} %second_mix.1), channel_id=1, replica_groups=mesh['gx'=8,'gy'=16] {'gx','gy'}, dimensions={0} | all-to-all | bytes 1048576 | tf_op jit(solution)/shard_map/all_to_all | solution.py:590
  88.3 5.2 %fine_level.1 = f32[4,16,16,128]{3,2,1,0:T(8,128)} custom-call(f32[1024,128]{1,0:T(8,128)S(1)} %bitcast.12, bf16[2,512,512]{2,1,0:T(8,128)(2,1)S(1)} %copy-done.1, bf16[512,256]{1,0:T(8,128)(2,1)} %constant.20.clone.z_back_h, f32[8,128,512]{2,1,0:T(8,128)} %get-tuple-element.77.skip, bf16[128,512]{1,0:T(8,128)(2,1)} %get-tuple-element.78.project_h, ...), custom_call_target="tpu_custom_call" | custom-call | tf_op jit(solution)/shard_map/fine_level/pallas_call | solution.py:699
  (33 shorter events, 0.9 us)
Async XLA Ops:
  3.1 21.2 %all-to-all-start = ((f32[128,1,128]{2,1,0:T(1,128)}), f32[128,1,128]{2,1,0:T(1,128)S(1)}, u32[]{:S(2)}, u32[]{:S(2)}) async-start(f32[128,1,128]{2,1,0:T(1,128)} %bitcast.22), calls=%async_computation | async-start | bytes 131072 | tf_op jit(solution)/shard_map/all_to_all | solution.py:590
  16.1 0.7 copy-start.7
  16.8 13.2 %copy-start.13 = (f32[64,32]{0,1:T(8,128)S(1)}, f32[64,32]{0,1:T(8,128)}, u32[]{:S(2)}) copy-start(f32[64,32]{0,1:T(8,128)} %param.22) | copy-start | bytes 24580
  16.8 13.3 %copy-start.4 = (s32[2,512]{1,0:T(2,128)S(1)}, s32[2,512]{1,0:T(2,128)}, u32[]{:S(2)}) copy-start(s32[2,512]{1,0:T(2,128)} %constant.16.clone.steps_h.steps) | copy-start | bytes 12292
  16.8 13.3 %copy-start.5 = (f32[32]{0:T(128)S(1)}, f32[32]{0:T(128)}, u32[]{:S(2)}) copy-start(f32[32]{0:T(128)} %param.20) | copy-start | bytes 388
  16.8 13.3 %copy-start.6 = (f32[32,64]{1,0:T(8,128)S(1)}, f32[32,64]{1,0:T(8,128)}, u32[]{:S(2)}) copy-start(f32[32,64]{1,0:T(8,128)} %bypass_out.1) | copy-start | bytes 24580
  16.8 13.3 %copy-start.8 = (f32[4,32]{1,0:T(4,128)S(1)}, f32[4,32]{1,0:T(4,128)}, u32[]{:S(2)}) copy-start(f32[4,32]{1,0:T(4,128)} %project.3) | copy-start | bytes 1540
  16.8 13.3 %copy-start.9 = (f32[64]{0:T(128)S(1)}, f32[64]{0:T(128)}, u32[]{:S(2)}) copy-start(f32[64]{0:T(128)} %param.23) | copy-start | bytes 772
  16.9 13.3 %copy-start.10 = (f32[32]{0:T(128)S(1)}, f32[32]{0:T(128)}, u32[]{:S(2)}) copy-start(f32[32]{0:T(128)} %param.26) | copy-start | bytes 388
  16.9 13.3 %copy-start.11 = (f32[4,16,512]{2,1,0:T(8,128)S(1)}, f32[4,16,512]{2,1,0:T(8,128)}, u32[]{:S(2)}) copy-start(f32[4,16,512]{2,1,0:T(8,128)} %constant.17.clone.waves) | copy-start | bytes 393220
  25.8 18.4 %all-to-all-start.1 = ((f32[128,8,128]{2,1,0:T(8,128)}), f32[128,8,128]{2,1,0:T(8,128)S(1)}, u32[]{:S(2)}, u32[]{:S(2)}) async-start(f32[128,8,128]{2,1,0:T(8,128)} %get-tuple-element.52), calls=%async_computation.1 | async-start | bytes 1048576 | tf_op jit(solution)/shard_map/all_to_all | solution.py:590
  44.5 1.7 %copy-start = (f32[4,16,16,128]{3,2,1,0:T(8,128)S(1)}, f32[4,16,16,128]{3,2,1,0:T(8,128)}, u32[]{:S(2)}) copy-start(f32[4,16,16,128]{3,2,1,0:T(8,128)} %fields.5) | copy-start | bytes 1572868
  44.5 1.7 %copy-start.2 = (bf16[64,128]{1,0:T(8,128)(2,1)S(1)}, bf16[64,128]{1,0:T(8,128)(2,1)}, u32[]{:S(2)}) copy-start(bf16[64,128]{1,0:T(8,128)(2,1)} %constant.18.clone.z_back) | copy-start | bytes 49156
  44.6 1.7 %copy-start.3 = (bf16[32,256]{1,0:T(8,128)(2,1)S(1)}, bf16[32,256]{1,0:T(8,128)(2,1)}, u32[]{:S(2)}) copy-start(bf16[32,256]{1,0:T(8,128)(2,1)} %constant.19.clone.z_fwd) | copy-start | bytes 49156
  44.6 1.7 %collective-permute-start = (f32[2,128,128]{2,1,0:T(8,128)S(1)}, f32[2,128,128]{2,1,0:T(8,128)S(1)}, u32[]{:S(2)}, u32[]{:S(2)}) collective-permute-start(f32[2,128,128]{2,1,0:T(8,128)S(1)} %invert_mate.1), channel_id=1, source_target_pairs={{0,16},{16,0},{32,48},{48,32},{64,80},{80,64},{96,112},{112,96},{1... | collective-permute-start | bytes 393224 | tf_op jit(solution)/shard_map/ppermute | solution.py:594
  45.6 9.9 %copy-start.14 = (f32[4]{0:T(128)S(1)}, f32[4]{0:T(128)}, u32[]{:S(2)}) copy-start(f32[4]{0:T(128)} %param.28) | copy-start | bytes 52
  45.6 10.0 %copy-start.12 = (f32[2,2,8,64,32]{3,4,2,1,0:T(8,128)S(1)}, f32[2,2,8,64,32]{3,4,2,1,0:T(8,128)}, u32[]{:S(2)}) copy-start(f32[2,2,8,64,32]{3,4,2,1,0:T(8,128)} %param.24) | copy-start | bytes 786436
  49.1 1.4 %collective-permute-start.1 = (f32[2,128,128]{2,1,0:T(8,128)S(1)}, f32[2,128,128]{2,1,0:T(8,128)S(1)}, u32[]{:S(2)}, u32[]{:S(2)}) collective-permute-start(f32[2,128,128]{2,1,0:T(8,128)S(1)} %get-tuple-element.67), channel_id=1, source_target_pairs={{0,16},{16,0},{32,48},{48,32},{64,80},{80,64},{96,112},{112,96},{1... | collective-permute-start | bytes 393224 | tf_op jit(solution)/shard_map/ppermute | solution.py:594
  51.6 18.0 %all-to-all-start.2 = ((f32[128,8,128]{2,1,0:T(8,128)}), f32[128,8,128]{2,1,0:T(8,128)S(1)}, u32[]{:S(2)}, u32[]{:S(2)}) async-start(f32[128,8,128]{2,1,0:T(8,128)} %bitcast.21), calls=%async_computation.2 | async-start | bytes 1048576 | tf_op jit(solution)/shard_map/all_to_all | solution.py:590
  61.8 26.5 %copy-start.1 = (bf16[2,512,512]{2,1,0:T(8,128)(2,1)S(1)}, bf16[2,512,512]{2,1,0:T(8,128)(2,1)}, u32[]{:S(2)}) copy-start(bf16[2,512,512]{2,1,0:T(8,128)(2,1)} %get-tuple-element.76.table) | copy-start | bytes 3145732

commit v8 on v7

--- a/solution.py
+++ b/solution.py
@@ -12,7 +12,8 @@
 KX, KY, KZ = 16, 16, 8
 NX, NY, NZ = 128, 256, 128
 CIN, C1, C2 = 4, 32, 64
-AXES = ("gx", "gy")
+AXES = ("x", "core", "gy")
+CHIPS = ("x", "gy")
 OWNERS = 128
 TOTAL = NX * NY * NZ
 BACK = math.sqrt(2.0 / (KX * KY * KZ))
@@ -162,13 +163,17 @@
 
 
 def my_place():
-    return lax.axis_index("gx"), lax.axis_index("gy")
+    return 2 * lax.axis_index("x") + lax.axis_index("core"), lax.axis_index("gy")
 
 
 def phases(steps, place):
     turns = (steps[0:1] * place[0] + steps[1:2] * place[1]) & 15
-    angle = turns.astype(F32) * (2.0 * math.pi / 16)
-    return jnp.cos(angle), jnp.sin(angle)
+    cos = sin = jnp.zeros(turns.shape, F32)
+    for n in range(16):
+        here = turns == n
+        cos = jnp.where(here, math.cos(2.0 * math.pi * n / 16), cos)
+        sin = jnp.where(here, math.sin(2.0 * math.pi * n / 16), sin)
+    return cos, sin
 
 
 def device_waves(waves, steps, place):
@@ -410,7 +415,7 @@
         return jnp.concatenate([stacked[rows, at : at + 1], stacked[rows, at + 8 : at + 9]], axis=0)
 
     (block,) = mixed_row(column, weights, 32)
-    for n in range(OWNERS):
+    for n in range(OWNERS // 2):
         out[n] = block
 
 
@@ -430,7 +435,7 @@
     own, got, pack, fields, z_back, z_fwd,
     kept, sent, values, y_s, rhs_s, g_s, t_s, values_v, sems,
 ):
-    core = lax.axis_index("gx") % 2
+    core = lax.axis_index("core")
     for t in range(2):
         y_s[2 * core + t] = own[t]
         y_s[2 * (1 - core) + t] = got[t]
@@ -508,7 +513,7 @@
 
 
 def fine_level(
-    arrived, table, z_back_h, skip, project_h, bias_h, base_h, out, base, out_v,
+    mine, other, table, z_back_h, skip, project_h, bias_h, base_h, out, base, out_v,
     y_s, rhs_s, skip_v, z_back, project_mix, bias_mix, sems, base_sems, out_sems,):
     def taken(p):
         rows = pl.ds(2 * p, 2)
@@ -532,9 +537,15 @@
     for p in range(8):
         for copy in taken(p):
             copy.start()
+    first = lax.axis_index("core") == 0
     modes = []
     for t in range(4):
-        tiles = [arrived[pl.ds(2 * t + u, OWNERS, stride=8), :] for u in range(2)]
+        tiles = []
+        for u in range(2):
+            a, b = [ref[pl.ds(2 * t + u, OWNERS // 2, stride=8), :] for ref in (mine, other)]
+            cores = jnp.where(first, a, b), jnp.where(first, b, a)
+            rows = [cores[c][16 * x : 16 * x + 16] for x in range(4) for c in range(2)]
+            tiles.append(jnp.concatenate(rows, axis=0))
         modes.append(jnp.concatenate(tiles, axis=1))
     mh, ml = split(jnp.concatenate(modes, axis=0))
     for t in range(4):
@@ -586,12 +597,12 @@
         given(p).wait()
 
 
-def exchange(tiles):
-    return lax.all_to_all(tiles, AXES, split_axis=0, concat_axis=0, tiled=True)
+def exchange(tiles, axes=AXES):
+    return lax.all_to_all(tiles, axes, split_axis=0, concat_axis=0, tiled=True)
 
 
 def between_cores(array):
-    return lax.ppermute(array, "gx", [(i, i ^ 1) for i in range(lax.axis_size("gx"))])
+    return lax.ppermute(array, "core", [(0, 1), (1, 0)])
 
 
 def stay(array):
@@ -693,13 +704,14 @@
     skip, base = prepared
     mixed = call(
         second_mix,
-        out_shape=shape((OWNERS, 8, 128), F32),
+        out_shape=shape((OWNERS // 2, 8, 128), F32),
         in_specs=[VMEM, VMEM], out_specs=VMEM, name="second_mix",
     )(arrived, spectral_out)
+    mine = exchange(mixed, CHIPS).reshape(OWNERS * 4, 128)
     return pl.pallas_call(
         fine_level, compiler_params=pltpu.CompilerParams(vmem_limit_bytes=32 << 20),
         out_shape=shape((CIN, 16, 16, NZ), F32),
-        in_specs=[VMEM, VMEM] + [HBM] * 5, out_specs=HBM, name="fine_level",
+        in_specs=[VMEM] * 3 + [HBM] * 5, out_specs=HBM, name="fine_level",
         scratch_shapes=[
             pltpu.VMEM((CIN, 16, 16, NZ), F32), pltpu.VMEM((CIN, 16, 16, NZ), F32),
             pltpu.VMEM((2, 512, 128), F32), pltpu.VMEM((4, 256, 128), F32),
@@ -708,15 +720,16 @@
             dma((8,)),
         ],
     )(
-        exchange(mixed).reshape(OWNERS * 8, 128), fine_t, stay(jnp.asarray(fine_z_table())), stay(skip),
+        mine, between_cores(mine), fine_t, stay(jnp.asarray(fine_z_table())), stay(skip),
         stay(project_mix), stay(bias_mix), stay(base),
     )
 
 
 def solution(mesh):
     owned = P(AXES, None, None, None, None)
-    grid = P(None, "gx", "gy", None)
+    grid = P(None, ("x", "core"), "gy", None)
     in_specs = (grid, P(), P(), owned, P(), P(), owned, P(), P(), P(), P())
+    cores = jax.sharding.Mesh(mesh.devices.reshape(4, 2, 16), AXES)
     return jax.shard_map(
-        on_device, mesh=mesh, in_specs=in_specs, out_specs=grid, check_vma=False
-    )
+        on_device, mesh=cores, in_specs=in_specs, out_specs=grid, check_vma=False
+    )

time: 94.1 us -> 93 us (0.988)
  blocking collectives: 17.9 us -> 13.3 us
  starting transfers between devices: 20.7 us -> 23 us
  waiting for transfers between devices: 26.4 us -> 27.6 us
    all_to_all x1, blocking collectives: 17.9 us -> 13.3 us  [exchange(): return lax.all_to_all(tiles, axes, split_axis=0, concat_axis=0, tiled=True)]
    ppermute x2 -> x3, starting transfers between devices: 1.12 us -> 3.44 us  [between_cores(): return lax.ppermute(array, 'core', [(0, 1), (1, 0)])]
    ppermute x2 -> x3, waiting for transfers between devices: 1.61 us -> 2.78 us  [between_cores(): return lax.ppermute(array, 'core', [(0, 1), (1, 0)])]
  transfers between devices with their start and end apart: 5 -> 6, of which waited for: 5 -> 6; matrix products, arithmetic and copies ran while one was open for 2% -> 2% of each run, Pallas kernels for 11% -> 12%
where the time goes in v8:
time: 93 us; the launch traced here: 92.6 us
  waiting for transfers between devices  27.6 us (30%)
  Pallas kernels  25.5 us (27%)
  starting transfers between devices  23 us (25%)
  blocking collectives  13.3 us (14%)
  local copies, waits for them, and re-layouts  2.78 us (3%)
    all_to_all x3, waiting for transfers between devices, exchange(): return lax.all_to_all(tiles, axes, split_axis=0, concat_axis=0, tiled=True)  24.8 us
    all_to_all x3, starting transfers between devices, exchange(): return lax.all_to_all(tiles, axes, split_axis=0, concat_axis=0, tiled=True)  19.6 us
    all_to_all x1, blocking collectives, exchange(): return lax.all_to_all(tiles, axes, split_axis=0, concat_axis=0, tiled=True)  13.3 us
    pallas_call x1, Pallas kernels, on_device(): call(bypass, out_shape=(pltpu.HBM((8, NZ, 512), F32), pltpu.HBM((CIN, 16,...  5.92 us
    pallas_call x1, Pallas kernels, on_device(): pl.pallas_call(fine_level, compiler_params=pltpu.CompilerParams(vmem_limi...  5.24 us
    ppermute x3, starting transfers between devices, between_cores(): return lax.ppermute(array, 'core', [(0, 1), (1, 0)])  3.44 us
    pallas_call x1, Pallas kernels, on_device(): call(prepare, out_shape=(shape((256, 512), BF16), shape((256, 512), BF16)...  3.3 us
    pallas_call x1, Pallas kernels, on_device(): pl.pallas_call(first_spectrum, out_shape=(shape((OWNERS, 128), F32), shap...  3.12 us
  transfers between devices with their start and end apart: 6, of which 6 were waited for; matrix products, arithmetic and copies ran while one was open for 2% of the time, Pallas kernels for 12%

profile of v8, /device:TPU:1, one launch (start us, length us, event | category | flops | bytes accessed | tf_op | source)
XLA Modules:
  0.0 92.6 jit_solution(5937804990643434320)
XLA Ops:
  0.0 3.1 %first_spectrum.1 = (f32[128,128]{1,0:T(8,128)}, f32[8,128]{1,0:T(8,128)}) custom-call(f32[4,16,16,128]{3,2,1,0:T(8,128)} %fields.5, bf16[384,128]{1,0:T(8,128)(2,1)} %constant.14.clone.ztab_h, bf16[2,512,256]{2,1,0:T(8,128)(2,1)} %constant.15.clone.ptab_h, s32[2,512]{1,0:T(2,128)} %constant.16.clone.steps_h.steps), custom_call_target="tpu_custom_call" | custom-call | tf_op jit(solution)/shard_map/first_spectrum/pallas_call | solution.py:622
  3.1 11.5 %all-to-all-start = ((f32[128,1,128]{2,1,0:T(1,128)}), f32[128,1,128]{2,1,0:T(1,128)S(1)}, u32[]{:S(2)}, u32[]{:S(2)}) async-start(f32[128,1,128]{2,1,0:T(1,128)} %bitcast.23), calls=%async_computation | async-start | bytes 131072 | tf_op jit(solution)/shard_map/all_to_all | solution.py:601
  14.6 0.8 copy.27.lift
  15.4 0.7 copy.28.lift_bias
  16.1 0.7 copy-done.7
  16.9 1.1 %prepare_mix.1 = (f32[2,2,8,32,64]{4,3,2,1,0:T(8,128)S(1)}, f32[32,128]{1,0:T(8,128)S(1)}, f32[32,32]{1,0:T(8,128)S(1)}) custom-call(f32[8,128]{1,0:T(8,128)S(1)} %copy-done.7, f32[2,2,8,32,64]{4,3,2,1,0:T(8,128)} %weights.2, f32[32,4]{1,0:T(8,128)S(1)} %copy.27.lift, f32[32,1]{1,0:T(8,128)S(1)} %copy.28.lift_bias), custom_call_target="tpu_custom_call" | custom-call | flops 2147483648 | bytes 6291456 | tf_op jit(solution)/shard_map/prepare_mix/pallas_call | solution.py:632
  18.0 6.3 %all-to-all-done = f32[128,1,128]{2,1,0:T(1,128)S(1)} async-done(((f32[128,1,128]{2,1,0:T(1,128)}), f32[128,1,128]{2,1,0:T(1,128)S(1)}, u32[]{:S(2)}, u32[]{:S(2)}) %all-to-all-start) | async-done | bytes 65568 | tf_op jit(solution)/shard_map/all_to_all | solution.py:601
  24.3 1.4 %first_mix.1 = (f32[128,8,128]{2,1,0:T(8,128)}, f32[8,128]{1,0:T(8,128)S(1)}) custom-call(f32[128,128]{1,0:T(8,128)S(1)} %bitcast.16, f32[32,128]{1,0:T(8,128)S(1)} %get-tuple-element.49.lift_wide, f32[32,32]{1,0:T(8,128)S(1)} %get-tuple-element.50.bias_column, f32[2,2,8,32,64]{4,3,2,1,0:T(8,128)S(1)} %get-tuple-element.51.weights), custom_call_target="tpu_custom_call" | custom-call | tf_op jit(solution)/shard_map/first_mix/pallas_call | solution.py:642
  25.8 4.3 %all-to-all-start.1 = ((f32[128,8,128]{2,1,0:T(8,128)}), f32[128,8,128]{2,1,0:T(8,128)S(1)}, u32[]{:S(2)}, u32[]{:S(2)}) async-start(f32[128,8,128]{2,1,0:T(8,128)} %get-tuple-element.52), calls=%async_computation.1 | async-start | bytes 1048576 | tf_op jit(solution)/shard_map/all_to_all | solution.py:601
  30.2 3.3 %prepare.1 = (bf16[256,512]{1,0:T(8,128)(2,1)S(1)}, bf16[256,512]{1,0:T(8,128)(2,1)S(1)}, bf16[2,512,256]{2,1,0:T(8,128)(2,1)S(1)}, bf16[112,512]{1,0:T(8,128)(2...) custom-call(f32[8,128]{1,0:T(8,128)S(1)} %get-tuple-element.53.after, ...), custom_call_target="tpu_custom_call" | custom-call | flops 2147483648 | bytes 6291456 | tf_op jit(solution)/shard_map/prepare/pallas_call | solution.py:648
  33.5 10.7 %all-to-all-done.1 = f32[128,8,128]{2,1,0:T(8,128)S(1)} async-done(((f32[128,8,128]{2,1,0:T(8,128)}), f32[128,8,128]{2,1,0:T(8,128)S(1)}, u32[]{:S(2)}, u32[]{:S(2)}) %all-to-all-start.1) | async-done | bytes 524320 | tf_op jit(solution)/shard_map/all_to_all | solution.py:601
  44.6 0.7 collective-permute-start
  45.6 0.6 collective-permute-done.got
  46.2 2.9 %coarse_level.1 = (f32[2,128,128]{2,1,0:T(8,128)S(1)}, f32[2,128,128]{2,1,0:T(8,128)S(1)}, bf16[8,2,128,512]{3,2,1,0:T(8,128)(2,1)}) custom-call(f32[2,128,128]{2,1,0:T(8,128)S(1)} %invert_own.1.own, f32[2,128,128]{2,1,0:T(8,128)S(1)} %collective-permute-done.got, bf16[112,512]{1,0:T(8,128)(2,1)S(1)} %get-tuple-element.65.pack, ...), custom_call_target="tpu_custom_call" | custom-call | tf_op jit(solution)/shard_map/coarse_level/pallas_call | solution.py:670
  49.5 1.0 %collective-permute-done.1.got = f32[2,128,128]{2,1,0:T(8,128)S(1)} collective-permute-done((f32[2,128,128]{2,1,0:T(8,128)S(1)}, f32[2,128,128]{2,1,0:T(8,128)S(1)}, u32[]{:S(2)}, u32[]{:S(2)}) %collective-permute-start.1) | collective-permute-done | bytes 131104 | tf_op jit(solution)/shard_map/ppermute | solution.py:605
  50.5 1.1 %spread.1 = (f32[1024,128]{1,0:T(8,128)}, f32[8,128]{1,0:T(8,128)S(1)}) custom-call(f32[2,128,128]{2,1,0:T(8,128)S(1)} %get-tuple-element.66.kept, f32[2,128,128]{2,1,0:T(8,128)S(1)} %collective-permute-done.1.got, bf16[2,512,256]{2,1,0:T(8,128)(2,1)S(1)} %get-tuple-element.68.table), custom_call_target="tpu_custom_call" | custom-call | tf_op jit(solution)/shard_map/spread/pallas_call | solution.py:682
  51.7 3.8 %all-to-all-start.2 = ((f32[128,8,128]{2,1,0:T(8,128)}), f32[128,8,128]{2,1,0:T(8,128)S(1)}, u32[]{:S(2)}, u32[]{:S(2)}) async-start(f32[128,8,128]{2,1,0:T(8,128)} %bitcast.22), calls=%async_computation.2 | async-start | bytes 1048576 | tf_op jit(solution)/shard_map/all_to_all | solution.py:601
  55.9 5.9 %bypass.1 = (f32[8,128,512]{2,1,0:T(8,128)}, f32[4,16,16,128]{3,2,1,0:T(8,128)}) custom-call(f32[8,128]{1,0:T(8,128)S(1)} %get-tuple-element.70.after, bf16[8,2,128,512]{3,2,1,0:T(8,128)(2,1)} %get-tuple-element.71.values, bf16[256,512]{1,0:T(8,128)(2,1)} %get-tuple-element.72.wide_mix_h, f32[4,16,16,128]{3,2,1,0:T(8,128)S(1)} %copy-done, ...), custom_call_target="tpu_custom_call" | custom-call | flops 2147483648 | bytes 6291456 | tf_op jit(solution)/shard_map/bypass/pallas_call | solution.py:688
  61.9 7.8 %all-to-all-done.2.arrived = f32[128,8,128]{2,1,0:T(8,128)S(1)} async-done(((f32[128,8,128]{2,1,0:T(8,128)}), f32[128,8,128]{2,1,0:T(8,128)S(1)}, u32[]{:S(2)}, u32[]{:S(2)}) %all-to-all-start.2) | async-done | bytes 524320 | tf_op jit(solution)/shard_map/all_to_all | solution.py:601
  69.7 0.7 second_mix.1
  70.4 13.3 %all_to_all.27 = f32[64,8,128]{2,1,0:T(8,128)S(1)} all-to-all(f32[64,8,128]{2,1,0:T(8,128)S(1)} %second_mix.1), channel_id=1, replica_groups=mesh['x'=4,'core'=2,'gy'=16] {'x','gy'}, dimensions={0} | all-to-all | bytes 524288 | tf_op jit(solution)/shard_map/all_to_all | solution.py:601
  83.7 2.3 %collective-permute-start.2 = (f32[512,128]{1,0:T(8,128)S(1)}, f32[512,128]{1,0:T(8,128)S(1)}, u32[]{:S(2)}, u32[]{:S(2)}) collective-permute-start(f32[512,128]{1,0:T(8,128)S(1)} %bitcast.12), channel_id=1, source_target_pairs={{0,16},{16,0},{1,17},{17,1},{2,18},{18,2},{3,19},{19,3},{4,20},{20... | collective-permute-start | bytes 786440 | tf_op jit(solution)/shard_map/ppermute | solution.py:605
  86.1 1.2 %collective-permute-done.2.other = f32[512,128]{1,0:T(8,128)S(1)} collective-permute-done((f32[512,128]{1,0:T(8,128)S(1)}, f32[512,128]{1,0:T(8,128)S(1)}, u32[]{:S(2)}, u32[]{:S(2)}) %collective-permute-start.2) | collective-permute-done | bytes 262176 | tf_op jit(solution)/shard_map/ppermute | solution.py:605
  87.2 5.2 %fine_level.1 = f32[4,16,16,128]{3,2,1,0:T(8,128)} custom-call(f32[512,128]{1,0:T(8,128)S(1)} %bitcast.13, f32[512,128]{1,0:T(8,128)S(1)} %collective-permute-done.2.other, bf16[2,512,512]{2,1,0:T(8,128)(2,1)S(1)} %copy-done.1, bf16[512,256]{1,0:T(8,128)(2,1)} %constant.20.clone.z_back_h, f32[8,128,512]{2,1,0:T(8,128)} %get-tuple-element.77.skip, ...), custom_call_target="tpu_custom_call" | custom-call | tf_op jit(solution)/shard_map/fine_level/pallas_call | solution.py:711
  (35 shorter events, 1.7 us)
Async XLA Ops:
  3.1 21.2 %all-to-all-start = ((f32[128,1,128]{2,1,0:T(1,128)}), f32[128,1,128]{2,1,0:T(1,128)S(1)}, u32[]{:S(2)}, u32[]{:S(2)}) async-start(f32[128,1,128]{2,1,0:T(1,128)} %bitcast.23), calls=%async_computation | async-start | bytes 131072 | tf_op jit(solution)/shard_map/all_to_all | solution.py:601
  16.1 0.7 copy-start.7
  16.8 13.2 %copy-start.13 = (f32[64,32]{0,1:T(8,128)S(1)}, f32[64,32]{0,1:T(8,128)}, u32[]{:S(2)}) copy-start(f32[64,32]{0,1:T(8,128)} %param.22) | copy-start | bytes 24580
  16.8 13.3 %copy-start.4 = (s32[2,512]{1,0:T(2,128)S(1)}, s32[2,512]{1,0:T(2,128)}, u32[]{:S(2)}) copy-start(s32[2,512]{1,0:T(2,128)} %constant.16.clone.steps_h.steps) | copy-start | bytes 12292
  16.8 13.3 %copy-start.5 = (f32[32]{0:T(128)S(1)}, f32[32]{0:T(128)}, u32[]{:S(2)}) copy-start(f32[32]{0:T(128)} %param.20) | copy-start | bytes 388
  16.8 13.3 %copy-start.6 = (f32[32,64]{1,0:T(8,128)S(1)}, f32[32,64]{1,0:T(8,128)}, u32[]{:S(2)}) copy-start(f32[32,64]{1,0:T(8,128)} %bypass_out.1) | copy-start | bytes 24580
  16.8 13.3 %copy-start.8 = (f32[4,32]{1,0:T(4,128)S(1)}, f32[4,32]{1,0:T(4,128)}, u32[]{:S(2)}) copy-start(f32[4,32]{1,0:T(4,128)} %project.3) | copy-start | bytes 1540
  16.8 13.3 %copy-start.9 = (f32[64]{0:T(128)S(1)}, f32[64]{0:T(128)}, u32[]{:S(2)}) copy-start(f32[64]{0:T(128)} %param.23) | copy-start | bytes 772
  16.8 13.3 %copy-start.10 = (f32[32]{0:T(128)S(1)}, f32[32]{0:T(128)}, u32[]{:S(2)}) copy-start(f32[32]{0:T(128)} %param.26) | copy-start | bytes 388
  16.9 13.3 %copy-start.11 = (f32[4,16,512]{2,1,0:T(8,128)S(1)}, f32[4,16,512]{2,1,0:T(8,128)}, u32[]{:S(2)}) copy-start(f32[4,16,512]{2,1,0:T(8,128)} %constant.17.clone.waves) | copy-start | bytes 393220
  25.8 18.4 %all-to-all-start.1 = ((f32[128,8,128]{2,1,0:T(8,128)}), f32[128,8,128]{2,1,0:T(8,128)S(1)}, u32[]{:S(2)}, u32[]{:S(2)}) async-start(f32[128,8,128]{2,1,0:T(8,128)} %get-tuple-element.52), calls=%async_computation.1 | async-start | bytes 1048576 | tf_op jit(solution)/shard_map/all_to_all | solution.py:601
  44.5 1.7 %copy-start = (f32[4,16,16,128]{3,2,1,0:T(8,128)S(1)}, f32[4,16,16,128]{3,2,1,0:T(8,128)}, u32[]{:S(2)}) copy-start(f32[4,16,16,128]{3,2,1,0:T(8,128)} %fields.5) | copy-start | bytes 1572868
  44.5 1.7 %copy-start.2 = (bf16[64,128]{1,0:T(8,128)(2,1)S(1)}, bf16[64,128]{1,0:T(8,128)(2,1)}, u32[]{:S(2)}) copy-start(bf16[64,128]{1,0:T(8,128)(2,1)} %constant.18.clone.z_back) | copy-start | bytes 49156
  44.6 1.7 %copy-start.3 = (bf16[32,256]{1,0:T(8,128)(2,1)S(1)}, bf16[32,256]{1,0:T(8,128)(2,1)}, u32[]{:S(2)}) copy-start(bf16[32,256]{1,0:T(8,128)(2,1)} %constant.19.clone.z_fwd) | copy-start | bytes 49156
  44.6 1.7 %collective-permute-start = (f32[2,128,128]{2,1,0:T(8,128)S(1)}, f32[2,128,128]{2,1,0:T(8,128)S(1)}, u32[]{:S(2)}, u32[]{:S(2)}) collective-permute-start(f32[2,128,128]{2,1,0:T(8,128)S(1)} %invert_mate.1), channel_id=1, source_target_pairs={{0,16},{16,0},{1,17},{17,1},{2,18},{18,2},{3,19},{19,3},{4,20},{20... | collective-permute-start | bytes 393224 | tf_op jit(solution)/shard_map/ppermute | solution.py:605
  45.6 9.9 %copy-start.14 = (f32[4]{0:T(128)S(1)}, f32[4]{0:T(128)}, u32[]{:S(2)}) copy-start(f32[4]{0:T(128)} %param.28) | copy-start | bytes 52
  45.6 10.0 %copy-start.12 = (f32[2,2,8,64,32]{3,4,2,1,0:T(8,128)S(1)}, f32[2,2,8,64,32]{3,4,2,1,0:T(8,128)}, u32[]{:S(2)}) copy-start(f32[2,2,8,64,32]{3,4,2,1,0:T(8,128)} %param.24) | copy-start | bytes 786436
  49.1 1.4 %collective-permute-start.1 = (f32[2,128,128]{2,1,0:T(8,128)S(1)}, f32[2,128,128]{2,1,0:T(8,128)S(1)}, u32[]{:S(2)}, u32[]{:S(2)}) collective-permute-start(f32[2,128,128]{2,1,0:T(8,128)S(1)} %get-tuple-element.67), channel_id=1, source_target_pairs={{0,16},{16,0},{1,17},{17,1},{2,18},{18,2},{3,19},{19,3},{4,20},{20... | collective-permute-start | bytes 393224 | tf_op jit(solution)/shard_map/ppermute | solution.py:605
  51.7 18.0 %all-to-all-start.2 = ((f32[128,8,128]{2,1,0:T(8,128)}), f32[128,8,128]{2,1,0:T(8,128)S(1)}, u32[]{:S(2)}, u32[]{:S(2)}) async-start(f32[128,8,128]{2,1,0:T(8,128)} %bitcast.22), calls=%async_computation.2 | async-start | bytes 1048576 | tf_op jit(solution)/shard_map/all_to_all | solution.py:601
  61.9 25.4 %copy-start.1 = (bf16[2,512,512]{2,1,0:T(8,128)(2,1)S(1)}, bf16[2,512,512]{2,1,0:T(8,128)(2,1)}, u32[]{:S(2)}) copy-start(bf16[2,512,512]{2,1,0:T(8,128)(2,1)} %get-tuple-element.76.table) | copy-start | bytes 3145732
  83.7 3.5 %collective-permute-start.2 = (f32[512,128]{1,0:T(8,128)S(1)}, f32[512,128]{1,0:T(8,128)S(1)}, u32[]{:S(2)}, u32[]{:S(2)}) collective-permute-start(f32[512,128]{1,0:T(8,128)S(1)} %bitcast.12), channel_id=1, source_target_pairs={{0,16},{16,0},{1,17},{17,1},{2,18},{18,2},{3,19},{19,3},{4,20},{20... | collective-permute-start | bytes 786440 | tf_op jit(solution)/shard_map/ppermute | solution.py:605

commit v9 on v8

--- a/solution.py
+++ b/solution.py
@@ -239,6 +239,21 @@
     copy.wait()
 
 
+def core_columns(table):
+    first = lax.axis_index("core") == 0
+    lane = iota((table.shape[0], 128), 1)
+    made = []
+    for t in range(4):
+        tile = table[:, 128 * t : 128 * t + 128]
+        tile = jnp.where(first, tile, pltpu.roll(tile, 112, 1))
+        total = tile
+        for x in range(1, 4):
+            total = jnp.where(lane // 16 == x, pltpu.roll(tile, 128 - 16 * x, 1), total)
+        made.append(total)
+    pairs = [jnp.where(lane < 64, made[t], pltpu.roll(made[t + 1], 64, 1)) for t in (0, 2)]
+    return jnp.concatenate(pairs, axis=1)
+
+
 def prepare(
     after, waves, steps, lift, lift_bias, bypass_in, bias_in, bypass_out, bias_out, project,
     own_t, mate_t, spread_t, pack, fine_t, wide_mix, project_mix, bias_mix,
@@ -253,8 +268,8 @@
         jnp.concatenate(wave_rows(along, cos_y, sin_y, range(0, 16, 2)), axis=0)
         for along in (own, mate)
     ]
-    own_t[0:128], own_t[128:256] = split(tables[0] * BACK)
-    mate_t[0:128], mate_t[128:256] = split(tables[1] * BACK)
+    own_t[0:128], own_t[128:256] = split(core_columns(tables[0]) * BACK)
+    mate_t[0:128], mate_t[128:256] = split(core_columns(tables[1]) * BACK)
     scale = 1.0 / math.sqrt(TOTAL / 4.0)
     for patch in range(2):
         at = slice(128 * patch, 128 * patch + 128)
@@ -389,15 +404,14 @@
 
     halves = mixed_row(column, weights, 32)
     token[...] = halves[0]
-    copies = []
-    for half in range(2):
-        for i in range(16):
-            blocks[half, i] = halves[half]
-        for i in range(half, 8, 2):
-            copies.append(
-                pltpu.make_async_copy(blocks.at[half], out.at[pl.ds(16 * i, 16)], sems.at[i])
-            )
-            copies[-1].start()
+    block = jnp.concatenate(halves, axis=0)
+    for i in range(16):
+        blocks[i] = block
+    copies = [
+        pltpu.make_async_copy(blocks, out.at[pl.ds(16 * i, 16)], sems.at[i]) for i in range(4)
+    ]
+    for copy in copies:
+        copy.start()
     for copy in copies:
         copy.wait()
 
@@ -422,13 +436,17 @@
 def invert(arrived, table, out):
     modes = []
     for t in range(4):
-        tiles = [arrived[pl.ds(2 * t + u, OWNERS, stride=8), :] for u in range(2)]
+        tiles = [
+            arrived[pl.ds(8 * h + 2 * t + u, OWNERS // 2, stride=16), :]
+            for h in range(2)
+            for u in range(2)
+        ]
         modes.append(jnp.concatenate(tiles, axis=1))
     mh, ml = split(jnp.concatenate(modes, axis=0))
     made = mm(table[...], mh)
     made = made[:128] + made[128:] + mm(table[:128], ml)
-    out[0] = made[:, :128]
-    out[1] = made[:, 128:]
+    for j in range(4):
+        out[j] = made[:, 128 * j : 128 * j + 128]
 
 
 def coarse_level(
@@ -436,9 +454,8 @@
     kept, sent, values, y_s, rhs_s, g_s, t_s, values_v, sems,
 ):
     core = lax.axis_index("core")
-    for t in range(2):
-        y_s[2 * core + t] = own[t]
-        y_s[2 * (1 - core) + t] = got[t]
+    for j in range(4):
+        y_s[j] = own[j] + got[j]
     for h in range(2):
         for t in range(2):
             for q in range(2):
@@ -641,14 +658,14 @@
     weights, lift_wide, bias_column = prepared
     mixed, token = call(
         first_mix,
-        out_shape=(pltpu.HBM((OWNERS, 8, 128), F32), shape((8, 128), F32)),
+        out_shape=(pltpu.HBM((OWNERS // 2, 16, 128), F32), shape((8, 128), F32)),
         in_specs=[VMEM] * 4, out_specs=(HBM, VMEM), name="first_mix",
-        scratch_shapes=[pltpu.VMEM((2, 16, 8, 128), F32), dma((8,))],
+        scratch_shapes=[pltpu.VMEM((16, 16, 128), F32), dma((4,))],
     )(arrived, lift_wide, bias_column, weights)
     prepared = call(
         prepare,
         out_shape=(
-            shape((256, 512), BF16), shape((256, 512), BF16), shape((2, 512, 256), BF16),
+            shape((256, 256), BF16), shape((256, 256), BF16), shape((2, 512, 256), BF16),
             shape((112, 512), BF16), pltpu.HBM((2, 512, 512), BF16), pltpu.HBM((256, 512), BF16),
             pltpu.HBM((128, 512), BF16), pltpu.HBM((16, 512), BF16),
         ),
@@ -657,12 +674,12 @@
         token, waves, steps, lift, lift_bias[None], bypass_in, bias_in[None], bypass_out,
         bias_out[None], project,
     )
-    mine, prepared = lax.optimization_barrier((exchange(mixed), prepared))
+    mine, prepared = lax.optimization_barrier((exchange(mixed, CHIPS), prepared))
     own_t, mate_t, spread_t, pack, fine_t, wide_mix, project_mix, bias_mix = prepared
     mine = mine.reshape(OWNERS * 8, 128)
     own, got = [
         call(
-            invert, out_shape=shape((2, 128, 128), F32), in_specs=[VMEM] * 2, out_specs=VMEM,
+            invert, out_shape=shape((4, 128, 128), F32), in_specs=[VMEM] * 2, out_specs=VMEM,
             name=name, cost_estimate=work,
         )(mine, table)
         for name, table in (("invert_own", own_t), ("invert_mate", mate_t))

time: 93 us -> 93 us (level)
  starting transfers between devices: 23 us -> 25.3 us
  waiting for transfers between devices: 27.6 us -> 25.6 us
    all_to_all x3, waiting for transfers between devices: 24.8 us -> 22.7 us  [exchange(): return lax.all_to_all(tiles, axes, split_axis=0, concat_axis=0, tiled=True)]
    ppermute x3, starting transfers between devices: 3.44 us -> 5.34 us  [between_cores(): return lax.ppermute(array, 'core', [(0, 1), (1, 0)])]
  transfers between devices with their start and end apart: 6 -> 6, of which waited for: 6 -> 6; matrix products, arithmetic and copies ran while one was open for 2% -> 2% of each run, Pallas kernels for 12% -> 11%
where the time goes in v9:
time: 93 us; the launch traced here: 92.5 us
  waiting for transfers between devices  25.6 us (28%)
  starting transfers between devices  25.3 us (27%)
  Pallas kernels  25.1 us (27%)
  blocking collectives  13.3 us (14%)
  local copies, waits for them, and re-layouts  2.78 us (3%)
    all_to_all x3, waiting for transfers between devices, exchange(): return lax.all_to_all(tiles, axes, split_axis=0, concat_axis=0, tiled=True)  22.7 us
    all_to_all x3, starting transfers between devices, exchange(): return lax.all_to_all(tiles, axes, split_axis=0, concat_axis=0, tiled=True)  20 us
    all_to_all x1, blocking collectives, exchange(): return lax.all_to_all(tiles, axes, split_axis=0, concat_axis=0, tiled=True)  13.3 us
    pallas_call x1, Pallas kernels, on_device(): call(bypass, out_shape=(pltpu.HBM((8, NZ, 512), F32), pltpu.HBM((CIN, 16,...  5.92 us
    ppermute x3, starting transfers between devices, between_cores(): return lax.ppermute(array, 'core', [(0, 1), (1, 0)])  5.34 us
    pallas_call x1, Pallas kernels, on_device(): pl.pallas_call(fine_level, compiler_params=pltpu.CompilerParams(vmem_limi...  5.24 us
    pallas_call x1, Pallas kernels, on_device(): pl.pallas_call(first_spectrum, out_shape=(shape((OWNERS, 128), F32), shap...  3.12 us
    ppermute x3, waiting for transfers between devices, between_cores(): return lax.ppermute(array, 'core', [(0, 1), (1, 0)])  2.88 us
  transfers between devices with their start and end apart: 6, of which 6 were waited for; matrix products, arithmetic and copies ran while one was open for 2% of the time, Pallas kernels for 11%

profile of v9, /device:TPU:1, one launch (start us, length us, event | category | flops | bytes accessed | tf_op | source)
XLA Modules:
  0.0 92.5 jit_solution(124468715492386001)
XLA Ops:
  0.0 3.1 %first_spectrum.1 = (f32[128,128]{1,0:T(8,128)}, f32[8,128]{1,0:T(8,128)}) custom-call(f32[4,16,16,128]{3,2,1,0:T(8,128)} %fields.5, bf16[384,128]{1,0:T(8,128)(2,1)} %constant.14.clone.ztab_h, bf16[2,512,256]{2,1,0:T(8,128)(2,1)} %constant.15.clone.ptab_h, s32[2,512]{1,0:T(2,128)} %constant.16.clone.steps_h.steps), custom_call_target="tpu_custom_call" | custom-call | tf_op jit(solution)/shard_map/first_spectrum/pallas_call | solution.py:639
  3.1 11.5 %all-to-all-start = ((f32[128,1,128]{2,1,0:T(1,128)}), f32[128,1,128]{2,1,0:T(1,128)S(1)}, u32[]{:S(2)}, u32[]{:S(2)}) async-start(f32[128,1,128]{2,1,0:T(1,128)} %bitcast.23), calls=%async_computation | async-start | bytes 131072 | tf_op jit(solution)/shard_map/all_to_all | solution.py:618
  14.6 0.8 copy.27.lift
  15.4 0.7 copy.28.lift_bias
  16.1 0.7 copy-done.7
  16.9 1.1 %prepare_mix.1 = (f32[2,2,8,32,64]{4,3,2,1,0:T(8,128)S(1)}, f32[32,128]{1,0:T(8,128)S(1)}, f32[32,32]{1,0:T(8,128)S(1)}) custom-call(f32[8,128]{1,0:T(8,128)S(1)} %copy-done.7, f32[2,2,8,32,64]{4,3,2,1,0:T(8,128)} %weights.2, f32[32,4]{1,0:T(8,128)S(1)} %copy.27.lift, f32[32,1]{1,0:T(8,128)S(1)} %copy.28.lift_bias), custom_call_target="tpu_custom_call" | custom-call | flops 2147483648 | bytes 6291456 | tf_op jit(solution)/shard_map/prepare_mix/pallas_call | solution.py:649
  18.0 6.3 %all-to-all-done = f32[128,1,128]{2,1,0:T(1,128)S(1)} async-done(((f32[128,1,128]{2,1,0:T(1,128)}), f32[128,1,128]{2,1,0:T(1,128)S(1)}, u32[]{:S(2)}, u32[]{:S(2)}) %all-to-all-start) | async-done | bytes 65568 | tf_op jit(solution)/shard_map/all_to_all | solution.py:618
  24.3 1.4 %first_mix.1 = (f32[64,16,128]{2,1,0:T(8,128)}, f32[8,128]{1,0:T(8,128)S(1)}) custom-call(f32[128,128]{1,0:T(8,128)S(1)} %bitcast.16, f32[32,128]{1,0:T(8,128)S(1)} %get-tuple-element.49.lift_wide, f32[32,32]{1,0:T(8,128)S(1)} %get-tuple-element.50.bias_column, f32[2,2,8,32,64]{4,3,2,1,0:T(8,128)S(1)} %get-tuple-element.51.weights), custom_call_target="tpu_custom_call" | custom-call | tf_op jit(solution)/shard_map/first_mix/pallas_call | solution.py:659
  25.7 4.6 %all-to-all-start.1 = ((f32[64,16,128]{2,1,0:T(8,128)}), f32[64,16,128]{2,1,0:T(8,128)S(1)}, u32[]{:S(2)}, u32[]{:S(2)}) async-start(f32[64,16,128]{2,1,0:T(8,128)} %get-tuple-element.52), calls=%async_computation.1 | async-start | bytes 1048576 | tf_op jit(solution)/shard_map/all_to_all | solution.py:618
  30.5 2.8 %prepare.1 = (bf16[256,256]{1,0:T(8,128)(2,1)S(1)}, bf16[256,256]{1,0:T(8,128)(2,1)S(1)}, bf16[2,512,256]{2,1,0:T(8,128)(2,1)S(1)}, bf16[112,512]{1,0:T(8,128)(2...) custom-call(f32[8,128]{1,0:T(8,128)S(1)} %get-tuple-element.53.after, ...), custom_call_target="tpu_custom_call" | custom-call | flops 2147483648 | bytes 6291456 | tf_op jit(solution)/shard_map/prepare/pallas_call | solution.py:665
  33.3 8.6 %all-to-all-done.1 = f32[64,16,128]{2,1,0:T(8,128)S(1)} async-done(((f32[64,16,128]{2,1,0:T(8,128)}), f32[64,16,128]{2,1,0:T(8,128)S(1)}, u32[]{:S(2)}, u32[]{:S(2)}) %all-to-all-start.1) | async-done | bytes 524320 | tf_op jit(solution)/shard_map/all_to_all | solution.py:618
  42.4 2.6 %collective-permute-start = (f32[4,128,128]{2,1,0:T(8,128)S(1)}, f32[4,128,128]{2,1,0:T(8,128)S(1)}, u32[]{:S(2)}, u32[]{:S(2)}) collective-permute-start(f32[4,128,128]{2,1,0:T(8,128)S(1)} %invert_mate.1), channel_id=1, source_target_pairs={{0,16},{16,0},{1,17},{17,1},{2,18},{18,2},{3,19},{19,3},{4,20},{20... | collective-permute-start | bytes 786440 | tf_op jit(solution)/shard_map/ppermute | solution.py:622
  45.4 0.7 collective-permute-done.got
  46.1 2.8 %coarse_level.1 = (f32[2,128,128]{2,1,0:T(8,128)S(1)}, f32[2,128,128]{2,1,0:T(8,128)S(1)}, bf16[8,2,128,512]{3,2,1,0:T(8,128)(2,1)}) custom-call(f32[4,128,128]{2,1,0:T(8,128)S(1)} %invert_own.1.own, f32[4,128,128]{2,1,0:T(8,128)S(1)} %collective-permute-done.got, bf16[112,512]{1,0:T(8,128)(2,1)S(1)} %get-tuple-element.65.pack, ...), custom_call_target="tpu_custom_call" | custom-call | tf_op jit(solution)/shard_map/coarse_level/pallas_call | solution.py:687
  49.4 1.0 %collective-permute-done.1.got = f32[2,128,128]{2,1,0:T(8,128)S(1)} collective-permute-done((f32[2,128,128]{2,1,0:T(8,128)S(1)}, f32[2,128,128]{2,1,0:T(8,128)S(1)}, u32[]{:S(2)}, u32[]{:S(2)}) %collective-permute-start.1) | collective-permute-done | bytes 131104 | tf_op jit(solution)/shard_map/ppermute | solution.py:622
  50.4 1.1 %spread.1 = (f32[1024,128]{1,0:T(8,128)}, f32[8,128]{1,0:T(8,128)S(1)}) custom-call(f32[2,128,128]{2,1,0:T(8,128)S(1)} %get-tuple-element.66.kept, f32[2,128,128]{2,1,0:T(8,128)S(1)} %collective-permute-done.1.got, bf16[2,512,256]{2,1,0:T(8,128)(2,1)S(1)} %get-tuple-element.68.table), custom_call_target="tpu_custom_call" | custom-call | tf_op jit(solution)/shard_map/spread/pallas_call | solution.py:699
  51.5 3.9 %all-to-all-start.2 = ((f32[128,8,128]{2,1,0:T(8,128)}), f32[128,8,128]{2,1,0:T(8,128)S(1)}, u32[]{:S(2)}, u32[]{:S(2)}) async-start(f32[128,8,128]{2,1,0:T(8,128)} %bitcast.22), calls=%async_computation.2 | async-start | bytes 1048576 | tf_op jit(solution)/shard_map/all_to_all | solution.py:618
  55.9 5.9 %bypass.1 = (f32[8,128,512]{2,1,0:T(8,128)}, f32[4,16,16,128]{3,2,1,0:T(8,128)}) custom-call(f32[8,128]{1,0:T(8,128)S(1)} %get-tuple-element.70.after, bf16[8,2,128,512]{3,2,1,0:T(8,128)(2,1)} %get-tuple-element.71.values, bf16[256,512]{1,0:T(8,128)(2,1)} %get-tuple-element.72.wide_mix_h, f32[4,16,16,128]{3,2,1,0:T(8,128)S(1)} %copy-done, ...), custom_call_target="tpu_custom_call" | custom-call | flops 2147483648 | bytes 6291456 | tf_op jit(solution)/shard_map/bypass/pallas_call | solution.py:705
  61.8 7.8 %all-to-all-done.2.arrived = f32[128,8,128]{2,1,0:T(8,128)S(1)} async-done(((f32[128,8,128]{2,1,0:T(8,128)}), f32[128,8,128]{2,1,0:T(8,128)S(1)}, u32[]{:S(2)}, u32[]{:S(2)}) %all-to-all-start.2) | async-done | bytes 524320 | tf_op jit(solution)/shard_map/all_to_all | solution.py:618
  69.6 0.7 second_mix.1
  70.3 13.3 %all_to_all.27 = f32[64,8,128]{2,1,0:T(8,128)S(1)} all-to-all(f32[64,8,128]{2,1,0:T(8,128)S(1)} %second_mix.1), channel_id=1, replica_groups=mesh['x'=4,'core'=2,'gy'=16] {'x','gy'}, dimensions={0} | all-to-all | bytes 524288 | tf_op jit(solution)/shard_map/all_to_all | solution.py:618
  83.6 2.3 %collective-permute-start.2 = (f32[512,128]{1,0:T(8,128)S(1)}, f32[512,128]{1,0:T(8,128)S(1)}, u32[]{:S(2)}, u32[]{:S(2)}) collective-permute-start(f32[512,128]{1,0:T(8,128)S(1)} %bitcast.12), channel_id=1, source_target_pairs={{0,16},{16,0},{1,17},{17,1},{2,18},{18,2},{3,19},{19,3},{4,20},{20... | collective-permute-start | bytes 786440 | tf_op jit(solution)/shard_map/ppermute | solution.py:622
  85.9 1.2 %collective-permute-done.2.other = f32[512,128]{1,0:T(8,128)S(1)} collective-permute-done((f32[512,128]{1,0:T(8,128)S(1)}, f32[512,128]{1,0:T(8,128)S(1)}, u32[]{:S(2)}, u32[]{:S(2)}) %collective-permute-start.2) | collective-permute-done | bytes 262176 | tf_op jit(solution)/shard_map/ppermute | solution.py:622
  87.1 5.2 %fine_level.1 = f32[4,16,16,128]{3,2,1,0:T(8,128)} custom-call(f32[512,128]{1,0:T(8,128)S(1)} %bitcast.13, f32[512,128]{1,0:T(8,128)S(1)} %collective-permute-done.2.other, bf16[2,512,512]{2,1,0:T(8,128)(2,1)S(1)} %copy-done.1, bf16[512,256]{1,0:T(8,128)(2,1)} %constant.20.clone.z_back_h, f32[8,128,512]{2,1,0:T(8,128)} %get-tuple-element.77.skip, ...), custom_call_target="tpu_custom_call" | custom-call | tf_op jit(solution)/shard_map/fine_level/pallas_call | solution.py:728
  (35 shorter events, 1.9 us)
Async XLA Ops:
  3.1 21.2 %all-to-all-start = ((f32[128,1,128]{2,1,0:T(1,128)}), f32[128,1,128]{2,1,0:T(1,128)S(1)}, u32[]{:S(2)}, u32[]{:S(2)}) async-start(f32[128,1,128]{2,1,0:T(1,128)} %bitcast.23), calls=%async_computation | async-start | bytes 131072 | tf_op jit(solution)/shard_map/all_to_all | solution.py:618
  16.1 0.7 copy-start.7
  16.8 13.6 %copy-start.13 = (f32[64,32]{0,1:T(8,128)S(1)}, f32[64,32]{0,1:T(8,128)}, u32[]{:S(2)}) copy-start(f32[64,32]{0,1:T(8,128)} %param.22) | copy-start | bytes 24580
  16.8 13.7 %copy-start.4 = (s32[2,512]{1,0:T(2,128)S(1)}, s32[2,512]{1,0:T(2,128)}, u32[]{:S(2)}) copy-start(s32[2,512]{1,0:T(2,128)} %constant.16.clone.steps_h.steps) | copy-start | bytes 12292
  16.8 13.7 %copy-start.5 = (f32[32]{0:T(128)S(1)}, f32[32]{0:T(128)}, u32[]{:S(2)}) copy-start(f32[32]{0:T(128)} %param.20) | copy-start | bytes 388
  16.8 13.7 %copy-start.6 = (f32[32,64]{1,0:T(8,128)S(1)}, f32[32,64]{1,0:T(8,128)}, u32[]{:S(2)}) copy-start(f32[32,64]{1,0:T(8,128)} %bypass_out.1) | copy-start | bytes 24580
  16.8 13.7 %copy-start.8 = (f32[4,32]{1,0:T(4,128)S(1)}, f32[4,32]{1,0:T(4,128)}, u32[]{:S(2)}) copy-start(f32[4,32]{1,0:T(4,128)} %project.3) | copy-start | bytes 1540
  16.8 13.7 %copy-start.9 = (f32[64]{0:T(128)S(1)}, f32[64]{0:T(128)}, u32[]{:S(2)}) copy-start(f32[64]{0:T(128)} %param.23) | copy-start | bytes 772
  16.8 13.7 %copy-start.10 = (f32[32]{0:T(128)S(1)}, f32[32]{0:T(128)}, u32[]{:S(2)}) copy-start(f32[32]{0:T(128)} %param.26) | copy-start | bytes 388
  16.9 13.7 %copy-start.11 = (f32[4,16,512]{2,1,0:T(8,128)S(1)}, f32[4,16,512]{2,1,0:T(8,128)}, u32[]{:S(2)}) copy-start(f32[4,16,512]{2,1,0:T(8,128)} %constant.17.clone.waves) | copy-start | bytes 393220
  25.7 16.2 %all-to-all-start.1 = ((f32[64,16,128]{2,1,0:T(8,128)}), f32[64,16,128]{2,1,0:T(8,128)S(1)}, u32[]{:S(2)}, u32[]{:S(2)}) async-start(f32[64,16,128]{2,1,0:T(8,128)} %get-tuple-element.52), calls=%async_computation.1 | async-start | bytes 1048576 | tf_op jit(solution)/shard_map/all_to_all | solution.py:618
  42.4 3.8 %copy-start = (f32[4,16,16,128]{3,2,1,0:T(8,128)S(1)}, f32[4,16,16,128]{3,2,1,0:T(8,128)}, u32[]{:S(2)}) copy-start(f32[4,16,16,128]{3,2,1,0:T(8,128)} %fields.5) | copy-start | bytes 1572868
  42.4 3.8 %copy-start.2 = (bf16[64,128]{1,0:T(8,128)(2,1)S(1)}, bf16[64,128]{1,0:T(8,128)(2,1)}, u32[]{:S(2)}) copy-start(bf16[64,128]{1,0:T(8,128)(2,1)} %constant.18.clone.z_back) | copy-start | bytes 49156
  42.4 3.7 %copy-start.3 = (bf16[32,256]{1,0:T(8,128)(2,1)S(1)}, bf16[32,256]{1,0:T(8,128)(2,1)}, u32[]{:S(2)}) copy-start(bf16[32,256]{1,0:T(8,128)(2,1)} %constant.19.clone.z_fwd) | copy-start | bytes 49156
  42.4 3.7 %collective-permute-start = (f32[4,128,128]{2,1,0:T(8,128)S(1)}, f32[4,128,128]{2,1,0:T(8,128)S(1)}, u32[]{:S(2)}, u32[]{:S(2)}) collective-permute-start(f32[4,128,128]{2,1,0:T(8,128)S(1)} %invert_mate.1), channel_id=1, source_target_pairs={{0,16},{16,0},{1,17},{17,1},{2,18},{18,2},{3,19},{19,3},{4,20},{20... | collective-permute-start | bytes 786440 | tf_op jit(solution)/shard_map/ppermute | solution.py:622
  45.4 10.0 %copy-start.14 = (f32[4]{0:T(128)S(1)}, f32[4]{0:T(128)}, u32[]{:S(2)}) copy-start(f32[4]{0:T(128)} %param.28) | copy-start | bytes 52
  45.4 10.1 %copy-start.12 = (f32[2,2,8,64,32]{3,4,2,1,0:T(8,128)S(1)}, f32[2,2,8,64,32]{3,4,2,1,0:T(8,128)}, u32[]{:S(2)}) copy-start(f32[2,2,8,64,32]{3,4,2,1,0:T(8,128)} %param.24) | copy-start | bytes 786436
  49.0 1.4 %collective-permute-start.1 = (f32[2,128,128]{2,1,0:T(8,128)S(1)}, f32[2,128,128]{2,1,0:T(8,128)S(1)}, u32[]{:S(2)}, u32[]{:S(2)}) collective-permute-start(f32[2,128,128]{2,1,0:T(8,128)S(1)} %get-tuple-element.67), channel_id=1, source_target_pairs={{0,16},{16,0},{1,17},{17,1},{2,18},{18,2},{3,19},{19,3},{4,20},{20... | collective-permute-start | bytes 393224 | tf_op jit(solution)/shard_map/ppermute | solution.py:622
  51.5 18.0 %all-to-all-start.2 = ((f32[128,8,128]{2,1,0:T(8,128)}), f32[128,8,128]{2,1,0:T(8,128)S(1)}, u32[]{:S(2)}, u32[]{:S(2)}) async-start(f32[128,8,128]{2,1,0:T(8,128)} %bitcast.22), calls=%async_computation.2 | async-start | bytes 1048576 | tf_op jit(solution)/shard_map/all_to_all | solution.py:618
  61.8 25.3 %copy-start.1 = (bf16[2,512,512]{2,1,0:T(8,128)(2,1)S(1)}, bf16[2,512,512]{2,1,0:T(8,128)(2,1)}, u32[]{:S(2)}) copy-start(bf16[2,512,512]{2,1,0:T(8,128)(2,1)} %get-tuple-element.76.table) | copy-start | bytes 3145732
  83.6 3.5 %collective-permute-start.2 = (f32[512,128]{1,0:T(8,128)S(1)}, f32[512,128]{1,0:T(8,128)S(1)}, u32[]{:S(2)}, u32[]{:S(2)}) collective-permute-start(f32[512,128]{1,0:T(8,128)S(1)} %bitcast.12), channel_id=1, source_target_pairs={{0,16},{16,0},{1,17},{17,1},{2,18},{18,2},{3,19},{19,3},{4,20},{20... | collective-permute-start | bytes 786440 | tf_op jit(solution)/shard_map/ppermute | solution.py:622

commit v10 on v9

--- a/solution.py
+++ b/solution.py
@@ -273,7 +273,7 @@
     scale = 1.0 / math.sqrt(TOTAL / 4.0)
     for patch in range(2):
         at = slice(128 * patch, 128 * patch + 128)
-        high, less = split(tables[patch].T * scale)
+        high, less = split(core_columns(tables[patch]).T * scale)
         spread_t[0, :, at] = high
         spread_t[1, :, at] = less
     lanes = [
@@ -417,11 +417,10 @@
 
 
 def second_mix(arrived, weights, out):
-    sums = [None, None]
-    for n in range(OWNERS):
-        half = n // 16 % 2
-        sums[half] = arrived[n] if sums[half] is None else sums[half] + arrived[n]
-    stacked = jnp.concatenate(sums + [jnp.zeros((112, 128), F32)], axis=0).T
+    rows = arrived[0]
+    for n in range(1, OWNERS // 2):
+        rows += arrived[n]
+    stacked = jnp.concatenate([rows, jnp.zeros((112, 128), F32)], axis=0).T
 
     def column(s, part, k):
         at = (s * 2 + part) * 2 + k // 4
@@ -451,9 +450,8 @@
 
 def coarse_level(
     own, got, pack, fields, z_back, z_fwd,
-    kept, sent, values, y_s, rhs_s, g_s, t_s, values_v, sems,
+    shared, values, y_s, rhs_s, g_s, values_v, sems,
 ):
-    core = lax.axis_index("core")
     for j in range(4):
         y_s[j] = own[j] + got[j]
     for h in range(2):
@@ -499,28 +497,27 @@
                     [g_s[2 * q + h, pl.ds(4 * t + v, 16, stride=8), :] for v in range(4)]
                 )
                 for u in range(4):
-                    t_s[2 * h + t, pl.ds(4 * q + u, 16, stride=8), :] = made[u]
-    for t in range(2):
-        kept[t] = t_s[2 * core + t]
-        sent[t] = t_s[2 * (1 - core) + t]
+                    shared[2 * h + t, pl.ds(4 * q + u, 16, stride=8), :] = made[u]
     for p in range(8):
         pltpu.make_async_copy(values_v.at[p], values.at[p], sems.at[p]).wait()
 
 
 def spread(kept, got, table, out, token, out_v, sems):
-    rows = [jnp.concatenate([ref[0], ref[1]], axis=1) for ref in (kept, got)]
+    rows = [jnp.concatenate([ref[t] for t in range(4)], axis=1) for ref in (kept, got)]
     th, tl = split(jnp.concatenate(rows, axis=0))
     copies = []
     for j in range(4):
         ah, al = [
-            jnp.concatenate([table[i, pl.ds(128 * t + 32 * j, 32)] for t in range(4)], axis=0)
+            jnp.concatenate([table[i, pl.ds(64 * t + 16 * j, 16)] for t in range(4)], axis=0)
             for i in range(2)
         ]
         made = mm(ah, th) + mm(ah, tl) + mm(al, th)
         for t in range(4):
-            for u in range(2):
-                piece = made[32 * t : 32 * t + 32, 128 * u : 128 * u + 128]
-                out_v[pl.ds(256 * j + 2 * t + u, 32, stride=8), :] = piece
+            for h in range(2):
+                for u in range(2):
+                    at = 128 * (2 * h + u)
+                    piece = made[16 * t : 16 * t + 16, at : at + 128]
+                    out_v[pl.ds(256 * j + 8 * h + 2 * t + u, 16, stride=16), :] = piece
         rows = pl.ds(256 * j, 256)
         copies.append(pltpu.make_async_copy(out_v.at[rows], out.at[rows], sems.at[j]))
         copies[-1].start()
@@ -665,7 +662,7 @@
     prepared = call(
         prepare,
         out_shape=(
-            shape((256, 256), BF16), shape((256, 256), BF16), shape((2, 512, 256), BF16),
+            shape((256, 256), BF16), shape((256, 256), BF16), shape((2, 256, 256), BF16),
             shape((112, 512), BF16), pltpu.HBM((2, 512, 512), BF16), pltpu.HBM((256, 512), BF16),
             pltpu.HBM((128, 512), BF16), pltpu.HBM((16, 512), BF16),
         ),
@@ -684,14 +681,13 @@
         )(mine, table)
         for name, table in (("invert_own", own_t), ("invert_mate", mate_t))
     ]
-    kept, sent, values = call(
+    shared, values = call(
         coarse_level,
         out_shape=(
-            shape((2, 128, 128), F32), shape((2, 128, 128), F32),
-            pltpu.HBM((8, 2, NZ, 512), BF16),
+            shape((4, 128, 128), F32), pltpu.HBM((8, 2, NZ, 512), BF16),
         ),
-        in_specs=[VMEM] * 6, out_specs=(VMEM, VMEM, HBM), name="coarse_level",
-        scratch_shapes=[pltpu.VMEM((4, 128, 128), F32)] * 4
+        in_specs=[VMEM] * 6, out_specs=(VMEM, HBM), name="coarse_level",
+        scratch_shapes=[pltpu.VMEM((4, 128, 128), F32)] * 3
         + [pltpu.VMEM((8, 2, NZ, 512), BF16), dma((8,))],
     )(
         own, between_cores(got), pack, fields, z_back, z_fwd,
@@ -701,7 +697,7 @@
         out_shape=(pltpu.HBM((OWNERS * 8, 128), F32), shape((8, 128), F32)),
         in_specs=[VMEM] * 3, out_specs=(HBM, VMEM), name="spread",
         scratch_shapes=[pltpu.VMEM((OWNERS * 8, 128), F32), dma((4,))],
-    )(kept, between_cores(sent), spread_t)
+    )(shared, between_cores(shared), spread_t)
     prepared = call(
         bypass,
         out_shape=(pltpu.HBM((8, NZ, 512), F32), pltpu.HBM((CIN, 16, 16, NZ), F32)),
@@ -716,7 +712,7 @@
         project_bias[:, None],
     )
     arrived, prepared = lax.optimization_barrier(
-        (exchange(spectrum.reshape(OWNERS, 8, 128)), prepared)
+        (exchange(spectrum.reshape(OWNERS // 2, 16, 128), CHIPS), prepared)
     )
     skip, base = prepared
     mixed = call(

time: 93 us -> 93.7 us (level)
  waiting for transfers between devices: 25.6 us -> 23.5 us
  starting transfers between devices: 25.3 us -> 27 us
    all_to_all x3, waiting for transfers between devices: 22.7 us -> 20.5 us  [exchange(): return lax.all_to_all(tiles, axes, split_axis=0, concat_axis=0, tiled=True)]
where the time goes in v10:
time: 93.7 us; the launch traced here: 93.2 us
  starting transfers between devices  27 us (29%)
  Pallas kernels  25.5 us (27%)
  waiting for transfers between devices  23.5 us (25%)
  blocking collectives  14 us (15%)
  local copies, waits for them, and re-layouts  2.78 us (3%)
    all_to_all x3, starting transfers between devices, exchange(): return lax.all_to_all(tiles, axes, split_axis=0, concat_axis=0, tiled=True)  20.8 us
    all_to_all x3, waiting for transfers between devices, exchange(): return lax.all_to_all(tiles, axes, split_axis=0, concat_axis=0, tiled=True)  20.5 us
    all_to_all x1, blocking collectives, exchange(): return lax.all_to_all(tiles, axes, split_axis=0, concat_axis=0, tiled=True)  14 us
    ppermute x3, starting transfers between devices, between_cores(): return lax.ppermute(array, 'core', [(0, 1), (1, 0)])  6.2 us
    pallas_call x1, Pallas kernels, on_device(): call(bypass, out_shape=(pltpu.HBM((8, NZ, 512), F32), pltpu.HBM((CIN, 16,...  5.92 us
    pallas_call x1, Pallas kernels, on_device(): pl.pallas_call(fine_level, compiler_params=pltpu.CompilerParams(vmem_limi...  5.23 us
    pallas_call x1, Pallas kernels, on_device(): pl.pallas_call(first_spectrum, out_shape=(shape((OWNERS, 128), F32), shap...  3.12 us
    ppermute x3, waiting for transfers between devices, between_cores(): return lax.ppermute(array, 'core', [(0, 1), (1, 0)])  3.06 us
  transfers between devices with their start and end apart: 6, of which 6 were waited for; matrix products, arithmetic and copies ran while one was open for 2% of the time, Pallas kernels for 11%

profile of v10, /device:TPU:1, one launch (start us, length us, event | category | flops | bytes accessed | tf_op | source)
XLA Modules:
  0.0 93.2 jit_solution(16728197542272617224)
XLA Ops:
  0.0 3.1 %first_spectrum.1 = (f32[128,128]{1,0:T(8,128)}, f32[8,128]{1,0:T(8,128)}) custom-call(f32[4,16,16,128]{3,2,1,0:T(8,128)} %fields.5, bf16[384,128]{1,0:T(8,128)(2,1)} %constant.14.clone.ztab_h, bf16[2,512,256]{2,1,0:T(8,128)(2,1)} %constant.15.clone.ptab_h, s32[2,512]{1,0:T(2,128)} %constant.16.clone.steps_h.steps), custom_call_target="tpu_custom_call" | custom-call | tf_op jit(solution)/shard_map/first_spectrum/pallas_call | solution.py:636
  3.1 11.5 %all-to-all-start = ((f32[128,1,128]{2,1,0:T(1,128)}), f32[128,1,128]{2,1,0:T(1,128)S(1)}, u32[]{:S(2)}, u32[]{:S(2)}) async-start(f32[128,1,128]{2,1,0:T(1,128)} %bitcast.23), calls=%async_computation | async-start | bytes 131072 | tf_op jit(solution)/shard_map/all_to_all | solution.py:615
  14.6 0.8 copy.27.lift
  15.4 0.7 copy.28.lift_bias
  16.1 0.7 copy-done.7
  16.9 1.1 %prepare_mix.1 = (f32[2,2,8,32,64]{4,3,2,1,0:T(8,128)S(1)}, f32[32,128]{1,0:T(8,128)S(1)}, f32[32,32]{1,0:T(8,128)S(1)}) custom-call(f32[8,128]{1,0:T(8,128)S(1)} %copy-done.7, f32[2,2,8,32,64]{4,3,2,1,0:T(8,128)} %weights.2, f32[32,4]{1,0:T(8,128)S(1)} %copy.27.lift, f32[32,1]{1,0:T(8,128)S(1)} %copy.28.lift_bias), custom_call_target="tpu_custom_call" | custom-call | flops 2147483648 | bytes 6291456 | tf_op jit(solution)/shard_map/prepare_mix/pallas_call | solution.py:646
  18.0 6.3 %all-to-all-done = f32[128,1,128]{2,1,0:T(1,128)S(1)} async-done(((f32[128,1,128]{2,1,0:T(1,128)}), f32[128,1,128]{2,1,0:T(1,128)S(1)}, u32[]{:S(2)}, u32[]{:S(2)}) %all-to-all-start) | async-done | bytes 65568 | tf_op jit(solution)/shard_map/all_to_all | solution.py:615
  24.3 1.4 %first_mix.1 = (f32[64,16,128]{2,1,0:T(8,128)}, f32[8,128]{1,0:T(8,128)S(1)}) custom-call(f32[128,128]{1,0:T(8,128)S(1)} %bitcast.16, f32[32,128]{1,0:T(8,128)S(1)} %get-tuple-element.48.lift_wide, f32[32,32]{1,0:T(8,128)S(1)} %get-tuple-element.49.bias_column, f32[2,2,8,32,64]{4,3,2,1,0:T(8,128)S(1)} %get-tuple-element.50.weights), custom_call_target="tpu_custom_call" | custom-call | tf_op jit(solution)/shard_map/first_mix/pallas_call | solution.py:656
  25.7 4.6 %all-to-all-start.1 = ((f32[64,16,128]{2,1,0:T(8,128)}), f32[64,16,128]{2,1,0:T(8,128)S(1)}, u32[]{:S(2)}, u32[]{:S(2)}) async-start(f32[64,16,128]{2,1,0:T(8,128)} %get-tuple-element.51), calls=%async_computation.1 | async-start | bytes 1048576 | tf_op jit(solution)/shard_map/all_to_all | solution.py:615
  30.5 2.9 %prepare.1 = (bf16[256,256]{1,0:T(8,128)(2,1)S(1)}, bf16[256,256]{1,0:T(8,128)(2,1)S(1)}, bf16[2,256,256]{2,1,0:T(8,128)(2,1)S(1)}, bf16[112,512]{1,0:T(8,128)(2...) custom-call(f32[8,128]{1,0:T(8,128)S(1)} %get-tuple-element.52.after, ...), custom_call_target="tpu_custom_call" | custom-call | flops 2147483648 | bytes 6291456 | tf_op jit(solution)/shard_map/prepare/pallas_call | solution.py:662
  33.4 8.5 %all-to-all-done.1 = f32[64,16,128]{2,1,0:T(8,128)S(1)} async-done(((f32[64,16,128]{2,1,0:T(8,128)}), f32[64,16,128]{2,1,0:T(8,128)S(1)}, u32[]{:S(2)}, u32[]{:S(2)}) %all-to-all-start.1) | async-done | bytes 524320 | tf_op jit(solution)/shard_map/all_to_all | solution.py:615
  42.4 2.6 %collective-permute-start = (f32[4,128,128]{2,1,0:T(8,128)S(1)}, f32[4,128,128]{2,1,0:T(8,128)S(1)}, u32[]{:S(2)}, u32[]{:S(2)}) collective-permute-start(f32[4,128,128]{2,1,0:T(8,128)S(1)} %invert_mate.1), channel_id=1, source_target_pairs={{0,16},{16,0},{1,17},{17,1},{2,18},{18,2},{3,19},{19,3},{4,20},{20... | collective-permute-start | bytes 786440 | tf_op jit(solution)/shard_map/ppermute | solution.py:619
  45.4 0.7 collective-permute-done.got
  46.1 2.8 %coarse_level.1 = (f32[4,128,128]{2,1,0:T(8,128)S(1)}, bf16[8,2,128,512]{3,2,1,0:T(8,128)(2,1)}) custom-call(f32[4,128,128]{2,1,0:T(8,128)S(1)} %invert_own.1.own, f32[4,128,128]{2,1,0:T(8,128)S(1)} %collective-permute-done.got, bf16[112,512]{1,0:T(8,128)(2,1)S(1)} %get-tuple-element.64.pack, f32[4,16,16,128]{3,2,1,0:T(8,128)S(1)} %copy-done, ...), custom_call_target="tpu_custom_call" | custom-call | tf_op jit(solution)/shard_map/coarse_level/pallas_call | solution.py:684
  49.4 1.2 %collective-permute-done.1.got = f32[4,128,128]{2,1,0:T(8,128)S(1)} collective-permute-done((f32[4,128,128]{2,1,0:T(8,128)S(1)}, f32[4,128,128]{2,1,0:T(8,128)S(1)}, u32[]{:S(2)}, u32[]{:S(2)}) %collective-permute-start.1) | collective-permute-done | bytes 262176 | tf_op jit(solution)/shard_map/ppermute | solution.py:619
  50.6 1.4 %spread.1 = (f32[1024,128]{1,0:T(8,128)}, f32[8,128]{1,0:T(8,128)S(1)}) custom-call(f32[4,128,128]{2,1,0:T(8,128)S(1)} %get-tuple-element.65.kept, f32[4,128,128]{2,1,0:T(8,128)S(1)} %collective-permute-done.1.got, bf16[2,256,256]{2,1,0:T(8,128)(2,1)S(1)} %get-tuple-element.66.table), custom_call_target="tpu_custom_call" | custom-call | tf_op jit(solution)/shard_map/spread/pallas_call | solution.py:695
  52.1 4.6 %all-to-all-start.2 = ((f32[64,16,128]{2,1,0:T(8,128)}), f32[64,16,128]{2,1,0:T(8,128)S(1)}, u32[]{:S(2)}, u32[]{:S(2)}) async-start(f32[64,16,128]{2,1,0:T(8,128)} %bitcast.22), calls=%async_computation.2 | async-start | bytes 1048576 | tf_op jit(solution)/shard_map/all_to_all | solution.py:615
  57.2 5.9 %bypass.1 = (f32[8,128,512]{2,1,0:T(8,128)}, f32[4,16,16,128]{3,2,1,0:T(8,128)}) custom-call(f32[8,128]{1,0:T(8,128)S(1)} %get-tuple-element.68.after, bf16[8,2,128,512]{3,2,1,0:T(8,128)(2,1)} %get-tuple-element.69.values, bf16[256,512]{1,0:T(8,128)(2,1)} %get-tuple-element.70.wide_mix_h, f32[4,16,16,128]{3,2,1,0:T(8,128)S(1)} %copy-done, ...), custom_call_target="tpu_custom_call" | custom-call | flops 2147483648 | bytes 6291456 | tf_op jit(solution)/shard_map/bypass/pallas_call | solution.py:701
  63.1 5.6 %all-to-all-done.2.arrived = f32[64,16,128]{2,1,0:T(8,128)S(1)} async-done(((f32[64,16,128]{2,1,0:T(8,128)}), f32[64,16,128]{2,1,0:T(8,128)S(1)}, u32[]{:S(2)}, u32[]{:S(2)}) %all-to-all-start.2) | async-done | bytes 524320 | tf_op jit(solution)/shard_map/all_to_all | solution.py:615
  68.7 0.7 second_mix.1
  69.5 14.0 %all_to_all.27 = f32[64,8,128]{2,1,0:T(8,128)S(1)} all-to-all(f32[64,8,128]{2,1,0:T(8,128)S(1)} %second_mix.1), channel_id=1, replica_groups=mesh['x'=4,'core'=2,'gy'=16] {'x','gy'}, dimensions={0} | all-to-all | bytes 524288 | tf_op jit(solution)/shard_map/all_to_all | solution.py:615
  83.5 3.2 %collective-permute-start.2 = (f32[512,128]{1,0:T(8,128)S(1)}, f32[512,128]{1,0:T(8,128)S(1)}, u32[]{:S(2)}, u32[]{:S(2)}) collective-permute-start(f32[512,128]{1,0:T(8,128)S(1)} %bitcast.12), channel_id=1, source_target_pairs={{0,16},{16,0},{1,17},{17,1},{2,18},{18,2},{3,19},{19,3},{4,20},{20... | collective-permute-start | bytes 786440 | tf_op jit(solution)/shard_map/ppermute | solution.py:619
  86.7 1.2 %collective-permute-done.2.other = f32[512,128]{1,0:T(8,128)S(1)} collective-permute-done((f32[512,128]{1,0:T(8,128)S(1)}, f32[512,128]{1,0:T(8,128)S(1)}, u32[]{:S(2)}, u32[]{:S(2)}) %collective-permute-start.2) | collective-permute-done | bytes 262176 | tf_op jit(solution)/shard_map/ppermute | solution.py:619
  87.8 5.2 %fine_level.1 = f32[4,16,16,128]{3,2,1,0:T(8,128)} custom-call(f32[512,128]{1,0:T(8,128)S(1)} %bitcast.13, f32[512,128]{1,0:T(8,128)S(1)} %collective-permute-done.2.other, bf16[2,512,512]{2,1,0:T(8,128)(2,1)S(1)} %copy-done.1, bf16[512,256]{1,0:T(8,128)(2,1)} %constant.20.clone.z_back_h, f32[8,128,512]{2,1,0:T(8,128)} %get-tuple-element.75.skip, ...), custom_call_target="tpu_custom_call" | custom-call | tf_op jit(solution)/shard_map/fine_level/pallas_call | solution.py:724
  (35 shorter events, 1.9 us)
Async XLA Ops:
  3.1 21.2 %all-to-all-start = ((f32[128,1,128]{2,1,0:T(1,128)}), f32[128,1,128]{2,1,0:T(1,128)S(1)}, u32[]{:S(2)}, u32[]{:S(2)}) async-start(f32[128,1,128]{2,1,0:T(1,128)} %bitcast.23), calls=%async_computation | async-start | bytes 131072 | tf_op jit(solution)/shard_map/all_to_all | solution.py:615
  16.1 0.7 copy-start.7
  16.8 13.6 %copy-start.13 = (f32[64,32]{0,1:T(8,128)S(1)}, f32[64,32]{0,1:T(8,128)}, u32[]{:S(2)}) copy-start(f32[64,32]{0,1:T(8,128)} %param.22) | copy-start | bytes 24580
  16.8 13.7 %copy-start.4 = (s32[2,512]{1,0:T(2,128)S(1)}, s32[2,512]{1,0:T(2,128)}, u32[]{:S(2)}) copy-start(s32[2,512]{1,0:T(2,128)} %constant.16.clone.steps_h.steps) | copy-start | bytes 12292
  16.8 13.7 %copy-start.5 = (f32[32]{0:T(128)S(1)}, f32[32]{0:T(128)}, u32[]{:S(2)}) copy-start(f32[32]{0:T(128)} %param.20) | copy-start | bytes 388
  16.8 13.7 %copy-start.6 = (f32[32,64]{1,0:T(8,128)S(1)}, f32[32,64]{1,0:T(8,128)}, u32[]{:S(2)}) copy-start(f32[32,64]{1,0:T(8,128)} %bypass_out.1) | copy-start | bytes 24580
  16.8 13.7 %copy-start.8 = (f32[4,32]{1,0:T(4,128)S(1)}, f32[4,32]{1,0:T(4,128)}, u32[]{:S(2)}) copy-start(f32[4,32]{1,0:T(4,128)} %project.3) | copy-start | bytes 1540
  16.8 13.7 %copy-start.9 = (f32[64]{0:T(128)S(1)}, f32[64]{0:T(128)}, u32[]{:S(2)}) copy-start(f32[64]{0:T(128)} %param.23) | copy-start | bytes 772
  16.8 13.7 %copy-start.10 = (f32[32]{0:T(128)S(1)}, f32[32]{0:T(128)}, u32[]{:S(2)}) copy-start(f32[32]{0:T(128)} %param.26) | copy-start | bytes 388
  16.9 13.7 %copy-start.11 = (f32[4,16,512]{2,1,0:T(8,128)S(1)}, f32[4,16,512]{2,1,0:T(8,128)}, u32[]{:S(2)}) copy-start(f32[4,16,512]{2,1,0:T(8,128)} %constant.17.clone.waves) | copy-start | bytes 393220
  25.7 16.2 %all-to-all-start.1 = ((f32[64,16,128]{2,1,0:T(8,128)}), f32[64,16,128]{2,1,0:T(8,128)S(1)}, u32[]{:S(2)}, u32[]{:S(2)}) async-start(f32[64,16,128]{2,1,0:T(8,128)} %get-tuple-element.51), calls=%async_computation.1 | async-start | bytes 1048576 | tf_op jit(solution)/shard_map/all_to_all | solution.py:615
  42.4 3.8 %copy-start = (f32[4,16,16,128]{3,2,1,0:T(8,128)S(1)}, f32[4,16,16,128]{3,2,1,0:T(8,128)}, u32[]{:S(2)}) copy-start(f32[4,16,16,128]{3,2,1,0:T(8,128)} %fields.5) | copy-start | bytes 1572868
  42.4 3.8 %copy-start.2 = (bf16[64,128]{1,0:T(8,128)(2,1)S(1)}, bf16[64,128]{1,0:T(8,128)(2,1)}, u32[]{:S(2)}) copy-start(bf16[64,128]{1,0:T(8,128)(2,1)} %constant.18.clone.z_back) | copy-start | bytes 49156
  42.4 3.7 %copy-start.3 = (bf16[32,256]{1,0:T(8,128)(2,1)S(1)}, bf16[32,256]{1,0:T(8,128)(2,1)}, u32[]{:S(2)}) copy-start(bf16[32,256]{1,0:T(8,128)(2,1)} %constant.19.clone.z_fwd) | copy-start | bytes 49156
  42.4 3.7 %collective-permute-start = (f32[4,128,128]{2,1,0:T(8,128)S(1)}, f32[4,128,128]{2,1,0:T(8,128)S(1)}, u32[]{:S(2)}, u32[]{:S(2)}) collective-permute-start(f32[4,128,128]{2,1,0:T(8,128)S(1)} %invert_mate.1), channel_id=1, source_target_pairs={{0,16},{16,0},{1,17},{17,1},{2,18},{18,2},{3,19},{19,3},{4,20},{20... | collective-permute-start | bytes 786440 | tf_op jit(solution)/shard_map/ppermute | solution.py:619
  45.4 11.3 %copy-start.14 = (f32[4]{0:T(128)S(1)}, f32[4]{0:T(128)}, u32[]{:S(2)}) copy-start(f32[4]{0:T(128)} %param.28) | copy-start | bytes 52
  45.4 11.4 %copy-start.12 = (f32[2,2,8,64,32]{3,4,2,1,0:T(8,128)S(1)}, f32[2,2,8,64,32]{3,4,2,1,0:T(8,128)}, u32[]{:S(2)}) copy-start(f32[2,2,8,64,32]{3,4,2,1,0:T(8,128)} %param.24) | copy-start | bytes 786436
  49.0 1.6 %collective-permute-start.1 = (f32[4,128,128]{2,1,0:T(8,128)S(1)}, f32[4,128,128]{2,1,0:T(8,128)S(1)}, u32[]{:S(2)}, u32[]{:S(2)}) collective-permute-start(f32[4,128,128]{2,1,0:T(8,128)S(1)} %get-tuple-element.65.kept), channel_id=1, source_target_pairs={{0,16},{16,0},{1,17},{17,1},{2,18},{18,2},{3,19},{19,3},{4,20},{20... | collective-permute-start | bytes 786440 | tf_op jit(solution)/shard_map/ppermute | solution.py:619
  52.1 16.6 %all-to-all-start.2 = ((f32[64,16,128]{2,1,0:T(8,128)}), f32[64,16,128]{2,1,0:T(8,128)S(1)}, u32[]{:S(2)}, u32[]{:S(2)}) async-start(f32[64,16,128]{2,1,0:T(8,128)} %bitcast.22), calls=%async_computation.2 | async-start | bytes 1048576 | tf_op jit(solution)/shard_map/all_to_all | solution.py:615
  63.1 24.7 %copy-start.1 = (bf16[2,512,512]{2,1,0:T(8,128)(2,1)S(1)}, bf16[2,512,512]{2,1,0:T(8,128)(2,1)}, u32[]{:S(2)}) copy-start(bf16[2,512,512]{2,1,0:T(8,128)(2,1)} %get-tuple-element.74.table) | copy-start | bytes 3145732
  83.5 4.3 %collective-permute-start.2 = (f32[512,128]{1,0:T(8,128)S(1)}, f32[512,128]{1,0:T(8,128)S(1)}, u32[]{:S(2)}, u32[]{:S(2)}) collective-permute-start(f32[512,128]{1,0:T(8,128)S(1)} %bitcast.12), channel_id=1, source_target_pairs={{0,16},{16,0},{1,17},{17,1},{2,18},{18,2},{3,19},{19,3},{4,20},{20... | collective-permute-start | bytes 786440 | tf_op jit(solution)/shard_map/ppermute | solution.py:619
